TPU v7x, 128 devices: a whole 4x4x4 slice. The times are simulated.
128 devices in a mesh: fsdp: 16 (over y, x_lo, core), tp: 8 (over z, x_hi).
Axes of the slice: x: 4 (x_hi: 2, x_lo: 2; x = x_hi * 2 + x_lo), y: 4, z: 4, core: 2. Of those that a mesh axis runs over, the one named last changes fastest.
Arguments:
- tokens: bfloat16 [16384, 2048], P(('fsdp', 'tp')), may hold values from -6 to 6
- prefixes: int32 [8], replicated, may hold values from 1152 to 1536, as said below
- norm_gain: bfloat16 [2048], replicated, may hold values from 0.5 to 1.5
- query_weight: bfloat16 [2048, 2048], P('fsdp', 'tp'), may hold values from -0.1875 to 0.1875
- key_weight: bfloat16 [2048, 2048], P('fsdp', 'tp'), may hold values from -0.1875 to 0.1875
- value_weight: bfloat16 [2048, 2048], P('fsdp', 'tp'), may hold values from -0.125 to 0.125
- output_weight: bfloat16 [2048, 2048], P('tp', 'fsdp'), may hold values from -0.5 to 0.5
- feed_gain: bfloat16 [2048], replicated, may hold values from 0.5 to 1.5
- gate_weight: bfloat16 [2048, 5504], P('fsdp', 'tp'), may hold values from -0.125 to 0.125
- up_weight: bfloat16 [2048, 5504], P('fsdp', 'tp'), may hold values from -0.125 to 0.125
- down_weight: bfloat16 [5504, 2048], P('tp', 'fsdp'), may hold values from -0.15625 to 0.15625
- cotangent: bfloat16 [16384, 2048], P(('fsdp', 'tp')), may hold values from -6 to 6
Outputs:
- layer_output: bfloat16 [16384, 2048], P(('fsdp', 'tp'))
- token_grad: float32 [16384, 2048], P(('fsdp', 'tp'))
- norm_grad: float32 [2048], P('fsdp')
- query_grad: float32 [2048, 2048], P('fsdp', 'tp')
- key_grad: float32 [2048, 2048], P('fsdp', 'tp')
- value_grad: float32 [2048, 2048], P('fsdp', 'tp')
- output_grad: float32 [2048, 2048], P('tp', 'fsdp')
- feed_grad: float32 [2048], P('fsdp')
- gate_grad: float32 [2048, 5504], P('fsdp', 'tp')
- up_grad: float32 [2048, 5504], P('fsdp', 'tp')
- down_grad: float32 [5504, 2048], P('tp', 'fsdp')
Inputs may be any that keep to these rules, and one draw needn't show every extreme that they name: prefixes[s] tokens at the start of sequence s attend both ways; some sequence has the shortest prefix 9 * 128 and some the longest 3 * 512.
All inputs are finite; a program needn't handle non-finite values.
Results may differ from a plain program's by a relative error of at most 0.03.
Values may be sent and summed in bfloat16 or wider, within the bound.
A program may use at most 192 MiB of HBM per device.

v0:
```python
import math

import jax
import jax.numpy as jnp
from jax import lax
from jax.sharding import PartitionSpec as P

HD = 128
MIN_LEN = 2048


epsilon = 1e-05
rope_base = 10000.0


def partner_2(block, axis, apart):
    count = lax.axis_size(axis)
    route = []
    for low in range(count):
        high = low | 1 << apart
        if high != low and high < count:
            route += [(low, high), (high, low)]
    return lax.ppermute(block, axis, route)


def times_right(factor_left, factor_right):
    return jnp.dot(factor_left, factor_right, preferred_element_type=jnp.float32)


def across_rows(factor_left, factor_right):
    return lax.dot_general(
        factor_left, factor_right, (((0,), (0,)), ((), ())), preferred_element_type=jnp.float32
    )


def against_rows(factor_left, factor_right):
    return lax.dot_general(
        factor_left, factor_right, (((1,), (1,)), ((), ())), preferred_element_type=jnp.float32
    )


def rope_tables(positions, head_width):
    midway = head_width // 2
    counter = jnp.arange(midway, dtype=jnp.float32)
    inverse = jnp.exp(counter * (-2.0 / head_width) * math.log(rope_base))
    frequency = jnp.concatenate([inverse, inverse])
    angles = positions.astype(jnp.float32)[:, None] * frequency[None, :]
    return (jnp.cos(angles), jnp.sin(angles))


def rotate(values, cosine, sine_table):
    midway = values.shape[-1] // 2
    turned = jnp.concatenate([-values[..., midway:], values[..., :midway]], -1)
    return values * cosine[:, None, :] + turned * sine_table[:, None, :]


def unrotate(grads_in, cosine, sine_table):
    midway = grads_in.shape[-1] // 2
    scaled = grads_in * sine_table[:, None, :]
    back_turn = jnp.concatenate([scaled[..., midway:], -scaled[..., :midway]], -1)
    return grads_in * cosine[:, None, :] + back_turn


def spread(local_rows):
    return lax.all_gather(local_rows, "tp", axis=0, tiled=True)


def collect(partial_rows):
    return lax.psum_scatter(
        partial_rows.astype(jnp.bfloat16), "tp", scatter_dimension=0, tiled=True
    ).astype(jnp.float32)


def norm_forward(rows_in, gain_wide):
    inverse = lax.rsqrt(jnp.mean(rows_in * rows_in, -1, keepdims=True) + epsilon)
    scaled = rows_in * inverse
    return (inverse, scaled, (scaled * gain_wide).astype(jnp.bfloat16))


def norm_backward(upstream, inverse, scaled, gain_wide):
    weighted = upstream * gain_wide
    through = inverse * (weighted - scaled * jnp.mean(weighted * scaled, -1, keepdims=True))
    return (through, jnp.sum(upstream * scaled, 0))


def group_gather(packed, wide_place):
    partner = partner_2(packed, "fsdp", 0)
    is_upper = wide_place >> 0 & 1 == 1
    packed = jnp.where(
        is_upper, jnp.concatenate([partner, packed], 0), jnp.concatenate([packed, partner], 0)
    )
    return packed


def group_sum(packed, levels, wide_place):
    for bit_level in reversed(range(levels)):
        midway = packed.shape[0] // 2
        is_upper = wide_place >> bit_level & 1 == 1
        kept_part = jnp.where(is_upper, packed[midway:], packed[:midway])
        given_part = jnp.where(is_upper, packed[:midway], packed[midway:])
        packed = kept_part + partner_2(given_part.astype(jnp.bfloat16), "fsdp", bit_level).astype(
            given_part.dtype
        )
    return packed


def head_pieces(queries, key_value, head_number, head_size, head_columns):
    column_start = head_number * head_size
    query_head = lax.dynamic_slice_in_dim(queries, column_start, head_size, 1)
    key_head = lax.dynamic_slice_in_dim(key_value, column_start, head_size, 1)
    value_head = lax.dynamic_slice_in_dim(key_value, head_columns + column_start, head_size, 1)
    return (query_head, key_head, value_head)


def attend_forward(queries, key_value, allowed, heads_here, head_size):
    head_columns = heads_here * head_size
    score_scale = 1.0 / math.sqrt(head_size)

    def one_head(head_number):
        query_head, key_head, value_head = head_pieces(
            queries, key_value, head_number, head_size, head_columns
        )
        scores = jnp.where(allowed, against_rows(query_head, key_head) * score_scale, -1e30)
        top_score = jnp.max(scores, -1, keepdims=True)
        raised = jnp.exp(scores - top_score)
        totals = jnp.sum(raised, -1, keepdims=True)
        weights = (raised / totals).astype(jnp.bfloat16)
        mixed_head = times_right(weights, value_head)
        return (mixed_head, top_score[:, 0] + jnp.log(totals[:, 0]))

    return lax.map(one_head, jnp.arange(heads_here, dtype=jnp.int32))


def attend_backward(queries, key_value, allowed, log_totals, grad_mixed, heads_here, head_size):
    head_columns = heads_here * head_size
    score_scale = 1.0 / math.sqrt(head_size)

    def one_head(pair):
        head_number, log_total = pair
        query_head, key_head, value_head = head_pieces(
            queries, key_value, head_number, head_size, head_columns
        )
        grad_head = lax.dynamic_slice_in_dim(grad_mixed, head_number * head_size, head_size, 1)
        scores = jnp.where(allowed, against_rows(query_head, key_head) * score_scale, -1e30)
        probability = jnp.exp(scores - log_total[:, None])
        grad_probs = against_rows(grad_head, value_head)
        row_delta = jnp.sum(probability * grad_probs, -1, keepdims=True)
        grad_scores = (probability * (grad_probs - row_delta)).astype(jnp.bfloat16)
        grad_query = times_right(grad_scores, key_head) * score_scale
        grad_key = across_rows(grad_scores, query_head) * score_scale
        grad_value = across_rows(probability.astype(jnp.bfloat16), grad_head)
        return (grad_query, grad_key, grad_value)

    return lax.map(one_head, (jnp.arange(heads_here, dtype=jnp.int32), log_totals))


def on_device(
    tokens,
    prefixes,
    norm_gain,
    query_weight,
    key_weight,
    value_weight,
    output_weight,
    feed_gain,
    gate_weight,
    up_weight,
    down_weight,
    cotangent,
):
    tensor_count = lax.axis_size("tp")
    local_rows = tokens.shape[0]
    block_rows = local_rows * tensor_count
    sequence_rows = max(MIN_LEN, block_rows)
    group_span = sequence_rows // block_rows
    levels = group_span.bit_length() - 1
    head_size = HD
    heads_here = query_weight.shape[1] // head_size
    head_columns = heads_here * head_size
    wide_place = lax.axis_index("fsdp")
    first_row = wide_place * block_rows
    sequence_index = first_row // sequence_rows
    offset = first_row - sequence_index * sequence_rows
    prefix_here = jnp.sum(
        jnp.where(jnp.arange(prefixes.shape[0], dtype=jnp.int32) == sequence_index, prefixes, 0)
    )
    query_places = offset + jnp.arange(block_rows, dtype=jnp.int32)
    key_places = jnp.arange(sequence_rows, dtype=jnp.int32)
    allowed = (key_places[None, :] <= query_places[:, None]) | (key_places[None, :] < prefix_here)
    cosine, sine_table = rope_tables(query_places, head_size)
    gain_one = norm_gain.astype(jnp.float32)
    gain_two = feed_gain.astype(jnp.float32)
    tokens_wide = tokens.astype(jnp.float32)
    inverse_one, scaled_one, normed_one = norm_forward(tokens_wide, gain_one)
    query_full, key_full, value_full, output_full = (
        lax.all_gather(query_weight, "fsdp", axis=0, tiled=True),
        lax.all_gather(key_weight, "fsdp", axis=0, tiled=True),
        lax.all_gather(value_weight, "fsdp", axis=0, tiled=True),
        lax.all_gather(output_weight, "fsdp", axis=1, tiled=True),
    )
    rows_one = spread(normed_one)
    query_pre = times_right(rows_one, query_full).reshape(block_rows, heads_here, head_size)
    key_pre = times_right(rows_one, key_full).reshape(block_rows, heads_here, head_size)
    value_rows = times_right(rows_one, value_full).astype(jnp.bfloat16)
    query_rot = (
        rotate(query_pre, cosine, sine_table).reshape(block_rows, head_columns).astype(jnp.bfloat16)
    )
    key_rot = (
        rotate(key_pre, cosine, sine_table).reshape(block_rows, head_columns).astype(jnp.bfloat16)
    )
    key_value = group_gather(jnp.concatenate([key_rot, value_rows], 1), wide_place)
    mixed_all, log_totals = attend_forward(query_rot, key_value, allowed, heads_here, head_size)
    attended = mixed_all.transpose(1, 0, 2).reshape(block_rows, head_columns).astype(jnp.bfloat16)
    middle = tokens_wide + collect(times_right(attended, output_full))
    inverse_two, scaled_two, normed_two = norm_forward(middle, gain_two)
    gate_full, up_full, down_full = (
        lax.all_gather(gate_weight, "fsdp", axis=0, tiled=True),
        lax.all_gather(up_weight, "fsdp", axis=0, tiled=True),
        lax.all_gather(down_weight, "fsdp", axis=1, tiled=True),
    )
    rows_two = spread(normed_two)
    gating = times_right(rows_two, gate_full)
    upward = times_right(rows_two, up_full)
    hidden = (jax.nn.silu(gating) * upward).astype(jnp.bfloat16)
    layer_output = (middle + collect(times_right(hidden, down_full))).astype(jnp.bfloat16)
    upstream = cotangent.astype(jnp.float32)
    grad_rows = spread(cotangent)
    grad_hidden = against_rows(grad_rows, down_full)
    down_grad = across_rows(hidden, grad_rows)
    sigma = jax.nn.sigmoid(gating)
    grad_up = (grad_hidden * gating * sigma).astype(jnp.bfloat16)
    grad_gate = (grad_hidden * upward * sigma * (1.0 + gating * (1.0 - sigma))).astype(jnp.bfloat16)
    gate_grad = across_rows(rows_two, grad_gate)
    up_grad = across_rows(rows_two, grad_up)
    grad_normed_two = collect(against_rows(grad_gate, gate_full) + against_rows(grad_up, up_full))
    grad_middle_norm, feed_part = norm_backward(grad_normed_two, inverse_two, scaled_two, gain_two)
    grad_middle = upstream + grad_middle_norm
    grad_attended = spread(grad_middle.astype(jnp.bfloat16))
    output_grad = across_rows(attended, grad_attended)
    grad_mixed = against_rows(grad_attended, output_full).astype(jnp.bfloat16)
    grad_query_heads, grad_key_heads, grad_value_heads = attend_backward(
        query_rot, key_value, allowed, log_totals, grad_mixed, heads_here, head_size
    )
    grad_key_group = grad_key_heads.transpose(1, 0, 2).reshape(sequence_rows, head_columns)
    grad_value_group = grad_value_heads.transpose(1, 0, 2).reshape(sequence_rows, head_columns)
    owned = group_sum(jnp.concatenate([grad_key_group, grad_value_group], 1), levels, wide_place)
    grad_query_pre = (
        unrotate(grad_query_heads.transpose(1, 0, 2), cosine, sine_table)
        .reshape(block_rows, head_columns)
        .astype(jnp.bfloat16)
    )
    grad_key_pre = (
        unrotate(
            owned[:, :head_columns].reshape(block_rows, heads_here, head_size), cosine, sine_table
        )
        .reshape(block_rows, head_columns)
        .astype(jnp.bfloat16)
    )
    grad_value = owned[:, head_columns:].astype(jnp.bfloat16)
    query_grad = across_rows(rows_one, grad_query_pre)
    key_grad = across_rows(rows_one, grad_key_pre)
    value_grad = across_rows(rows_one, grad_value)
    grad_normed_one = collect(
        against_rows(grad_query_pre, query_full)
        + against_rows(grad_key_pre, key_full)
        + against_rows(grad_value, value_full)
    )
    grad_tokens_norm, norm_part = norm_backward(grad_normed_one, inverse_one, scaled_one, gain_one)
    token_grad = grad_middle + grad_tokens_norm
    (
        query_grad,
        key_grad,
        value_grad,
        output_grad,
        gate_grad,
        up_grad,
        down_grad,
        norm_part,
        feed_part,
    ) = (
        lax.psum_scatter(
            query_grad.astype(jnp.bfloat16), "fsdp", scatter_dimension=0, tiled=True
        ).astype(jnp.float32),
        lax.psum_scatter(
            key_grad.astype(jnp.bfloat16), "fsdp", scatter_dimension=0, tiled=True
        ).astype(jnp.float32),
        lax.psum_scatter(
            value_grad.astype(jnp.bfloat16), "fsdp", scatter_dimension=0, tiled=True
        ).astype(jnp.float32),
        lax.psum_scatter(
            output_grad.astype(jnp.bfloat16), "fsdp", scatter_dimension=1, tiled=True
        ).astype(jnp.float32),
        lax.psum_scatter(
            gate_grad.astype(jnp.bfloat16), "fsdp", scatter_dimension=0, tiled=True
        ).astype(jnp.float32),
        lax.psum_scatter(
            up_grad.astype(jnp.bfloat16), "fsdp", scatter_dimension=0, tiled=True
        ).astype(jnp.float32),
        lax.psum_scatter(
            down_grad.astype(jnp.bfloat16), "fsdp", scatter_dimension=1, tiled=True
        ).astype(jnp.float32),
        lax.psum_scatter(
            norm_part.astype(jnp.bfloat16), "fsdp", scatter_dimension=0, tiled=True
        ).astype(jnp.float32),
        lax.psum_scatter(
            feed_part.astype(jnp.bfloat16), "fsdp", scatter_dimension=0, tiled=True
        ).astype(jnp.float32),
    )
    norm_grad, feed_grad = lax.psum((norm_part, feed_part), "tp")
    return (
        layer_output,
        token_grad,
        norm_grad,
        query_grad,
        key_grad,
        value_grad,
        output_grad,
        feed_grad,
        gate_grad,
        up_grad,
        down_grad,
    )


def solution(mesh):
    placed = (
        P(("fsdp", "tp"), None),
        P(),
        P(),
        P("fsdp", "tp"),
        P("fsdp", "tp"),
        P("fsdp", "tp"),
        P("tp", "fsdp"),
        P(),
        P("fsdp", "tp"),
        P("fsdp", "tp"),
        P("tp", "fsdp"),
        P(("fsdp", "tp"), None),
    )
    return jax.shard_map(
        on_device,
        mesh=mesh,
        in_specs=placed,
        out_specs=(
            P(("fsdp", "tp"), None),
            P(("fsdp", "tp"), None),
            P("fsdp"),
            P("fsdp", "tp"),
            P("fsdp", "tp"),
            P("fsdp", "tp"),
            P("tp", "fsdp"),
            P("fsdp"),
            P("fsdp", "tp"),
            P("fsdp", "tp"),
            P("tp", "fsdp"),
        ),
        check_vma=False,
    )
```

profile of v0, /device:TPU:1, one launch (start us, length us, event | category | flops | bytes accessed | tf_op | source)
XLA Modules:
  0.0 1405.2 jit_solution(6720128584923134884)
XLA Ops:
  15.8 29.9 %all-gather.16.cloned.1.call-done = bf16[2048,256]{1,0:T(8,128)(2,1)} async-done(((bf16[128,256]{1,0:T(8,128)(2,1)}), bf16[2048,256]{1,0:T(8,128)(2,1)}) %all-gather.16.cloned.1.call-update) | async-done | bytes 1048592 | tf_op jit(solution)/shard_map/all_gather | solution.py:197
  45.8 73.8 %all-gather.12.cloned.1.call-done = bf16[1024,2048]{1,0:T(8,128)(2,1)} async-done(((bf16[128,2048]{1,0:T(8,128)(2,1)}), bf16[1024,2048]{1,0:T(8,128)(2,1)}) %all-gather.12.cloned.1.call-update) | async-done | bytes 4194320 | tf_op jit(solution)/shard_map/all_gather | solution.py:65
  119.6 3.8 fusion.75
  123.3 29.0 %all-gather.14.cloned.1.call-done = bf16[2048,256]{1,0:T(8,128)(2,1)} async-done(((bf16[128,256]{1,0:T(8,128)(2,1)}), bf16[2048,256]{1,0:T(8,128)(2,1)}) %all-gather.14.cloned.1.call-update) | async-done | bytes 1048592 | tf_op jit(solution)/shard_map/all_gather | solution.py:196
  157.2 29.2 %all-gather.18.cloned.1.call-done = bf16[2048,256]{1,0:T(8,128)(2,1)} async-done(((bf16[128,256]{1,0:T(8,128)(2,1)}), bf16[2048,256]{1,0:T(8,128)(2,1)}) %all-gather.18.cloned.1.call-update) | async-done | bytes 1048592 | tf_op jit(solution)/shard_map/all_gather | solution.py:198
  194.0 6.3 maximum_select_fusion
  202.9 27.9 %while.34 = (s32[]{:T(128)}, bf16[2,1024,128]{1,2,0:T(8,128)(2,1)S(1)}, f32[2,1024]{1,0:T(2,128)S(1)}, s32[2]{0:T(128)S(1)}, bf16[1024,256]{1,0:T(8,128)(2,1)}, ...) while((s32[]{:T(128)}, ...), condition=%wide.region_5.6_spmd.clone.clone, body=%wide.region_2.5_spmd.clone.sunk.clone | while | flops 1111489536 | bytes 27060460 | solution.py:131
  211.6 5.2 fusion.158
  218.1 3.8 fusion.156
  225.5 5.2 fusion.158
  230.9 4.5 convolution_convert_fusion.1
  236.2 82.6 %reduce-scatter.20.cloned.1.call-done = bf16[128,2048]{1,0:T(8,128)(2,1)} async-done(((bf16[1024,2048]{1,0:T(8,128)(2,1)}), bf16[128,2048]{1,0:T(8,128)(2,1)}) %reduce-scatter.20.cloned.1.call-update) | async-done | bytes 524304 | tf_op jit(solution)/shard_map/reduce_scatter | solution.py:69
  324.7 35.8 %all-gather.26.cloned.1.call-done = bf16[2048,688]{0,1:T(8,128)(2,1)} async-done(((bf16[128,688]{0,1:T(8,128)(2,1)}), bf16[2048,688]{0,1:T(8,128)(2,1)}) %all-gather.26.cloned.1.call-update) | async-done | bytes 2818064 | tf_op jit(solution)/shard_map/all_gather | solution.py:218
  360.5 74.3 %all-gather.22.cloned.1.call-done = bf16[1024,2048]{1,0:T(8,128)(2,1)} async-done(((bf16[128,2048]{1,0:T(8,128)(2,1)}), bf16[1024,2048]{1,0:T(8,128)(2,1)}) %all-gather.22.cloned.1.call-update) | async-done | bytes 4194320 | tf_op jit(solution)/shard_map/all_gather | solution.py:65
  434.9 7.8 fusion.77
  442.7 32.2 %all-gather.24.cloned.1.call-done = bf16[2048,688]{0,1:T(8,128)(2,1)} async-done(((bf16[128,688]{0,1:T(8,128)(2,1)}), bf16[2048,688]{0,1:T(8,128)(2,1)}) %all-gather.24.cloned.1.call-update) | async-done | bytes 2818064 | tf_op jit(solution)/shard_map/all_gather | solution.py:217
  475.0 7.7 fusion.76
  482.7 34.0 %all-gather.28.cloned.1.call-done = bf16[688,2048]{1,0:T(8,128)(2,1)} async-done(((bf16[688,128]{1,0:T(8,128)(2,1)}), bf16[688,2048]{1,0:T(8,128)(2,1)}) %all-gather.28.cloned.1.call-update) | async-done | bytes 2818064 | tf_op jit(solution)/shard_map/all_gather | solution.py:219
  516.7 73.8 %all-gather.30.cloned.1.call-done = bf16[1024,2048]{1,0:T(8,128)(2,1)} async-done(((bf16[128,2048]{1,0:T(8,128)(2,1)}), bf16[1024,2048]{1,0:T(8,128)(2,1)}) %all-gather.30.cloned.1.call-update) | async-done | bytes 4194320 | tf_op jit(solution)/shard_map/all_gather | solution.py:65
  590.5 10.0 multiply_convert_fusion.1
  604.0 5.6 add_convert_fusion.1
  609.7 82.1 %reduce-scatter.24.cloned.1.call-done = bf16[128,2048]{1,0:T(8,128)(2,1)} async-done(((bf16[1024,2048]{1,0:T(8,128)(2,1)}), bf16[128,2048]{1,0:T(8,128)(2,1)}) %reduce-scatter.24.cloned.1.call-update) | async-done | bytes 524304 | tf_op jit(solution)/shard_map/reduce_scatter | solution.py:69
  696.3 7.2 convolution_convert_fusion.4
  703.5 4.7 copy.55
  709.5 6.5 convolution_convert_fusion.3
  716.1 4.6 copy.51
  722.1 6.5 convolution_convert_fusion.2
  728.6 4.6 copy.53
  733.4 33.9 %all-gather.32.cloned.1.call-done = bf16[1024,2048]{1,0:T(8,128)(2,1)} async-done(((bf16[128,2048]{1,0:T(8,128)(2,1)}), bf16[1024,2048]{1,0:T(8,128)(2,1)}) %all-gather.32.cloned.1.call-update) | async-done | bytes 4194320 | tf_op jit(solution)/shard_map/all_gather | solution.py:65
  772.0 4.3 convolution_convert_fusion.9
  776.3 60.9 %while.35 = (s32[]{:T(128)}, f32[2,1024,128]{1,2,0:T(8,128)}, f32[2,2048,128]{2,1,0:T(8,128)}, f32[2,2048,128]{2,1,0:T(8,128)}, s32[2]{0:T(128)S(1)}, /*index=5*...) while((s32[]{:T(128)}, f32[2,1024,128]{1,2,0:T(8,128)}, ...), condition=%wide.region_13.14_spmd.clone.clone, body=%wide.region_11.13_spmd.clone.sunk.clone | while | flops 2707815424 | bytes 103835960 | solution.py:154
  780.2 7.7 multiply_reduce_fusion.4
  787.9 6.7 multiply_convert_fusion.7
  794.6 5.7 fusion.170
  810.5 7.7 multiply_reduce_fusion.4
  818.2 6.7 multiply_convert_fusion.7
  824.9 5.7 fusion.170
  875.5 6.5 convolution_convert_fusion
  885.8 14.6 %reduce-scatter.36.cloned.1.call-done = bf16[128,688]{1,0:T(8,128)(2,1)} async-done(((bf16[2048,688]{1,0:T(8,128)(2,1)}), bf16[128,688]{1,0:T(8,128)(2,1)}) %reduce-scatter.36.cloned.1.call-update) | async-done | bytes 176144
  902.2 66.0 %reduce-scatter.38.cloned.1.call-done = bf16[128,688]{1,0:T(8,128)(2,1)} async-done(((bf16[2048,688]{1,0:T(8,128)(2,1)}), bf16[128,688]{1,0:T(8,128)(2,1)}) %reduce-scatter.38.cloned.1.call-update) | async-done | bytes 176144
  970.0 59.5 %reduce-scatter.34.cloned.1.call-done = bf16[128,256]{1,0:T(8,128)(2,1)} async-done(((bf16[2048,256]{1,0:T(8,128)(2,1)}), bf16[128,256]{1,0:T(8,128)(2,1)}) %reduce-scatter.34.cloned.1.call-update) | async-done | bytes 65552
  1031.1 61.1 %reduce-scatter.28.cloned.1.call-done = bf16[128,256]{1,0:T(8,128)(2,1)} async-done(((bf16[2048,256]{1,0:T(8,128)(2,1)}), bf16[128,256]{1,0:T(8,128)(2,1)}) %reduce-scatter.28.cloned.1.call-update) | async-done | bytes 65552 | tf_op jit(solution)/shard_map/reduce_scatter | solution.py:281
  1093.7 60.8 %reduce-scatter.32.cloned.1.call-done = bf16[128,256]{1,0:T(8,128)(2,1)} async-done(((bf16[2048,256]{1,0:T(8,128)(2,1)}), bf16[128,256]{1,0:T(8,128)(2,1)}) %reduce-scatter.32.cloned.1.call-update) | async-done | bytes 65552 | tf_op jit(solution)/shard_map/reduce_scatter | solution.py:287
  1156.1 60.8 %reduce-scatter.30.cloned.1.call-done = bf16[128,256]{1,0:T(8,128)(2,1)} async-done(((bf16[2048,256]{1,0:T(8,128)(2,1)}), bf16[128,256]{1,0:T(8,128)(2,1)}) %reduce-scatter.30.cloned.1.call-update) | async-done | bytes 65552 | tf_op jit(solution)/shard_map/reduce_scatter | solution.py:284
  1218.4 88.2 %reduce-scatter.26.cloned.1.call-done = bf16[128,2048]{1,0:T(8,128)(2,1)} async-done(((bf16[1024,2048]{1,0:T(8,128)(2,1)}), bf16[128,2048]{1,0:T(8,128)(2,1)}) %reduce-scatter.26.cloned.1.call-update) | async-done | bytes 524304 | tf_op jit(solution)/shard_map/reduce_scatter | solution.py:69
  1308.0 28.9 %all-reduce.3 = (bf16[2048]{0:T(1024)(128)(2,1)S(1)}, bf16[2048]{0:T(1024)(128)(2,1)S(1)}) all-reduce(bf16[2048]{0:T(1024)(128)(2,1)S(1)} %get-tuple-element.338, bf16[2048]{0:T(1024)(128)(2,1)S(1)} %copy-done.26), channel_id=6, replica_groups=mesh['fsdp'=16,'tp'=8] {'fsdp'}, use_global_device_ids=true, to_apply=%region_17.18.clone | all-reduce | flops 4096 | bytes 16384
  1337.1 18.7 %all-reduce.2 = (f32[128]{0:T(128)}, f32[128]{0:T(128)}) all-reduce(f32[128]{0:T(128)S(1)} %dynamic-slice_convert_fusion.1, f32[128]{0:T(128)S(1)} %dynamic-slice_convert_fusion), channel_id=1, replica_groups=mesh['fsdp'=16,'tp'=8] {'tp'}, use_global_device_ids=true, to_apply=%region_18.19 | all-reduce | flops 256 | bytes 2048 | tf_op jit(solution)/shard_map/psum | solution.py:309
  1355.8 38.9 %reduce-scatter.22.cloned.1.call-done = bf16[128,2048]{1,0:T(8,128)(2,1)} async-done(((bf16[1024,2048]{1,0:T(8,128)(2,1)}), bf16[128,2048]{1,0:T(8,128)(2,1)}) %reduce-scatter.22.cloned.1.call-update) | async-done | bytes 524304 | tf_op jit(solution)/shard_map/reduce_scatter | solution.py:69
  (239 shorter events, 133.0 us)
Async XLA Ops:
  7.2 38.6 %all-gather.16.cloned.1.call-start = ((), (), s32[]{:S(2)}) async-start(), calls=%async_computation.13 | async-start | bytes 1114112 | tf_op jit(solution)/shard_map/all_gather | solution.py:197
  7.9 111.6 %all-gather.12.cloned.1.call-start = ((), (), s32[]{:S(2)}) async-start(), calls=%async_computation.11 | async-start | bytes 4718592 | tf_op jit(solution)/shard_map/all_gather | solution.py:65
  12.5 139.8 %all-gather.14.cloned.1.call-start = ((), (), s32[]{:S(2)}) async-start(), calls=%async_computation.12 | async-start | bytes 1114112 | tf_op jit(solution)/shard_map/all_gather | solution.py:196
  13.2 173.2 %all-gather.18.cloned.1.call-start = ((), (), s32[]{:S(2)}) async-start(), calls=%async_computation.14 | async-start | bytes 1114112 | tf_op jit(solution)/shard_map/all_gather | solution.py:198
  13.8 217.1 %all-gather.20.cloned.1.call-start = ((), (), s32[]{:S(2)}) async-start(), calls=%async_computation.15 | async-start | bytes 1114112 | tf_op jit(solution)/shard_map/all_gather | solution.py:199
  15.8 140.4 %copy-start.8 = (f32[1024,128]{0,1:T(8,128)}, f32[1024,128]{0,1:T(8,128)S(1)}, u32[]{:S(2)}) copy-start(f32[1024,128]{0,1:T(8,128)S(1)} %get-tuple-element.404) | copy-start | bytes 1572868
  15.8 140.7 %copy-start.9 = (f32[1024,128]{0,1:T(8,128)}, f32[1024,128]{0,1:T(8,128)S(1)}, u32[]{:S(2)}) copy-start(f32[1024,128]{0,1:T(8,128)S(1)} %get-tuple-element.403) | copy-start | bytes 1572868
  157.2 34.5 %copy-start.40 = (s32[8]{0:T(128)S(1)}, s32[8]{0:T(128)}, u32[]{:S(2)}) copy-start(s32[8]{0:T(128)} %param.17) | copy-start | bytes 100
  191.0 3.0 collective-permute-start
  191.4 127.4 %reduce-scatter.20.cloned.1.call-start = ((), (), s32[]{:S(2)}) async-start(), calls=%async_computation.16 | async-start | bytes 4718592 | tf_op jit(solution)/shard_map/reduce_scatter | solution.py:69
  235.4 83.4 %copy-start.1 = (bf16[128,2048]{1,0:T(8,128)(2,1)S(1)}, bf16[128,2048]{1,0:T(8,128)(2,1)}, u32[]{:S(2)}) copy-start(bf16[128,2048]{1,0:T(8,128)(2,1)} %param.16) | copy-start | bytes 1572868
  235.4 125.1 %all-gather.26.cloned.1.call-start = ((), (), s32[]{:S(2)}) async-start(), calls=%async_computation.19 | async-start | bytes 2994176 | tf_op jit(solution)/shard_map/all_gather | solution.py:218
  236.2 198.7 %all-gather.22.cloned.1.call-start = ((), (), s32[]{:S(2)}) async-start(), calls=%async_computation.17 | async-start | bytes 4718592 | tf_op jit(solution)/shard_map/all_gather | solution.py:65
  236.2 457.7 %copy-start.22 = (f32[2048]{0:T(1024)}, f32[2048]{0:T(1024)S(1)}, u32[]{:S(2)}) copy-start(f32[2048]{0:T(1024)S(1)} %convert_element_type.185) | copy-start | bytes 24580
  320.1 373.8 %copy-start.27 = (f32[128]{0:T(128)}, f32[128]{0:T(128)S(1)}, u32[]{:S(2)}) copy-start(f32[128]{0:T(128)S(1)} %add_rsqrt_fusion) | copy-start | bytes 1540
  322.2 152.8 %all-gather.24.cloned.1.call-start = ((), (), s32[]{:S(2)}) async-start(), calls=%async_computation.18 | async-start | bytes 2994176 | tf_op jit(solution)/shard_map/all_gather | solution.py:217
  322.9 193.7 %all-gather.28.cloned.1.call-start = ((), (), s32[]{:S(2)}) async-start(), calls=%async_computation.20 | async-start | bytes 2994176 | tf_op jit(solution)/shard_map/all_gather | solution.py:219
  323.5 266.9 %all-gather.30.cloned.1.call-start = ((), (), s32[]{:S(2)}) async-start(), calls=%async_computation.22 | async-start | bytes 4718592 | tf_op jit(solution)/shard_map/all_gather | solution.py:65
  324.3 367.5 %reduce-scatter.24.cloned.1.call-start = ((), (), s32[]{:S(2)}) async-start(), calls=%async_computation.23 | async-start | bytes 4718592 | tf_op jit(solution)/shard_map/reduce_scatter | solution.py:69
  590.5 10.0 copy-start.39
  609.6 82.1 %copy-start.6 = (bf16[128,2048]{1,0:T(8,128)(2,1)S(1)}, bf16[128,2048]{1,0:T(8,128)(2,1)}, u32[]{:S(2)}) copy-start(bf16[128,2048]{1,0:T(8,128)(2,1)} %reduce-scatter.20.cloned.1.call-done) | copy-start | bytes 1572868
  609.6 84.3 %copy-start.12 = (bf16[128,2048]{1,0:T(8,128)(2,1)S(1)}, bf16[128,2048]{1,0:T(8,128)(2,1)}, u32[]{:S(2)}) copy-start(bf16[128,2048]{1,0:T(8,128)(2,1)} %param.27) | copy-start | bytes 1572868
  609.6 157.6 %all-gather.32.cloned.1.call-start = ((), (), s32[]{:S(2)}) async-start(), calls=%async_computation.24 | async-start | bytes 4718592 | tf_op jit(solution)/shard_map/all_gather | solution.py:65
  693.9 9.6 copy-start.32
  696.2 187.7 %reduce-scatter.40.cloned.1.call-start = ((), (), s32[]{:S(2)}) async-start(), calls=%async_computation.32 | async-start | bytes 3342336
  708.2 192.1 %reduce-scatter.36.cloned.1.call-start = ((), (), s32[]{:S(2)}) async-start(), calls=%async_computation.30 | async-start | bytes 3342336
  720.7 247.4 %reduce-scatter.38.cloned.1.call-start = ((), (), s32[]{:S(2)}) async-start(), calls=%async_computation.31 | async-start | bytes 3342336
  733.3 296.2 %reduce-scatter.34.cloned.1.call-start = ((), (), s32[]{:S(2)}) async-start(), calls=%async_computation.29 | async-start | bytes 1114112
  772.0 320.3 %reduce-scatter.28.cloned.1.call-start = ((), (), s32[]{:S(2)}) async-start(), calls=%async_computation.26 | async-start | bytes 1114112 | tf_op jit(solution)/shard_map/reduce_scatter | solution.py:281
  780.2 7.7 copy-start
  810.5 7.7 copy-start
  843.7 310.9 %reduce-scatter.32.cloned.1.call-start = ((), (), s32[]{:S(2)}) async-start(), calls=%async_computation.28 | async-start | bytes 1114112 | tf_op jit(solution)/shard_map/reduce_scatter | solution.py:287
  848.6 5.8 copy-start.3
  850.7 5.8 copy-start.35
  850.7 3.8 collective-permute-start.1
  858.9 358.0 %reduce-scatter.30.cloned.1.call-start = ((), (), s32[]{:S(2)}) async-start(), calls=%async_computation.27 | async-start | bytes 1114112 | tf_op jit(solution)/shard_map/reduce_scatter | solution.py:284
  866.2 440.3 %reduce-scatter.26.cloned.1.call-start = ((), (), s32[]{:S(2)}) async-start(), calls=%async_computation.25 | async-start | bytes 4718592 | tf_op jit(solution)/shard_map/reduce_scatter | solution.py:69
  873.7 520.9 %reduce-scatter.22.cloned.1.call-start = ((), (), s32[]{:S(2)}) async-start(), calls=%async_computation.21 | async-start | bytes 4718592 | tf_op jit(solution)/shard_map/reduce_scatter | solution.py:69
  882.0 424.5 %copy-start.2 = (bf16[128,2048]{1,0:T(8,128)(2,1)S(1)}, bf16[128,2048]{1,0:T(8,128)(2,1)}, u32[]{:S(2)}) copy-start(bf16[128,2048]{1,0:T(8,128)(2,1)} %param.16) | copy-start | bytes 1572868
  882.0 424.5 %copy-start.25 = (f32[2048]{0:T(1024)S(1)}, f32[2048]{0:T(1024)}, u32[]{:S(2)}) copy-start(f32[2048]{0:T(1024)} %copy-done.24) | copy-start | bytes 24580
  882.1 424.5 %copy-start.30 = (f32[128]{0:T(128)S(1)}, f32[128]{0:T(128)}, u32[]{:S(2)}) copy-start(f32[128]{0:T(128)} %copy-done.29) | copy-start | bytes 1540
  882.1 425.9 %copy-start.26 = (bf16[2048]{0:T(1024)(128)(2,1)S(1)}, bf16[2048]{0:T(1024)(128)(2,1)}, u32[]{:S(2)}) copy-start(bf16[2048]{0:T(1024)(128)(2,1)} %get-tuple-element.336) | copy-start | bytes 12292
  882.1 512.6 %copy-start.7 = (bf16[128,2048]{1,0:T(8,128)(2,1)S(1)}, bf16[128,2048]{1,0:T(8,128)(2,1)}, u32[]{:S(2)}) copy-start(bf16[128,2048]{1,0:T(8,128)(2,1)} %reduce-scatter.20.cloned.1.call-done) | copy-start | bytes 1572868
  882.1 512.6 %copy-start.13 = (bf16[128,2048]{1,0:T(8,128)(2,1)S(1)}, bf16[128,2048]{1,0:T(8,128)(2,1)}, u32[]{:S(2)}) copy-start(bf16[128,2048]{1,0:T(8,128)(2,1)} %param.27) | copy-start | bytes 1572868
  882.1 512.6 %copy-start.14 = (bf16[128,2048]{1,0:T(8,128)(2,1)S(1)}, bf16[128,2048]{1,0:T(8,128)(2,1)}, u32[]{:S(2)}) copy-start(bf16[128,2048]{1,0:T(8,128)(2,1)} %reduce-scatter.24.cloned.1.call-done) | copy-start | bytes 1572868
  882.1 512.6 %copy-start.23 = (f32[2048]{0:T(1024)S(1)}, f32[2048]{0:T(1024)}, u32[]{:S(2)}) copy-start(f32[2048]{0:T(1024)} %copy-done.22) | copy-start | bytes 24580
  882.1 512.6 %copy-start.28 = (f32[128]{0:T(128)S(1)}, f32[128]{0:T(128)}, u32[]{:S(2)}) copy-start(f32[128]{0:T(128)} %copy-done.27) | copy-start | bytes 1540
  882.1 512.6 %copy-start.33 = (f32[128]{0:T(128)S(1)}, f32[128]{0:T(128)}, u32[]{:S(2)}) copy-start(f32[128]{0:T(128)} %copy-done.32) | copy-start | bytes 1540
  (24 other events, 42.5 us)
Sparse Core Ops, SparseCore 0:
  9.7 36.0 all-gather.15
  48.7 70.8 all-gather.11
  121.3 30.9 all-gather.13
  153.8 32.4 all-gather.17
  191.5 33.9 all-gather.19
  235.5 83.2 reduce-scatter.19
  320.5 39.9 all-gather.25
  363.7 71.1 all-gather.21
  436.6 38.3 all-gather.23
  476.5 40.1 all-gather.27
  519.3 71.1 all-gather.29
  609.8 81.9 reduce-scatter.23
  696.3 70.8 all-gather.31
  769.5 62.7 reduce-scatter.39
  834.5 65.8 reduce-scatter.35
  902.6 65.5 reduce-scatter.37
  970.4 59.0 reduce-scatter.33
  1032.4 59.7 reduce-scatter.27
  1094.6 59.9 reduce-scatter.31
  1156.9 59.9 reduce-scatter.29
  1220.7 85.7 reduce-scatter.25
  1310.8 83.8 reduce-scatter.21
where the time goes:
time: 1410 us
  waiting for transfers between devices  1070 us (76%)
  matrix products  160 us (11%)
  other arithmetic  61.7 us (4%)
  blocking collectives  47.6 us (3%)
  local copies, waits for them, and re-layouts  45.9 us (3%)
  between operations  16.1 us (1%)
    reduce_scatter x4, waiting for transfers between devices, collect(): lax.psum_scatter(partial_rows.astype(jnp.bfloat16), 'tp', scatter_dimensi...  292 us
    all_gather x4, waiting for transfers between devices, spread(): return lax.all_gather(local_rows, 'tp', axis=0, tiled=True)  256 us
    unnamed x26, waiting for transfers between devices  145 us
    reduce_scatter x1, waiting for transfers between devices, on_device(): lax.psum_scatter(query_grad.astype(jnp.bfloat16), 'fsdp', scatter_dimensi...  61.1 us
    reduce_scatter x1, waiting for transfers between devices, on_device(): lax.psum_scatter(value_grad.astype(jnp.bfloat16), 'fsdp', scatter_dimensi...  60.8 us
    reduce_scatter x1, waiting for transfers between devices, on_device(): lax.psum_scatter(key_grad.astype(jnp.bfloat16), 'fsdp', scatter_dimension...  60.8 us
    dot_general x13, matrix products, against_rows(): lax.dot_general(factor_left, factor_right, (((1,), (1,)), ((), ())), pref...  58.5 us
    dot_general x11, matrix products, times_right(): jnp.dot(factor_left, factor_right, preferred_element_type=jnp.float32)  52.9 us
  transfers between devices with their start and end apart: 24, of which 21 were waited for; matrix products, arithmetic and copies ran while one was open for 16% of the time, Pallas kernels for 0%

commit v1 on v0

v1 whole, which is shorter than its diff:
```python
import functools
import math

import jax
import jax.numpy as jnp
from jax import lax
from jax.experimental import pallas as pl
from jax.experimental.pallas import tpu as pltpu
from jax.sharding import PartitionSpec as P

HD = 128
EPS = 1e-05
ROPE_BASE = 10000.0
F32 = jnp.float32
BF16 = jnp.bfloat16
MESH = pl.DeviceIdType.MESH
AXES = ("fsdp", "tp")
ROWS = 128
WIDE = 2048
PACK = 768
SCALE = 1.0 / math.sqrt(HD)
LOG2E = 1.4426950408889634
VMEM = 56 << 20


class Spot:
    def __init__(self):
        f, t = lax.axis_index("fsdp"), lax.axis_index("tp")
        self.y, self.xl, self.c = lax.div(f, 4), lax.rem(lax.div(f, 2), 2), lax.rem(f, 2)
        self.z, self.xh = lax.div(t, 2), lax.rem(t, 2)
        self.x = self.xh * 2 + self.xl
        self.own = self.xl * 2 + self.c
        self.away = lax.rem(self.xh + self.c, 2)
        self.home = self.away == 0

    def at(self, dy=0, dx=0, dz=0, core=None):
        y, z, x = lax.rem(self.y + dy, 4), lax.rem(self.z + dz, 4), lax.rem(self.x + dx, 4)
        return (y * 4 + lax.rem(x, 2) * 2 + (self.c if core is None else core), z * 2 + lax.div(x, 2))

    def other(self):
        return self.at(core=1 - self.c)

    def seat(self, slot):
        return (self.y * 4 + slot, self.z * 2 + self.c)

    def bench(self, slot):
        return (self.y * 4 + slot, self.z * 2 + self.xh)

    def block(self, dz=0, flip=False):
        return (1 - self.c if flip else self.c) * 4 + lax.rem(self.z + dz, 4)


class Post:
    def __init__(self, out_sems, in_sems):
        self.out_sems, self.in_sems, self.n_out, self.n_in = out_sems, in_sems, 0, 0

    def slots(self, n):
        base = self.n_in
        self.n_in += n
        return base

    def copy(self, src, dst, device, slot=None):
        slot = self.slots(1) if slot is None else slot
        self.n_out += 1
        return pltpu.make_async_remote_copy(
            src_ref=src,
            dst_ref=dst,
            send_sem=self.out_sems.at[self.n_out - 1],
            recv_sem=self.in_sems.at[slot],
            device_id=device,
            device_id_type=MESH,
        )

    def local(self, src, dst):
        self.n_out += 1
        return pltpu.make_async_copy(src, dst, self.out_sems.at[self.n_out - 1])


def greet(spot, sources, away_source, count):
    barrier = pltpu.get_barrier_semaphore()
    for source in sources:
        pl.semaphore_signal(barrier, inc=1, device_id=source, device_id_type=MESH)
    if away_source is not None:

        @pl.when(jnp.logical_not(spot.home))
        def _():
            pl.semaphore_signal(barrier, inc=1, device_id=away_source, device_id_type=MESH)

        count = count + spot.away
    pl.semaphore_wait(barrier, count)


def row_peers(spot):
    return [spot.at(dz=1), spot.at(dz=3), spot.other()]


def y_peers(spot):
    return [spot.at(dy=k) for k in (1, 2, 3)]


def after(spot, k):
    return lax.rem(spot.own + k, 4)


def run(*jobs):
    live = list(jobs)
    while live:
        for job in list(live):
            try:
                next(job)
            except StopIteration:
                live.remove(job)


def gather_rows(spot, post, own, rows):
    up, down, core = spot.at(dz=1), spot.at(dz=3), spot.other()
    half = ROWS // 2
    low, high = pl.ds(0, half), pl.ds(half, half)
    here, below, above, far = (spot.block(dz) for dz in (0, 3, 1, 2))
    a = post.copy(own, rows.at[here], up)
    b = post.copy(own, rows.at[here], down)
    k0 = post.copy(own, rows.at[here], core)
    keep = post.local(own, rows.at[here])
    for copy in (a, b, k0, keep):
        copy.start()
    yield
    a.wait_recv()
    fa = post.copy(rows.at[below, low], rows.at[below, low], up)
    k1 = post.copy(rows.at[below], rows.at[below], core)
    fa.start()
    k1.start()
    b.wait_recv()
    fb = post.copy(rows.at[above, high], rows.at[above, high], down)
    k2 = post.copy(rows.at[above], rows.at[above], core)
    fb.start()
    k2.start()
    yield
    fa.wait_recv()
    fb.wait_recv()
    k3 = post.copy(rows.at[far], rows.at[far], core)
    k3.start()
    yield
    keep.wait()
    for copy in (k0, k1, k2, k3):
        copy.wait_recv()
    for copy in (a, b, fa, fb, k0, k1, k2, k3):
        copy.wait_send()


def in_strips(count, body):
    def step(i, carry):
        body(pl.ds(pl.multiple_of(i * 16, 16), 16))
        return carry

    lax.fori_loop(0, count // 16, step, 0)


def add_into(target, other, rows=ROWS, start=0):
    def body(strip):
        strip = pl.ds(pl.multiple_of(strip.start + start, 16), 16)
        target[strip, :] = (target[strip, :].astype(F32) + other[strip, :].astype(F32)).astype(BF16)

    in_strips(rows, body)


def scatter_rows(spot, post, part, mine, land, far, gone):
    up, down, core = spot.at(dz=1), spot.at(dz=3), spot.other()
    half = ROWS // 2
    low, high = pl.ds(0, half), pl.ds(half, half)
    steps = [lax.rem(spot.z + dz, 4) for dz in (2, 3, 1, 0)]
    to_core = [post.copy(part.at[(1 - spot.c) * 4 + s], land.at[s], core) for s in steps]
    load = [post.local(part.at[spot.c * 4 + s], mine.at[s]) for s in steps]
    for a, b in zip(to_core, load):
        a.start()
        b.start()
    yield

    def ready(k):
        to_core[k].wait_recv()
        load[k].wait()

    distant, lower, upper, here = steps
    ready(0)
    add_into(mine.at[distant], land.at[distant])
    f_low = post.copy(mine.at[distant, low], far.at[low], down)
    f_high = post.copy(mine.at[distant, high], far.at[high], up)
    f_low.start()
    f_high.start()
    ready(1)
    add_into(mine.at[lower], land.at[lower])
    d_high = post.copy(mine.at[lower, high], gone.at[0, high], down)
    d_high.start()
    ready(2)
    add_into(mine.at[upper], land.at[upper])
    u_low = post.copy(mine.at[upper, low], gone.at[1, low], up)
    u_low.start()
    ready(3)
    yield
    f_low.wait_recv()
    add_into(mine.at[lower], far, half)
    d_low = post.copy(mine.at[lower, low], gone.at[0, low], down)
    d_low.start()
    f_high.wait_recv()
    add_into(mine.at[upper], far, half, half)
    u_high = post.copy(mine.at[upper, high], gone.at[1, high], up)
    u_high.start()
    yield
    for copy in (d_high, u_low, d_low, u_high):
        copy.wait_recv()
    for copy in to_core + [f_low, f_high, d_high, u_low, d_low, u_high]:
        copy.wait_send()


def row_sum(spot, mine, land, gone, strip):
    parts = [mine[spot.z, strip, :], land[spot.z, strip, :], gone[0, strip, :], gone[1, strip, :]]
    return sum(part.astype(F32) for part in parts)


def scatter_scratch():
    block = (ROWS, WIDE)
    return [
        pltpu.VMEM((4,) + block, BF16),
        pltpu.VMEM((4,) + block, BF16),
        pltpu.VMEM(block, BF16),
        pltpu.VMEM((2,) + block, BF16),
    ]


def x_spread(spot, post, src, dst_at):
    base = post.slots(4)
    copies = [post.copy(src, dst_at(spot.own), spot.at(dx=k, core=spot.xh), base + spot.own) for k in range(4)]
    keep = post.local(src, dst_at(spot.own))
    return x_start(spot, post, copies, keep, lambda k: (src, dst_at(after(spot, k)), base + after(spot, k)))


def x_collect(spot, post, src_at, dst):
    base = post.slots(4)
    copies = [post.copy(src_at(spot.own), dst.at[spot.x], spot.seat(spot.own), base + spot.x)]
    copies += [
        post.copy(src_at(after(spot, k)), dst.at[spot.x], spot.seat(after(spot, k)), base + spot.x) for k in (1, 2, 3)
    ]
    keep = post.local(src_at(spot.own), dst.at[spot.x])

    def arrival(k):
        x = lax.rem(spot.x + k, 4)
        return src_at(spot.own), dst.at[x], base + x

    return x_start(spot, post, copies, keep, arrival)


def x_start(spot, post, copies, keep, arrival):
    for k in (2, 1, 3):
        copies[k].start()

    @pl.when(spot.home)
    def _():
        keep.start()

    @pl.when(jnp.logical_not(spot.home))
    def _():
        copies[0].start()

    def landed(k):
        src, dst, slot = arrival(k)
        pltpu.make_async_remote_copy(
            src_ref=src,
            dst_ref=dst,
            send_sem=post.out_sems.at[0],
            recv_sem=post.in_sems.at[slot],
            device_id=spot.at(dx=1),
            device_id_type=MESH,
        ).wait_recv()

    def arrive():
        for k in (1, 3, 2):
            landed(k)

        @pl.when(spot.home)
        def _():
            keep.wait()

        @pl.when(jnp.logical_not(spot.home))
        def _():
            landed(0)

    def leave():
        for k in (1, 2, 3):
            copies[k].wait_send()

        @pl.when(jnp.logical_not(spot.home))
        def _():
            copies[0].wait_send()

    return arrive, leave


def gather_weights(spot, post, shard, full, stage):
    here = full.at[spot.y, :, 0]
    a1_arrive, a1_leave = x_spread(spot, post, shard.at[0], lambda slot: full.at[spot.y, slot, 0])
    keep = post.local(shard.at[1], stage.at[spot.y])
    b1 = [post.copy(shard.at[1], stage.at[spot.y], spot.at(dy=k)) for k in (2, 1, 3)]
    for copy in [keep] + b1:
        copy.start()
    yield
    a1_arrive()
    a2 = [post.copy(here, here, spot.at(dy=k)) for k in (2, 1, 3)]
    for copy in a2:
        copy.start()
    keep.wait()
    for copy in b1:
        copy.wait_recv()
    b2_arrive, b2_leave = x_spread(spot, post, stage, lambda slot: full.at[:, slot, 1])
    yield
    for copy in a2:
        copy.wait_recv()
    b2_arrive()
    a1_leave()
    b2_leave()
    for copy in b1 + a2:
        copy.wait_send()


def gather_sources(spot):
    return [spot.seat(after(spot, k)) for k in (1, 2, 3)], spot.seat(spot.own)


def scatter_sources(spot):
    return [spot.at(dx=k, core=spot.xh) for k in (1, 2, 3)], spot.at(core=spot.xh)


def sum_four(parts, write, rows=64):
    def body(strip):
        write(strip, sum(part[strip, :].astype(F32) for part in parts))

    in_strips(rows, body)


def scatter_weights(spot, post, full, out, from_x, from_y, sum_a, sum_b, last_y, last_x):
    a1_arrive, a1_leave = x_collect(spot, post, lambda slot: full.at[:, slot, 0], from_x)
    b1 = []
    for i, k in enumerate((2, 1, 3)):
        y = lax.rem(spot.y + k, 4)
        b1.append(post.copy(full.at[y, :, 1], from_y.at[i], spot.at(dy=k)))
    keep = post.local(full.at[spot.y, :, 1], from_y.at[3])
    for copy in b1 + [keep]:
        copy.start()
    yield
    a1_arrive()
    a2 = []
    for i, k in enumerate((2, 1, 3, 0)):
        y = lax.rem(spot.y + k, 4)

        def write_a(strip, total, y=y):
            sum_a[y, strip, :] = total.astype(BF16)

        sum_four([from_x.at[j, y] for j in range(4)], write_a)
        if k:
            a2.append(post.copy(sum_a.at[y], last_y.at[i], spot.at(dy=k)))
            a2[-1].start()
    for copy in b1:
        copy.wait_recv()
    keep.wait()
    for slot in range(4):

        def write_b(strip, total, slot=slot):
            sum_b[slot, strip, :] = total.astype(BF16)

        sum_four([from_y.at[j, slot] for j in range(4)], write_b)
    b2_arrive, b2_leave = x_collect(spot, post, lambda slot: sum_b.at[slot], last_x)
    yield
    for copy in a2:
        copy.wait_recv()

    def write_low(strip, total):
        out[strip, :] = total

    sum_four([last_y.at[0], last_y.at[1], last_y.at[2], sum_a.at[spot.y]], write_low)
    b2_arrive()

    def write_high(strip, total):
        out[pl.ds(pl.multiple_of(strip.start + 64, 16), 16), :] = total

    sum_four([last_x.at[j] for j in range(4)], write_high)
    a1_leave()
    b2_leave()
    for copy in b1 + a2:
        copy.wait_send()


def weight_scratch(n):
    return [
        pltpu.VMEM((4, 4, 64, n), BF16),
        pltpu.VMEM((4, 4, 64, n), BF16),
        pltpu.VMEM((4, 64, n), BF16),
        pltpu.VMEM((4, 64, n), BF16),
        pltpu.VMEM((3, 64, n), BF16),
        pltpu.VMEM((4, 64, n), BF16),
    ]


def sum_gains(spot, post, parts, out, from_y, over_y, from_chip, over_fsdp, from_tp):
    y_copies = []
    for i, k in enumerate((2, 1, 3)):
        y = lax.rem(spot.y + k, 4)
        y_copies.append(post.copy(parts.at[pl.ds(y * 4, 4)], from_y.at[i], spot.at(dy=k)))
        y_copies[-1].start()
    yield
    for copy in y_copies:
        copy.wait_recv()
    over_y[...] = parts[pl.ds(spot.y * 4, 4)] + from_y[0] + from_y[1] + from_y[2]
    chip_copies = []
    for i, k in enumerate((1, 2, 3)):
        slot = after(spot, k)
        chip_copies.append(post.copy(over_y.at[slot], from_chip.at[i], spot.bench(slot)))
        chip_copies[-1].start()
    yield
    for copy in chip_copies:
        copy.wait_recv()
    over_fsdp[...] = over_y[spot.own] + from_chip[0] + from_chip[1] + from_chip[2]
    tp_copies = []
    for i, (dz, dx) in enumerate(TP_MOVES):
        tp_copies.append(post.copy(over_fsdp, from_tp.at[i], spot.at(dz=dz, dx=dx)))
        tp_copies[-1].start()
    yield
    for copy in tp_copies:
        copy.wait_recv()
    out[...] = over_fsdp[...] + sum(from_tp[i] for i in range(7))
    for copy in y_copies + chip_copies + tp_copies:
        copy.wait_send()


TP_MOVES = [(dz, dx) for dx in (0, 2) for dz in (0, 1, 2, 3) if (dz, dx) != (0, 0)]


def gain_sources(spot):
    return (
        y_peers(spot)
        + [spot.bench(after(spot, k)) for k in (1, 2, 3)]
        + [spot.at(dz=(4 - dz) % 4, dx=dx) for dz, dx in TP_MOVES]
    )


ANY = pl.BlockSpec(memory_space=pl.ANY)
INSIDE = pl.BlockSpec(memory_space=pltpu.VMEM)


def sems(n):
    return [pltpu.SemaphoreType.DMA((n,)), pltpu.SemaphoreType.DMA((n,))]


def moving(kernel, name, outs, inputs, in_specs, out_specs, scratch, cid):
    return pl.pallas_call(
        kernel,
        name=name,
        out_shape=outs,
        in_specs=in_specs,
        out_specs=out_specs,
        scratch_shapes=scratch,
        compiler_params=pltpu.CompilerParams(collective_id=cid, has_side_effects=True, vmem_limit_bytes=VMEM),
    )(*inputs)


def shape(dims, dtype):
    return jax.ShapeDtypeStruct(dims, dtype)


def normed(rows, gain):
    inverse = lax.rsqrt(jnp.mean(rows * rows, -1, keepdims=True) + EPS)
    scaled = rows * inverse
    return inverse, scaled, (scaled * gain).astype(BF16)


def enter(tokens, gain, shard):
    n = shard.shape[1]

    def kernel(tokens_ref, gain_ref, shard_ref, rows_ref, full_ref, stage_ref, own, out_sems, in_sems):
        spot, post = Spot(), Post(out_sems, in_sems)
        seats, away = gather_sources(spot)
        greet(spot, row_peers(spot) + y_peers(spot) + seats, away, 9)
        weights = gather_weights(spot, post, shard_ref, full_ref, stage_ref)
        next(weights)

        def body(strip):
            own[strip, :] = normed(tokens_ref[strip, :].astype(F32), gain_ref[...])[2]

        in_strips(ROWS, body)
        run(weights, gather_rows(spot, post, own, rows_ref))

    return moving(
        kernel,
        "enter",
        (shape((8, ROWS, WIDE), BF16), shape((4, 4, 2, 64, n), BF16), shape((4, 64, n), BF16)),
        (tokens, gain, shard.reshape(2, 64, n)),
        [INSIDE, INSIDE, ANY],
        (ANY, ANY, ANY),
        [pltpu.VMEM((ROWS, WIDE), BF16)] + sems(40),
        1,
    )[:2]


def middle(part, tokens, gain, cotangent, shard):
    n = shard.shape[1]

    def kernel(
        part_ref, tokens_ref, gain_ref, cot_ref, shard_ref, mid_ref, rows_ref, grads_ref, full_ref, stage_ref, own, *rest
    ):
        scatter, (out_sems, in_sems) = rest[:4], rest[4:]
        mine, land, far, gone = scatter
        spot, post = Spot(), Post(out_sems, in_sems)
        seats, away = gather_sources(spot)
        greet(spot, row_peers(spot) + y_peers(spot) + seats, away, 9)

        def main():
            yield from scatter_rows(spot, post, part_ref, mine, land, far, gone)

            def body(strip):
                mid = tokens_ref[strip, :].astype(F32) + row_sum(spot, mine, land, gone, strip)
                mid_ref[strip, :] = mid
                own[strip, :] = normed(mid, gain_ref[...])[2]

            in_strips(ROWS, body)
            yield from gather_rows(spot, post, own, rows_ref)

        def second():
            for _ in range(4):
                yield
            yield from gather_rows(spot, post, cot_ref, grads_ref)

        run(main(), gather_weights(spot, post, shard_ref, full_ref, stage_ref), second())

    rows = shape((8, ROWS, WIDE), BF16)
    return moving(
        kernel,
        "middle",
        (shape((ROWS, WIDE), F32), rows, rows, shape((4, 4, 2, 64, n), BF16), shape((4, 64, n), BF16)),
        (part, tokens, gain, cotangent, shard.reshape(2, 64, n)),
        [ANY, INSIDE, INSIDE, ANY, ANY],
        (INSIDE, ANY, ANY, ANY, ANY),
        [pltpu.VMEM((ROWS, WIDE), BF16)] + scatter_scratch() + sems(64),
        2,
    )[:4]


def norm_back(upstream, rows, gain):
    inverse, scaled, _ = normed(rows, gain)
    weighted = upstream * gain
    through = inverse * (weighted - scaled * jnp.mean(weighted * scaled, -1, keepdims=True))
    return through, jnp.sum(upstream * scaled, 0, keepdims=True)


def turn(part, part_out, mid, gain, cotangent, full):
    n = full.shape[1]

    def kernel(
        part_ref, out_part_ref, mid_ref, gain_ref, cot_ref, full_ref, layer_ref, grad_ref, rows_ref, feed_ref, weight_ref,
        own, *rest,
    ):
        first, second, weights, (out_sems, in_sems) = rest[:4], rest[4:8], rest[8:14], rest[14:]
        spot, post = Spot(), Post(out_sems, in_sems)
        sources, away = scatter_sources(spot)
        greet(spot, row_peers(spot) + y_peers(spot) + sources, away, 9)

        def main():
            yield from scatter_rows(spot, post, part_ref, *first)
            feed_ref[...] = jnp.zeros_like(feed_ref)

            def body(strip):
                upstream = row_sum(spot, first[0], first[1], first[3], strip)
                through, feed = norm_back(upstream, mid_ref[strip, :], gain_ref[...])
                grad = cot_ref[strip, :].astype(F32) + through
                grad_ref[strip, :] = grad
                own[strip, :] = grad.astype(BF16)
                feed_ref[...] += feed

            in_strips(ROWS, body)
            yield from gather_rows(spot, post, own, rows_ref)

        def output():
            for _ in range(4):
                yield
            yield from scatter_rows(spot, post, out_part_ref, *second)

            def body(strip):
                layer_ref[strip, :] = (mid_ref[strip, :] + row_sum(spot, second[0], second[1], second[3], strip)).astype(BF16)

            in_strips(ROWS, body)

        run(main(), scatter_weights(spot, post, full_ref, weight_ref, *weights), output())

    return moving(
        kernel,
        "turn",
        (
            shape((ROWS, WIDE), BF16),
            shape((ROWS, WIDE), F32),
            shape((8, ROWS, WIDE), BF16),
            shape((1, WIDE), F32),
            shape((ROWS, n), F32),
        ),
        (part, part_out, mid, gain, cotangent, full.reshape(4, 4, 2, 64, n)),
        [ANY, ANY, INSIDE, INSIDE, INSIDE, ANY],
        (INSIDE, INSIDE, ANY, INSIDE, INSIDE),
        [pltpu.VMEM((ROWS, WIDE), BF16)] + scatter_scratch() * 2 + weight_scratch(n) + sems(80),
        3,
    )


def leave(part, tokens, gain, grad_mid, feed_part, full):
    n = full.shape[1]

    def kernel(
        part_ref, tokens_ref, gain_ref, grad_ref, feed_ref, full_ref, token_ref, gains_ref, weight_ref, norm_part, parts,
        from_y, over_y, from_chip, over_fsdp, from_tp, *rest,
    ):
        first, weights, (out_sems, in_sems) = rest[:4], rest[4:10], rest[10:]
        spot, post = Spot(), Post(out_sems, in_sems)
        sources, away = scatter_sources(spot)
        greet(spot, row_peers(spot) + y_peers(spot) + sources + gain_sources(spot), away, 9 + 13)

        def main():
            yield from scatter_rows(spot, post, part_ref, *first)
            norm_part[...] = jnp.zeros_like(norm_part)

            def body(strip):
                upstream = row_sum(spot, first[0], first[1], first[3], strip)
                through, norm = norm_back(upstream, tokens_ref[strip, :].astype(F32), gain_ref[...])
                token_ref[strip, :] = grad_ref[strip, :] + through
                norm_part[...] += norm

            in_strips(ROWS, body)
            parts[...] = jnp.zeros_like(parts)
            for f in range(16):
                parts[f, 0:1, :] = norm_part[:, f * 128 : (f + 1) * 128]
                parts[f, 1:2, :] = feed_ref[:, f * 128 : (f + 1) * 128]
            yield from sum_gains(spot, post, parts, gains_ref, from_y, over_y, from_chip, over_fsdp, from_tp)

        run(main(), scatter_weights(spot, post, full_ref, weight_ref, *weights))

    small = (8, 128)
    return moving(
        kernel,
        "leave",
        (shape((ROWS, WIDE), F32), shape(small, F32), shape((ROWS, n), F32)),
        (part, tokens, gain, grad_mid, feed_part, full.reshape(4, 4, 2, 64, n)),
        [ANY, INSIDE, INSIDE, INSIDE, INSIDE, ANY],
        (INSIDE, INSIDE, INSIDE),
        [pltpu.VMEM((1, WIDE), F32), pltpu.VMEM((16,) + small, F32)]
        + [pltpu.VMEM(dims + small, F32) for dims in ((3, 4), (4,), (3,), (), (7,))]
        + scatter_scratch()
        + weight_scratch(n)
        + sems(80),
        4,
    )


def dot(a, b, da=1, db=0):
    return lax.dot_general(a, b, (((da,), (db,)), ((), ())), preferred_element_type=F32)


def plain(kernel, name, grid, inputs, in_specs, outs, out_specs, scratch=()):
    return pl.pallas_call(
        kernel,
        name=name,
        out_shape=outs,
        grid=grid,
        in_specs=in_specs,
        out_specs=out_specs,
        scratch_shapes=list(scratch),
        compiler_params=pltpu.CompilerParams(vmem_limit_bytes=VMEM),
    )(*inputs)


def by_rows(n, width, column=0):
    return pl.BlockSpec((n, width), lambda i: (i, column))


def whole(dims, *index):
    at = index or (0,) * len(dims)
    return pl.BlockSpec(dims, lambda i: at)


def project(rows, weights, cosine, sine):
    step = 256

    def kernel(rows_ref, w_ref, cos_ref, sin_ref, q_ref, k_ref, v_ref):
        out = dot(rows_ref[...], w_ref[...])
        cos, sin = cos_ref[...], sin_ref[...]
        for head in range(4):
            u = out[:, head * HD : (head + 1) * HD]
            turned = (u * cos + pltpu.roll(u, HD // 2, 1) * sin).astype(BF16)
            target = q_ref if head < 2 else k_ref
            target[:, head % 2 * HD : (head % 2 + 1) * HD] = turned
        v_ref[...] = out[:, 4 * HD :].astype(BF16)

    out = shape((8 * ROWS, 2 * HD), BF16)
    return plain(
        kernel,
        "project",
        (8 * ROWS // step,),
        (rows, weights, cosine, sine),
        [by_rows(step, WIDE), whole((WIDE, PACK)), by_rows(step, HD), by_rows(step, HD)],
        (out, out, out),
        (by_rows(step, 2 * HD),) * 3,
    )


def partial_rows(pairs, name, extra=None):
    step = 256
    sets = [pairs] + ([extra] if extra else [])
    flat = [pair for group in sets for pair in group]

    def kernel(*refs):
        values, outs = refs[: 2 * len(flat)], refs[2 * len(flat) :]
        at = 0
        for group, out in zip(sets, outs):
            total = None
            for _ in group:
                term = dot(values[at][...], values[at + 1][...], 1, 1)
                total = term if total is None else total + term
                at += 2
            out[...] = total.astype(BF16)

    inputs, specs = [], []
    for a, b, width, column in flat:
        inputs += [a, b]
        specs += [by_rows(step, width), whole((WIDE, width), 0, column)]
    out = tuple(shape((8 * ROWS, WIDE), BF16) for _ in sets)
    return plain(kernel, name, (8 * ROWS // step,), inputs, specs, out, tuple(by_rows(step, WIDE) for _ in sets))


def feed_forward(rows, grads, weights):
    step = 256

    def kernel(rows_ref, grads_ref, g_ref, u_ref, d_ref, hid_ref, dgate_ref, dup_ref):
        gate = dot(rows_ref[...], g_ref[...])
        up = dot(rows_ref[...], u_ref[...])
        d_hid = dot(grads_ref[...], d_ref[...])
        sigma = 1.0 / (1.0 + jnp.exp(-gate))
        silu = gate * sigma
        hid_ref[...] = (silu * up).astype(BF16)
        dup_ref[...] = (d_hid * silu).astype(BF16)
        dgate_ref[...] = (d_hid * up * sigma * (1.0 + gate * (1.0 - sigma))).astype(BF16)

    out = shape((8 * ROWS, PACK), BF16)
    return plain(
        kernel,
        "feed_forward",
        (8 * ROWS // step,),
        (rows, grads, weights, weights, weights),
        [by_rows(step, WIDE)] * 2 + [whole((WIDE, PACK), 0, i) for i in range(3)],
        (out,) * 3,
        (by_rows(step, PACK),) * 3,
    )


def outer(groups, name):
    step = 256
    count = 8 * ROWS

    def kernel(*refs):
        out = refs[-1]
        at, column = 0, 0
        for rows, values in groups:
            left = refs[at][...]
            for i, value in enumerate(values):
                width = value.shape[1]
                out[:, column : column + width] = dot(left, refs[at + 1 + i][...], 0, 0).astype(BF16)
                column += width
            at += 1 + len(values)

    inputs, specs, total = [], [], 0
    for rows, values in groups:
        inputs += [rows] + list(values)
        specs += [pl.BlockSpec((count, step), lambda i: (0, i))] + [whole(value.shape) for value in values]
        total += sum(value.shape[1] for value in values)
    return plain(kernel, name, (WIDE // step,), inputs, specs, shape((WIDE, total), BF16), by_rows(step, total))


def back_to_heads(rows, weights):
    step = 256

    def kernel(rows_ref, w_ref, out_ref):
        out_ref[...] = dot(rows_ref[...], w_ref[...]).astype(BF16)

    return plain(
        kernel,
        "back_to_heads",
        (8 * ROWS // step,),
        (rows, weights),
        [by_rows(step, WIDE), whole((WIDE, 2 * HD), 0, 3)],
        shape((8 * ROWS, 2 * HD), BF16),
        by_rows(step, 2 * HD),
    )


TILE = 256
CHUNK = 512


def place_of(start, count, xh, axis):
    dims = (count, 1) if axis == 0 else (1, count)
    j = lax.broadcasted_iota(jnp.int32, dims, axis)
    return 2 * (j + start) - lax.rem(j, ROWS) + xh * ROWS


def key_chunks():
    return [(((0, 0, 512),), None), (((1, 0, 512),), None), (((0, 512, 256), (1, 512, 256)), "near")], (
        ((0, 768, 256), (1, 768, 256)),
        "far",
    )


def allowed_in(pieces, q_pos, prefix, xh):
    k_pos = jnp.concatenate([place_of(start, count, lax.rem(xh + side, 2), 0) for side, start, count in pieces], 0)
    return jnp.logical_or(k_pos <= q_pos, k_pos < prefix)


def take(pieces, sides, which, cols):
    parts = [sides[side][which, pl.ds(start, count), cols] for side, start, count in pieces]
    return parts[0] if len(parts) == 1 else jnp.concatenate(parts, 0)


def attend(meta, queries, here, there):
    def kernel(meta_ref, q_ref, here_ref, there_ref, o_ref, lse_ref, top_ref, sum_ref, acc_ref):
        prefix, xh = meta_ref[0], meta_ref[1]
        sides = (here_ref, there_ref)
        always, last = key_chunks()

        def step(i, carry):
            head, tile = lax.div(i, 4), lax.rem(i, 4)
            cols = pl.ds(pl.multiple_of(head * HD, HD), HD)
            rows = pl.ds(pl.multiple_of(tile * TILE, TILE), TILE)
            q = q_ref[rows, cols]
            q_pos = place_of(tile * TILE, TILE, xh, 1)

            def chunk(pieces, masked, first):
                keys = take(pieces, sides, 0, cols)
                scores = dot(keys, q, 1, 1) * (SCALE * LOG2E)
                if masked:
                    scores = jnp.where(allowed_in(pieces, q_pos, prefix, xh), scores, -1e30)
                top = jnp.max(scores, 0, keepdims=True)
                if not first:
                    before = top_ref[...]
                    top = jnp.maximum(top, before)
                raised = jnp.exp2(scores - top)
                total = jnp.sum(raised, 0, keepdims=True)
                mixed = dot(take(pieces, sides, 1, cols), raised.astype(BF16), 0, 0)
                if not first:
                    fade = jnp.exp2(before - top)
                    total = total + sum_ref[...] * fade
                    mixed = mixed + acc_ref[...] * fade
                top_ref[...] = top
                sum_ref[...] = total
                acc_ref[...] = mixed

            for number, (pieces, masked) in enumerate(always):
                chunk(pieces, masked, number == 0)

            @pl.when(tile == 3)
            def _():
                chunk(*last, False)

            total = sum_ref[...]
            o_ref[rows, cols] = (acc_ref[...] / total).T.astype(BF16)
            lse_ref[pl.ds(i, 1), :] = top_ref[...] + jnp.log2(total)
            return carry

        lax.fori_loop(0, 8, step, 0)

    return pl.pallas_call(
        kernel,
        name="attend",
        out_shape=(shape((8 * ROWS, 2 * HD), BF16), shape((8, TILE), F32)),
        in_specs=[pl.BlockSpec(memory_space=pltpu.SMEM), INSIDE, INSIDE, INSIDE],
        out_specs=(INSIDE, INSIDE),
        scratch_shapes=[pltpu.VMEM((1, TILE), F32), pltpu.VMEM((1, TILE), F32), pltpu.VMEM((HD, TILE), F32)],
        compiler_params=pltpu.CompilerParams(vmem_limit_bytes=VMEM),
    )(meta, queries, here, there)


def attend_back(meta, queries, here, there, grads, lse, delta, cosine, sine):
    def kernel(
        meta_ref, q_ref, here_ref, there_ref, g_ref, lse_ref, delta_ref, cos_ref, sin_ref, dq_ref, near_ref, far_ref,
        dq_acc, acc_here, acc_there,
    ):
        prefix, xh = meta_ref[0], meta_ref[1]
        sides, accs = (here_ref, there_ref), (acc_here, acc_there)
        always, last = key_chunks()
        acc_here[...] = jnp.zeros_like(acc_here)
        acc_there[...] = jnp.zeros_like(acc_there)

        def step(i, carry):
            head, tile = lax.div(i, 4), lax.rem(i, 4)
            cols = pl.ds(pl.multiple_of(head * HD, HD), HD)
            rows = pl.ds(pl.multiple_of(tile * TILE, TILE), TILE)
            q, g = q_ref[rows, cols], g_ref[rows, cols]
            q_pos = place_of(tile * TILE, TILE, xh, 1)
            level, offset = lse_ref[pl.ds(i, 1), :], delta_ref[pl.ds(i, 1), :]

            def chunk(pieces, masked, first):
                keys = take(pieces, sides, 0, cols)
                scores = dot(keys, q, 1, 1) * (SCALE * LOG2E)
                if masked:
                    scores = jnp.where(allowed_in(pieces, q_pos, prefix, xh), scores, -1e30)
                probs = jnp.exp2(scores - level)
                d_probs = dot(take(pieces, sides, 1, cols), g, 1, 1)
                d_scores = (probs * (d_probs - offset)).astype(BF16)
                d_values = dot(probs.astype(BF16), g)
                d_keys = dot(d_scores, q)
                at = 0
                for side, start, count in pieces:
                    span = pl.ds(start, count)
                    accs[side][0, span, cols] += d_keys[at : at + count]
                    accs[side][1, span, cols] += d_values[at : at + count]
                    at += count
                d_query = dot(d_scores, keys, 0, 0)
                dq_acc[...] = d_query if first else dq_acc[...] + d_query

            for number, (pieces, masked) in enumerate(always):
                chunk(pieces, masked, number == 0)

            @pl.when(tile == 3)
            def _():
                chunk(*last, False)

            u = dq_acc[...] * SCALE
            dq_ref[rows, cols] = (u * cos_ref[rows, :] - pltpu.roll(u, HD // 2, 1) * sin_ref[rows, :]).astype(BF16)
            return carry

        lax.fori_loop(0, 8, step, 0)
        near_ref[...] = acc_here[...]
        far_ref[...] = acc_there[...].astype(BF16)

    pair = (2, 8 * ROWS, 2 * HD)
    return pl.pallas_call(
        kernel,
        name="attend_back",
        out_shape=(shape((8 * ROWS, 2 * HD), BF16), shape(pair, F32), shape(pair, BF16)),
        in_specs=[pl.BlockSpec(memory_space=pltpu.SMEM)] + [INSIDE] * 8,
        out_specs=(INSIDE,) * 3,
        scratch_shapes=[pltpu.VMEM((TILE, HD), F32), pltpu.VMEM(pair, F32), pltpu.VMEM(pair, F32)],
        compiler_params=pltpu.CompilerParams(vmem_limit_bytes=VMEM),
    )(meta, queries, here, there, grads, lse, delta, cosine, sine)


def to_far_x(block):
    return lax.ppermute(block, "tp", [(t, t ^ 1) for t in range(8)])


def padded(shard):
    return jnp.pad(shard, ((0, 0), (0, PACK - shard.shape[1])))


def rope_tables(positions):
    counter = jnp.arange(HD // 2, dtype=F32)
    inverse = jnp.exp(counter * (-2.0 / HD) * math.log(ROPE_BASE))
    angles = positions.astype(F32)[:, None] * inverse[None, :]
    cosine, sine = jnp.cos(angles), jnp.sin(angles)
    return jnp.concatenate([cosine, cosine], 1), jnp.concatenate([-sine, sine], 1)


def on_device(
    tokens,
    prefixes,
    norm_gain,
    query_weight,
    key_weight,
    value_weight,
    output_weight,
    feed_gain,
    gate_weight,
    up_weight,
    down_weight,
    cotangent,
):
    sequence = lax.axis_index("fsdp") // 2
    xh = lax.axis_index("tp") % 2
    hidden_here = gate_weight.shape[1]
    width = 2 * HD
    prefix = jnp.sum(jnp.where(jnp.arange(prefixes.shape[0], dtype=jnp.int32) == sequence, prefixes, 0))
    meta = jnp.stack([prefix, xh]).astype(jnp.int32)
    j = jnp.arange(8 * ROWS, dtype=jnp.int32)
    cosine, sine = rope_tables(2 * j - j % ROWS + xh * ROWS)
    gain_one = norm_gain.astype(F32)[None]
    gain_two = feed_gain.astype(F32)[None]
    shard_one = jnp.concatenate([query_weight, key_weight, value_weight, output_weight.T], 1)
    shard_two = jnp.concatenate([padded(gate_weight), padded(up_weight), padded(down_weight.T)], 1)

    rows_one, full_one = enter(tokens, gain_one, shard_one)
    rows_one = rows_one.reshape(-1, WIDE)
    full_one = full_one.reshape(WIDE, -1)
    queries, keys, values = project(rows_one, full_one, cosine, sine)
    here = jnp.stack([keys, values])
    there = to_far_x(here)
    attended, lse = attend(meta, queries, here, there)
    (part,) = partial_rows([(attended, full_one, width, 3)], "attention_out")
    mid, rows_two, grad_rows, full_two = middle(part.reshape(8, ROWS, WIDE), tokens, gain_two, cotangent, shard_two)
    rows_two, grad_rows, full_two = (a.reshape(-1, a.shape[-1]) for a in (rows_two, grad_rows, full_two.reshape(WIDE, -1)))
    hidden, d_gate, d_up = feed_forward(rows_two, grad_rows, full_two)
    part, part_out = partial_rows(
        [(d_gate, full_two, PACK, 0), (d_up, full_two, PACK, 1)], "feed_back", [(hidden, full_two, PACK, 2)]
    )
    grads_two = outer([(rows_two, (d_gate, d_up)), (grad_rows, (hidden,))], "feed_grads")
    layer_output, grad_mid, mid_rows, feed_part, ffn_grad = turn(
        part.reshape(8, ROWS, WIDE), part_out.reshape(8, ROWS, WIDE), mid, gain_two, cotangent, grads_two
    )
    mid_rows = mid_rows.reshape(-1, WIDE)
    grad_mixed = back_to_heads(mid_rows, full_one)
    delta = jnp.sum((grad_mixed.astype(F32) * attended.astype(F32)).reshape(4, TILE, 2, HD), -1)
    delta = delta.transpose(2, 0, 1).reshape(8, TILE)
    d_query, near, far = attend_back(meta, queries, here, there, grad_mixed, lse, delta, cosine, sine)
    d_pair = near + to_far_x(far).astype(F32)
    d_key = (d_pair[0] * SCALE).reshape(-1, 2, HD)
    d_key = d_key * cosine[:, None] - jnp.roll(d_key, HD // 2, -1) * sine[:, None]
    d_qkv = jnp.concatenate([d_query, d_key.reshape(-1, width).astype(BF16), d_pair[1].astype(BF16)], 1)
    (part,) = partial_rows([(d_qkv, full_one, PACK, 0)], "attention_back")
    grads_one = outer([(rows_one, (d_qkv,)), (mid_rows, (attended,))], "attention_grads")
    token_grad, gains, attention_grad = leave(part.reshape(8, ROWS, WIDE), tokens, gain_one, grad_mid, feed_part, grads_one)
    return (
        layer_output,
        token_grad,
        gains[0],
        attention_grad[:, :width],
        attention_grad[:, width : 2 * width],
        attention_grad[:, 2 * width : 3 * width],
        attention_grad[:, 3 * width :].T,
        gains[1],
        ffn_grad[:, :hidden_here],
        ffn_grad[:, PACK : PACK + hidden_here],
        ffn_grad[:, 2 * PACK : 2 * PACK + hidden_here].T,
    )


def solution(mesh):
    rows = P(("fsdp", "tp"), None)
    wide = P("fsdp", "tp")
    tall = P("tp", "fsdp")
    return jax.shard_map(
        on_device,
        mesh=mesh,
        in_specs=(rows, P(), P(), wide, wide, wide, tall, P(), wide, wide, tall, rows),
        out_specs=(rows, rows, P("fsdp"), wide, wide, wide, tall, P("fsdp"), wide, wide, tall),
        check_vma=False,
    )
```

time: 1410 us -> 546 us (0.39)
  waiting for transfers between devices: 1070 us -> 40.4 us
  Pallas kernels: 0 us -> 462 us
  matrix products: 160 us -> 0 us
  blocking collectives: 47.6 us -> 0 us
  other arithmetic: 61.7 us -> 17.3 us
  local copies, waits for them, and re-layouts: 45.9 us -> 20.6 us
  between operations: 16.1 us -> 0.91 us
    reduce_scatter x7 -> x0, waiting for transfers between devices: 474 us -> none  [the longest x4 292 us: collect(): lax.psum_scatter(partial_rows.astype(jnp.bfloat16), 'tp', scatter_dimensi...]
    pallas_call x0 -> x14, Pallas kernels: none -> 462 us  [the longest x4 345 us: moving(): pl.pallas_call(kernel, name=name, out_shape=outs, in_specs=in_specs, out_...]
    all_gather x11 -> x0, waiting for transfers between devices: 446 us -> none  [the longest x4 256 us: spread(): return lax.all_gather(local_rows, 'tp', axis=0, tiled=True)]
    dot_general x35 -> x0, matrix products: 160 us -> none  [the longest x13 58.5 us: against_rows(): lax.dot_general(factor_left, factor_right, (((1,), (1,)), ((), ())), pref...]
    unnamed x26 -> x0, waiting for transfers between devices: 145 us -> none
    ppermute x2, waiting for transfers between devices: 2.29 us -> 40.4 us  [to_far_x(): return lax.ppermute(block, 'tp', [(t, t ^ 1) for t in range(8)])]
    convert_element_type x21 -> x2, other arithmetic: 31.2 us -> 0.38 us  [the longest x1 0.37 us: on_device(): d_key.reshape(-1, width).astype(BF16)]
    unnamed x1 -> x0, blocking collectives: 28.9 us -> none
  transfers between devices with their start and end apart: 24 -> 2, of which waited for: 21 -> 2; matrix products, arithmetic and copies ran while one was open for 16% -> 1% of each run, Pallas kernels for 0% -> 0%
where the time goes in v1:
time: 546 us; the launch traced here: 545 us
  Pallas kernels  462 us (85%)
  waiting for transfers between devices  40.4 us (7%)
  local copies, waits for them, and re-layouts  20.6 us (4%)
  other arithmetic  17.3 us (3%)
    pallas_call x4, Pallas kernels, moving(): pl.pallas_call(kernel, name=name, out_shape=outs, in_specs=in_specs, out_...  345 us
    pallas_call x8, Pallas kernels, plain(): pl.pallas_call(kernel, name=name, out_shape=outs, grid=grid, in_specs=in_...  84.6 us
    ppermute x2, waiting for transfers between devices, to_far_x(): return lax.ppermute(block, 'tp', [(t, t ^ 1) for t in range(8)])  40.4 us
    pallas_call x1, Pallas kernels, attend_back(): pl.pallas_call(kernel, name='attend_back', out_shape=(shape((8 * ROWS, 2...  16.7 us
    pallas_call x1, Pallas kernels, attend(): pl.pallas_call(kernel, name='attend', out_shape=(shape((8 * ROWS, 2 * HD)...  15.5 us
  transfers between devices with their start and end apart: 2, of which 2 were waited for; matrix products, arithmetic and copies ran while one was open for 1% of the time, Pallas kernels for 0%

profile of v1, /device:TPU:1, one launch (start us, length us, event | category | flops | bytes accessed | tf_op | source)
XLA Modules:
  0.0 544.5 jit_solution(6761271570888905113)
XLA Ops:
  0.7 1.3 broadcast_in_dim.23
  2.0 0.9 copy.34
  2.9 1.0 copy.33
  3.9 1.0 copy.32
  4.8 0.9 pad_maximum_fusion.4
  5.7 0.9 copy.35
  6.6 1.9 fusion.8
  8.5 53.7 %enter.1 = (bf16[8,128,2048]{2,1,0:T(8,128)(2,1)}, bf16[4,4,2,64,1024]{4,3,2,1,0:T(8,128)(2,1)}, bf16[4,64,1024]{2,1,0:T(8,128)(2,1)}) custom-call(bf16[128,2048]{1,0:T(8,128)(2,1)} %tokens_ref.5, f32[1,2048]{1,0:T(1,128)} %bitcast.77, bf16[2,64,1024]{2,1,0:T(8,128)(2,1)} %bitcast.73), custom_call_target="tpu_custom_call" | custom-call | tf_op jit(solution)/shard_map/enter/pallas_call | solution.py:452
  62.2 1.3 pad_maximum_fusion.2
  63.5 7.7 %project.1 = (bf16[1024,256]{1,0:T(8,128)(2,1)}, bf16[1024,256]{1,0:T(8,128)(2,1)}, bf16[1024,256]{1,0:T(8,128)(2,1)}) custom-call(bf16[1024,2048]{1,0:T(8,128)(2,1)} %bitcast.57, bf16[2048,1024]{1,0:T(8,128)(2,1)} %bitcast.51, f32[1024,128]{1,0:T(8,128)} %get-tuple-element.101.cos_ref, f32[1024,128]{1,0:T(8,128)} %get-tuple-element.102.sin_ref), custom_call_target="tpu_custom_call" | custom-call | tf_op jit(solution)/shard_map/project/pallas_call | solution.py:661
  71.2 1.4 pad_maximum_fusion.1.here_ref
  72.6 1.3 collective-permute-start
  74.6 1.1 copy.36
  76.3 1.2 pad_add_fusion.meta_ref
  77.6 21.3 %collective-permute-done.there_ref = bf16[2,1024,256]{2,1,0:T(8,128)(2,1)S(1)} collective-permute-done((bf16[2,1024,256]{2,1,0:T(8,128)(2,1)S(1)}, bf16[2,1024,256]{2,1,0:T(8,128)(2,1)S(1)}, u32[]{:S(2)}, u32[]{:S(2)}) %collective-permute-start) | collective-permute-done | bytes 1048608 | tf_op jit(solution)/shard_map/ppermute | solution.py:947
  98.8 1.0 copy-done.4
  99.9 15.5 %attend.1 = (bf16[1024,256]{1,0:T(8,128)(2,1)}, f32[8,256]{1,0:T(8,128)}) custom-call(s32[2]{0:T(128)} %pad_add_fusion.meta_ref, bf16[1024,256]{1,0:T(8,128)(2,1)} %get-tuple-element.40.q_ref, bf16[2,1024,256]{2,1,0:T(8,128)(2,1)} %copy-done, bf16[2,1024,256]{2,1,0:T(8,128)(2,1)} %copy-done.4), custom_call_target="tpu_custom_call" | custom-call | tf_op jit(solution)/shard_map/attend/pallas_call | solution.py:870
  115.4 5.2 attention_out.1
  120.6 117.2 %middle.1 = (f32[128,2048]{1,0:T(8,128)}, bf16[8,128,2048]{2,1,0:T(8,128)(2,1)}, bf16[8,128,2048]{2,1,0:T(8,128)(2,1)}, bf16[4,4,2,64,2304]{4,3,2,1,0:T(8,128)(2,1)}, bf16[4,64,2304]{2,1,0:T(8,128)(2,1)}) custom-call(bf16[8,128,2048]{2,1,0:T(8,128)(2,1)} %bitcast.66, bf16[128,2048]{1,0:T(8,128)(2,1)} %tokens_ref.5, f32[1,2048]{1,0:T(1,128)} %bitcast.79, ...), custom_call_target="tpu_custom_call" | custom-call | tf_op jit(solution)/shard_map/middle/pallas_call | solution.py:452
  237.8 16.3 %feed_forward.1 = (bf16[1024,768]{1,0:T(8,128)(2,1)}, bf16[1024,768]{1,0:T(8,128)(2,1)}, bf16[1024,768]{1,0:T(8,128)(2,1)}) custom-call(bf16[1024,2048]{1,0:T(8,128)(2,1)} %bitcast.62, bf16[1024,2048]{1,0:T(8,128)(2,1)} %bitcast.64, bf16[2048,2304]{1,0:T(8,128)(2,1)} %bitcast.45, bf16[2048,2304]{1,0:T(8,128)(2,1)} %bitcast.46, bf16[2048,2304]{1,0:T(8,128)(2,1)} %bitcast.47), custom_call_target="tpu_custom_call" | custom-call | tf_op jit(solution)/shard_map/feed_forward/pallas_call | solution.py:661
  254.2 16.0 %feed_back.1 = (bf16[1024,2048]{1,0:T(8,128)(2,1)}, bf16[1024,2048]{1,0:T(8,128)(2,1)}) custom-call(bf16[1024,768]{1,0:T(8,128)(2,1)} %get-tuple-element.47.refs_0_.refs_1_, bf16[2048,2304]{1,0:T(8,128)(2,1)} %bitcast.48, bf16[1024,768]{1,0:T(8,128)(2,1)} %get-tuple-element.48.refs_2_, bf16[2048,2304]{1,0:T(8,128)(2,1)} %bitcast.49, ...), custom_call_target="tpu_custom_call" | custom-call | tf_op jit(solution)/shard_map/feed_back/pallas_call | solution.py:661
  270.1 16.1 %feed_grads.1 = bf16[2048,2304]{1,0:T(8,128)(2,1)} custom-call(bf16[1024,2048]{1,0:T(8,128)(2,1)} %bitcast.63, bf16[1024,768]{1,0:T(8,128)(2,1)} %get-tuple-element.47.refs_0_.refs_1_, bf16[1024,768]{1,0:T(8,128)(2,1)} %get-tuple-element.48.refs_2_, bf16[1024,2048]{1,0:T(8,128)(2,1)} %bitcast.65, bf16[1024,768]{1,0:T(8,128)(2,1)} %get-tuple-element.49.refs_4_), custom_call_target="tpu_custom_call" | custom-call | tf_op jit(solution)/shard_map/feed_grads/pallas_call | solution.py:661
  286.2 117.5 %turn.1 = (bf16[128,2048]{1,0:T(8,128)(2,1)}, f32[128,2048]{1,0:T(8,128)}, bf16[8,128,2048]{2,1,0:T(8,128)(2,1)}, f32[1,2048]{1,0:T(1,128)}, f32[128,2304]{1,0:T(8,128)}) custom-call(bf16[8,128,2048]{2,1,0:T(8,128)(2,1)} %bitcast.69, bf16[8,128,2048]{2,1,0:T(8,128)(2,1)} %bitcast.70, f32[128,2048]{1,0:T(8,128)} %get-tuple-element.52.mid_ref, ...), custom_call_target="tpu_custom_call" | custom-call | tf_op jit(solution)/shard_map/turn/pallas_call | solution.py:452
  403.7 5.1 back_to_heads.1.g_ref
  408.8 1.2 convert_multiply_fusion
  410.5 1.1 reduce_sum.19
  412.5 16.7 %attend_back.1 = (bf16[1024,256]{1,0:T(8,128)(2,1)}, f32[2,1024,256]{2,1,0:T(8,128)}, bf16[2,1024,256]{2,1,0:T(8,128)(2,1)}) custom-call(s32[2]{0:T(128)} %pad_add_fusion.meta_ref, bf16[1024,256]{1,0:T(8,128)(2,1)} %get-tuple-element.40.q_ref, bf16[2,1024,256]{2,1,0:T(8,128)(2,1)} %copy-done, bf16[2,1024,256]{2,1,0:T(8,128)(2,1)} %copy-done.4, ...), custom_call_target="tpu_custom_call" | custom-call | tf_op jit(solution)/shard_map/attend_back/pallas_call | solution.py:935
  429.2 2.3 collective-permute-start.1
  431.6 0.9 copy.39
  432.5 0.9 copy.40
  433.4 0.9 copy.41
  434.3 19.1 %collective-permute-done.1 = bf16[2,1024,256]{2,1,0:T(8,128)(2,1)S(1)} collective-permute-done((bf16[2,1024,256]{2,1,0:T(8,128)(2,1)}, bf16[2,1024,256]{2,1,0:T(8,128)(2,1)S(1)}, u32[]{:S(2)}, u32[]{:S(2)}) %collective-permute-start.1) | collective-permute-done | bytes 1048608 | tf_op jit(solution)/shard_map/ppermute | solution.py:947
  453.4 1.8 convert_add_fusion
  455.2 0.9 fusion.7
  456.1 1.1 slice_multiply_fusion
  457.2 1.7 mul.93
  458.9 1.1 fusion.16
  460.1 1.2 maximum_multiply_fusion
  462.1 0.6 copy-done.5
  462.9 1.3 pad_maximum_fusion.refs_0_.refs_1_
  464.2 7.4 %attention_back.1 = bf16[1024,2048]{1,0:T(8,128)(2,1)} custom-call(bf16[1024,768]{1,0:T(8,128)(2,1)} %pad_maximum_fusion.refs_0_.refs_1_, bf16[2048,1024]{1,0:T(8,128)(2,1)} %bitcast.54), custom_call_target="tpu_custom_call" | custom-call | tf_op jit(solution)/shard_map/attention_back/pallas_call | solution.py:661
  471.5 10.8 %attention_grads.1 = bf16[2048,1024]{1,0:T(8,128)(2,1)} custom-call(bf16[1024,2048]{1,0:T(8,128)(2,1)} %bitcast.58, bf16[1024,768]{1,0:T(8,128)(2,1)} %pad_maximum_fusion.refs_0_.refs_1_, bf16[1024,2048]{1,0:T(8,128)(2,1)} %bitcast.60, bf16[1024,256]{1,0:T(8,128)(2,1)} %get-tuple-element.43.refs_0_.refs_3_), custom_call_target="tpu_custom_call" | custom-call | tf_op jit(solution)/shard_map/attention_grads/pallas_call | solution.py:661
  482.4 56.5 %leave.1 = (f32[128,2048]{1,0:T(8,128)}, f32[8,128]{1,0:T(8,128)}, f32[128,1024]{1,0:T(8,128)}) custom-call(bf16[8,128,2048]{2,1,0:T(8,128)(2,1)} %bitcast.61, bf16[128,2048]{1,0:T(8,128)(2,1)} %tokens_ref.5, f32[1,2048]{1,0:T(1,128)} %bitcast.78, f32[128,2048]{1,0:T(8,128)} %get-tuple-element.59.grad_ref, f32[1,2048]{1,0:T(1,128)} %get-tuple-element.60.feed_ref, ...), custom_call_target="tpu_custom_call" | custom-call | tf_op jit(solution)/shard_map/leave/pallas_call | solution.py:452
  538.9 1.3 slice_bitcast_fusion.2
  540.1 1.8 slice_bitcast_fusion.1
  542.0 0.8 copy.38
  542.8 0.8 copy.48
  543.5 1.0 copy.49
  (39 shorter events, 3.7 us)
Async XLA Ops:
  71.2 2.8 copy-start.13
  71.2 3.4 copy-start.10
  71.2 3.4 copy-start.11
  71.2 3.3 copy-start.12
  71.2 4.5 copy-start.14
  72.6 26.2 %copy-start = (bf16[2,1024,256]{2,1,0:T(8,128)(2,1)}, bf16[2,1024,256]{2,1,0:T(8,128)(2,1)S(1)}, u32[]{:S(2)}) copy-start(bf16[2,1024,256]{2,1,0:T(8,128)(2,1)S(1)} %pad_maximum_fusion.1.here_ref) | copy-start | bytes 3145732
  72.6 26.2 %collective-permute-start = (bf16[2,1024,256]{2,1,0:T(8,128)(2,1)S(1)}, bf16[2,1024,256]{2,1,0:T(8,128)(2,1)S(1)}, u32[]{:S(2)}, u32[]{:S(2)}) collective-permute-start(bf16[2,1024,256]{2,1,0:T(8,128)(2,1)S(1)} %pad_maximum_fusion.1.here_ref), channel_id=1, source_target_pairs={{0,1},{1,0},{2,3},{3,2},{4,5},{5,4},{6,7},{7,6},{8,9},{9,8},{10,11... | collective-permute-start | bytes 3145736 | tf_op jit(solution)/shard_map/ppermute | solution.py:947
  98.8 1.0 copy-start.4
  403.7 5.1 copy-start.3
  412.5 19.0 %copy-start.6 = (f32[128,2304]{1,0:T(8,128)S(1)}, f32[128,2304]{1,0:T(8,128)}, u32[]{:S(2)}) copy-start(f32[128,2304]{1,0:T(8,128)} %get-tuple-element.64) | copy-start | bytes 3538948
  429.2 24.2 %collective-permute-start.1 = (bf16[2,1024,256]{2,1,0:T(8,128)(2,1)}, bf16[2,1024,256]{2,1,0:T(8,128)(2,1)S(1)}, u32[]{:S(2)}, u32[]{:S(2)}) collective-permute-start(bf16[2,1024,256]{2,1,0:T(8,128)(2,1)} %get-tuple-element.58), channel_id=1, source_target_pairs={{0,1},{1,0},{2,3},{3,2},{4,5},{5,4},{6,7},{7,6},{8,9},{9,8},{10,11... | collective-permute-start | bytes 3145736 | tf_op jit(solution)/shard_map/ppermute | solution.py:947
  458.9 1.2 copy-start.2
  460.1 1.3 copy-start.1
  461.7 1.0 copy-start.5
  461.7 1.2 copy-start.9
  482.4 60.4 %copy-start.8 = (bf16[128,2048]{1,0:T(8,128)(2,1)S(1)}, bf16[128,2048]{1,0:T(8,128)(2,1)}, u32[]{:S(2)}) copy-start(bf16[128,2048]{1,0:T(8,128)(2,1)} %get-tuple-element.114) | copy-start | bytes 1572868
  538.9 4.7 copy-start.7

commit v2 on v1

--- a/solution.py
+++ b/solution.py
@@ -59,6 +59,11 @@
         self.n_in += n
         return base
 
+    def take_out(self, n):
+        base = self.n_out
+        self.n_out += n
+        return base
+
     def copy(self, src, dst, device, slot=None):
         slot = self.slots(1) if slot is None else slot
         self.n_out += 1
@@ -102,14 +107,12 @@
     return lax.rem(spot.own + k, 4)
 
 
-def run(*jobs):
-    live = list(jobs)
-    while live:
-        for job in list(live):
-            try:
-                next(job)
-            except StopIteration:
-                live.remove(job)
+def play(order, **jobs):
+    for letter in order:
+        next(jobs[letter], None)
+    for job in jobs.values():
+        for _ in job:
+            pass
 
 
 def gather_rows(spot, post, own, rows):
@@ -294,29 +297,54 @@
     return arrive, leave
 
 
-def gather_weights(spot, post, shard, full, stage):
+def gather_first(spot, post, shard, row, stage):
+    keep = post.local(shard.at[1], stage.at[spot.y])
+    along_y = [post.copy(shard.at[1], stage.at[spot.y], spot.at(dy=k)) for k in (2, 1, 3)]
+    for copy in [keep] + along_y:
+        copy.start()
+    yield
+    arrive, leave = x_spread(spot, post, shard.at[0], lambda slot: row.at[slot])
+    yield
+    keep.wait()
+    for copy in along_y:
+        copy.wait_recv()
+    arrive()
+    leave()
+    for copy in along_y:
+        copy.wait_send()
+
+
+def gather_second(spot, post, row, stage, full):
     here = full.at[spot.y, :, 0]
-    a1_arrive, a1_leave = x_spread(spot, post, shard.at[0], lambda slot: full.at[spot.y, slot, 0])
-    keep = post.local(shard.at[1], stage.at[spot.y])
-    b1 = [post.copy(shard.at[1], stage.at[spot.y], spot.at(dy=k)) for k in (2, 1, 3)]
-    for copy in [keep] + b1:
+    keep = post.local(row, here)
+    along_y = [post.copy(row, here, spot.at(dy=k)) for k in (2, 1, 3)]
+    for copy in along_y + [keep]:
         copy.start()
-    yield
-    a1_arrive()
-    a2 = [post.copy(here, here, spot.at(dy=k)) for k in (2, 1, 3)]
-    for copy in a2:
+    arrive, leave = x_spread(spot, post, stage, lambda slot: full.at[:, slot, 1])
+    yield
+    keep.wait()
+    for copy in along_y:
+        copy.wait_recv()
+    arrive()
+    leave()
+    for copy in along_y:
+        copy.wait_send()
+
+
+def gather_x_y(spot, post, shard, row, full):
+    arrive, leave = x_spread(spot, post, shard, lambda slot: row.at[slot])
+    yield
+    arrive()
+    keep = post.local(row, full.at[spot.y])
+    along_y = [post.copy(row, full.at[spot.y], spot.at(dy=k)) for k in (2, 1, 3)]
+    for copy in along_y + [keep]:
         copy.start()
+    leave()
+    yield
+    for copy in along_y:
+        copy.wait_recv()
     keep.wait()
-    for copy in b1:
-        copy.wait_recv()
-    b2_arrive, b2_leave = x_spread(spot, post, stage, lambda slot: full.at[:, slot, 1])
-    yield
-    for copy in a2:
-        copy.wait_recv()
-    b2_arrive()
-    a1_leave()
-    b2_leave()
-    for copy in b1 + a2:
+    for copy in along_y:
         copy.wait_send()
 
 
@@ -335,67 +363,173 @@
     in_strips(rows, body)
 
 
-def scatter_weights(spot, post, full, out, from_x, from_y, sum_a, sum_b, last_y, last_x):
-    a1_arrive, a1_leave = x_collect(spot, post, lambda slot: full.at[:, slot, 0], from_x)
-    b1 = []
+class Gradients:
+    def __init__(self, spot, post, groups, full, from_x, from_y, sum_a, sum_b):
+        self.spot, self.groups, self.full, self.from_x, self.from_y = spot, groups, full, from_x, from_y
+        self.sum_a, self.sum_b = sum_a, sum_b
+        self.out_sems, self.in_sems = post.out_sems, post.in_sems
+        self.out_x, self.out_y = post.take_out(16), post.take_out(4)
+        self.in_x, self.in_y = post.slots(16), post.slots(4)
+
+    def y_of(self, j):
+        return lax.rem(self.spot.y + j + 1, 4)
+
+    def along_x(self, j, k):
+        spot, y, slot = self.spot, self.y_of(j), after(self.spot, k)
+        return pltpu.make_async_remote_copy(
+            src_ref=self.full.at[y, slot, 0],
+            dst_ref=self.from_x.at[y, spot.x],
+            send_sem=self.out_sems.at[self.out_x + 4 * j + k],
+            recv_sem=self.in_sems.at[self.in_x + 4 * j + spot.x],
+            device_id=spot.seat(slot),
+            device_id_type=MESH,
+        )
+
+    def stay(self, j):
+        spot, y = self.spot, self.y_of(j)
+        return pltpu.make_async_copy(
+            self.full.at[y, spot.own, 0], self.from_x.at[y, spot.x], self.out_sems.at[self.out_x + 4 * j]
+        )
+
+    def from_chip(self, j, k):
+        spot, y = self.spot, self.y_of(j)
+        x = lax.rem(spot.x + k, 4)
+        return pltpu.make_async_remote_copy(
+            src_ref=self.full.at[y, spot.own, 0],
+            dst_ref=self.from_x.at[y, x],
+            send_sem=self.out_sems.at[self.out_x],
+            recv_sem=self.in_sems.at[self.in_x + 4 * j + x],
+            device_id=spot.at(dx=1),
+            device_id_type=MESH,
+        )
+
+    def along_y(self, j):
+        spot, y = self.spot, self.y_of(j)
+        return pltpu.make_async_remote_copy(
+            src_ref=self.full.at[y, :, 1],
+            dst_ref=self.from_y.at[j],
+            send_sem=self.out_sems.at[self.out_y + j],
+            recv_sem=self.in_sems.at[self.in_y + j],
+            device_id=spot.at(dy=j + 1),
+            device_id_type=MESH,
+        )
+
+    def make(self, j):
+        spot, y = self.spot, self.y_of(j)
+
+        def part(s, carry):
+            columns = pl.ds(pl.multiple_of(y * 512 + s * 256, 256), 256)
+            at = 0
+            for rows, values in self.groups:
+                left = rows[:, columns]
+                for value in values:
+                    width = value.shape[1]
+                    block = dot(left, value[...], 0, 0).astype(BF16)
+                    for i in range(4):
+                        self.full[y, 2 * s + i // 2, i % 2, :, at : at + width] = block[i * 64 : (i + 1) * 64]
+                    at += width
+            return carry
+
+        lax.fori_loop(0, 2, part, 0)
+        for k in (2, 1, 3):
+            self.along_x(j, k).start()
+
+        @pl.when(spot.home)
+        def _():
+            self.stay(j).start()
+
+        @pl.when(jnp.logical_not(spot.home))
+        def _():
+            self.along_x(j, 0).start()
+
+        if j < 3:
+            self.along_y(j).start()
+
+    def sum_x(self, j):
+        spot, y = self.spot, self.y_of(j)
+        for k in (1, 2, 3):
+            self.from_chip(j, k).wait_recv()
+            self.along_x(j, k).wait_send()
+
+        @pl.when(spot.home)
+        def _():
+            self.stay(j).wait()
+
+        @pl.when(jnp.logical_not(spot.home))
+        def _():
+            self.from_chip(j, 0).wait_recv()
+            self.along_x(j, 0).wait_send()
+
+        def write(strip, total):
+            self.sum_a[y, strip, :] = total.astype(BF16)
+
+        sum_four([self.from_x.at[y, x] for x in range(4)], write)
+
+    def sum_y(self):
+        for j in range(3):
+            self.along_y(j).wait_recv()
+            self.along_y(j).wait_send()
+
+        def slot_sum(slot, carry):
+            def write(strip, total):
+                self.sum_b[slot, strip, :] = total.astype(BF16)
+
+            sum_four([self.from_y.at[j, slot] for j in range(3)] + [self.full.at[self.spot.y, slot, 1]], write)
+            return carry
+
+        lax.fori_loop(0, 4, slot_sum, 0)
+
+    def steps(self):
+        for j in range(4):
+            self.make(j)
+            yield
+        for j in range(4):
+            self.sum_x(j)
+            yield
+        self.sum_y()
+
+
+def load(post, pairs):
+    copies = [post.local(src, dst) for src, dst in pairs]
+    for copy in copies:
+        copy.start()
+    return copies
+
+
+def gradient_scratch(n):
+    return [pltpu.VMEM((4, 4, 2, 64, n), BF16), pltpu.VMEM((4, 4, 64, n), BF16), pltpu.VMEM((3, 4, 64, n), BF16)]
+
+
+def scatter_second(spot, post, sum_a, sum_b, out, last_y, last_x):
+    along_y = []
     for i, k in enumerate((2, 1, 3)):
-        y = lax.rem(spot.y + k, 4)
-        b1.append(post.copy(full.at[y, :, 1], from_y.at[i], spot.at(dy=k)))
-    keep = post.local(full.at[spot.y, :, 1], from_y.at[3])
-    for copy in b1 + [keep]:
+        along_y.append(post.copy(sum_a.at[lax.rem(spot.y + k, 4)], last_y.at[i], spot.at(dy=k)))
+    keep = post.local(sum_a.at[spot.y], last_y.at[3])
+    for copy in along_y + [keep]:
         copy.start()
-    yield
-    a1_arrive()
-    a2 = []
-    for i, k in enumerate((2, 1, 3, 0)):
-        y = lax.rem(spot.y + k, 4)
-
-        def write_a(strip, total, y=y):
-            sum_a[y, strip, :] = total.astype(BF16)
-
-        sum_four([from_x.at[j, y] for j in range(4)], write_a)
-        if k:
-            a2.append(post.copy(sum_a.at[y], last_y.at[i], spot.at(dy=k)))
-            a2[-1].start()
-    for copy in b1:
+    arrive, leave = x_collect(spot, post, lambda slot: sum_b.at[slot], last_x)
+    yield
+    for copy in along_y:
         copy.wait_recv()
     keep.wait()
-    for slot in range(4):
-
-        def write_b(strip, total, slot=slot):
-            sum_b[slot, strip, :] = total.astype(BF16)
-
-        sum_four([from_y.at[j, slot] for j in range(4)], write_b)
-    b2_arrive, b2_leave = x_collect(spot, post, lambda slot: sum_b.at[slot], last_x)
-    yield
-    for copy in a2:
-        copy.wait_recv()
 
     def write_low(strip, total):
         out[strip, :] = total
 
-    sum_four([last_y.at[0], last_y.at[1], last_y.at[2], sum_a.at[spot.y]], write_low)
-    b2_arrive()
+    sum_four([last_y.at[j] for j in range(4)], write_low)
+    arrive()
 
     def write_high(strip, total):
         out[pl.ds(pl.multiple_of(strip.start + 64, 16), 16), :] = total
 
     sum_four([last_x.at[j] for j in range(4)], write_high)
-    a1_leave()
-    b2_leave()
-    for copy in b1 + a2:
+    leave()
+    for copy in along_y:
         copy.wait_send()
 
 
-def weight_scratch(n):
-    return [
-        pltpu.VMEM((4, 4, 64, n), BF16),
-        pltpu.VMEM((4, 4, 64, n), BF16),
-        pltpu.VMEM((4, 64, n), BF16),
-        pltpu.VMEM((4, 64, n), BF16),
-        pltpu.VMEM((3, 64, n), BF16),
-        pltpu.VMEM((4, 64, n), BF16),
-    ]
+def second_scratch(n):
+    return [pltpu.VMEM((4, 64, n), BF16), pltpu.VMEM((4, 64, n), BF16)]
 
 
 def sum_gains(spot, post, parts, out, from_y, over_y, from_chip, over_fsdp, from_tp):
@@ -473,37 +607,42 @@
 def enter(tokens, gain, shard):
     n = shard.shape[1]
 
-    def kernel(tokens_ref, gain_ref, shard_ref, rows_ref, full_ref, stage_ref, own, out_sems, in_sems):
+    def kernel(tokens_ref, gain_ref, shard_ref, rows_ref, full_ref, row_ref, stage_ref, own, out_sems, in_sems):
         spot, post = Spot(), Post(out_sems, in_sems)
         seats, away = gather_sources(spot)
         greet(spot, row_peers(spot) + y_peers(spot) + seats, away, 9)
-        weights = gather_weights(spot, post, shard_ref, full_ref, stage_ref)
-        next(weights)
+
+        def weights():
+            yield from gather_first(spot, post, shard_ref, row_ref, stage_ref)
+            yield from gather_second(spot, post, row_ref, stage_ref, full_ref)
+
+        w = weights()
+        next(w)
+        next(w)
 
         def body(strip):
             own[strip, :] = normed(tokens_ref[strip, :].astype(F32), gain_ref[...])[2]
 
         in_strips(ROWS, body)
-        run(weights, gather_rows(spot, post, own, rows_ref))
-
+        play("rwrrrw", r=gather_rows(spot, post, own, rows_ref), w=w)
+
+    half = pltpu.VMEM((4, 64, n), BF16)
     return moving(
         kernel,
         "enter",
-        (shape((8, ROWS, WIDE), BF16), shape((4, 4, 2, 64, n), BF16), shape((4, 64, n), BF16)),
+        (shape((8, ROWS, WIDE), BF16), shape((4, 4, 2, 64, n), BF16)),
         (tokens, gain, shard.reshape(2, 64, n)),
-        [INSIDE, INSIDE, ANY],
-        (ANY, ANY, ANY),
-        [pltpu.VMEM((ROWS, WIDE), BF16)] + sems(40),
+        [INSIDE] * 3,
+        (ANY,) * 2,
+        [half, half, pltpu.VMEM((ROWS, WIDE), BF16)] + sems(40),
         1,
-    )[:2]
-
-
-def middle(part, tokens, gain, cotangent, shard):
-    n = shard.shape[1]
-
-    def kernel(
-        part_ref, tokens_ref, gain_ref, cot_ref, shard_ref, mid_ref, rows_ref, grads_ref, full_ref, stage_ref, own, *rest
-    ):
+    )
+
+
+def middle(part, tokens, gain, row, stage):
+    n = row.shape[-1]
+
+    def kernel(part_ref, tokens_ref, gain_ref, row_ref, stage_ref, mid_ref, rows_ref, full_ref, own, *rest):
         scatter, (out_sems, in_sems) = rest[:4], rest[4:]
         mine, land, far, gone = scatter
         spot, post = Spot(), Post(out_sems, in_sems)
@@ -521,24 +660,18 @@
             in_strips(ROWS, body)
             yield from gather_rows(spot, post, own, rows_ref)
 
-        def second():
-            for _ in range(4):
-                yield
-            yield from gather_rows(spot, post, cot_ref, grads_ref)
-
-        run(main(), gather_weights(spot, post, shard_ref, full_ref, stage_ref), second())
-
-    rows = shape((8, ROWS, WIDE), BF16)
+        play("mwmmmmmm", m=main(), w=gather_second(spot, post, row_ref, stage_ref, full_ref))
+
     return moving(
         kernel,
         "middle",
-        (shape((ROWS, WIDE), F32), rows, rows, shape((4, 4, 2, 64, n), BF16), shape((4, 64, n), BF16)),
-        (part, tokens, gain, cotangent, shard.reshape(2, 64, n)),
-        [ANY, INSIDE, INSIDE, ANY, ANY],
-        (INSIDE, ANY, ANY, ANY, ANY),
+        (shape((ROWS, WIDE), F32), shape((8, ROWS, WIDE), BF16), shape((4, 4, 2, 64, n), BF16)),
+        (part, tokens, gain, row, stage),
+        [ANY, INSIDE, INSIDE, INSIDE, INSIDE],
+        (INSIDE, ANY, ANY),
         [pltpu.VMEM((ROWS, WIDE), BF16)] + scatter_scratch() + sems(64),
         2,
-    )[:4]
+    )
 
 
 def norm_back(upstream, rows, gain):
@@ -548,16 +681,23 @@
     return through, jnp.sum(upstream * scaled, 0, keepdims=True)
 
 
-def turn(part, part_out, mid, gain, cotangent, full):
-    n = full.shape[1]
+def turn(part, mid, gain, cotangent, rows, grads, d_gate, d_up, hidden, weights):
+    n = 3 * PACK
+    count = 8 * ROWS
 
     def kernel(
-        part_ref, out_part_ref, mid_ref, gain_ref, cot_ref, full_ref, layer_ref, grad_ref, rows_ref, feed_ref, weight_ref,
-        own, *rest,
+        part_ref, mid_ref, gain_ref, cot_ref, rows_hbm, grads_hbm, gate_hbm, up_hbm, hid_hbm, weights_hbm,
+        grad_ref, mid_rows_ref, feed_ref, sum_a, sum_b, out_hbm,
+        own, rows_ref, grads_ref, gate_ref, up_ref, hid_ref, down_ref, out_ref, *rest,
     ):
-        first, second, weights, (out_sems, in_sems) = rest[:4], rest[4:8], rest[8:14], rest[14:]
+        first, room, (out_sems, in_sems) = rest[:4], rest[4:7], rest[7:]
         spot, post = Spot(), Post(out_sems, in_sems)
         sources, away = scatter_sources(spot)
+        loads = load(
+            post,
+            [(gate_hbm, gate_ref), (up_hbm, up_ref), (rows_hbm, rows_ref), (hid_hbm, hid_ref), (grads_hbm, grads_ref)]
+            + [(weights_hbm.at[:, pl.ds(2 * PACK, PACK)], down_ref)],
+        )
         greet(spot, row_peers(spot) + y_peers(spot) + sources, away, 9)
 
         def main():
@@ -573,48 +713,66 @@
                 feed_ref[...] += feed
 
             in_strips(ROWS, body)
-            yield from gather_rows(spot, post, own, rows_ref)
+            yield from gather_rows(spot, post, own, mid_rows_ref)
+
+        def gradients():
+            for copy in loads:
+                copy.wait()
+            groups = [(rows_ref, (gate_ref, up_ref)), (grads_ref, (hid_ref,))]
+            yield from Gradients(spot, post, groups, *room, sum_a, sum_b).steps()
 
         def output():
-            for _ in range(4):
-                yield
-            yield from scatter_rows(spot, post, out_part_ref, *second)
-
-            def body(strip):
-                layer_ref[strip, :] = (mid_ref[strip, :] + row_sum(spot, second[0], second[1], second[3], strip)).astype(BF16)
-
-            in_strips(ROWS, body)
-
-        run(main(), scatter_weights(spot, post, full_ref, weight_ref, *weights), output())
-
+            def step(i, carry):
+                rows = pl.ds(pl.multiple_of(i * 256, 256), 256)
+                out_ref[rows, :] = dot(hid_ref[rows, :], down_ref[...], 1, 1).astype(BF16)
+                return carry
+
+            lax.fori_loop(0, count // 256, step, 0)
+            store = post.local(out_ref, out_hbm)
+            store.start()
+            yield
+            store.wait()
+
+        play("mgmgmgmgomgmmgggo", m=main(), g=gradients(), o=output())
+
+    half = shape((4, 64, n), BF16)
+    wide = pltpu.VMEM((count, WIDE), BF16)
+    narrow = pltpu.VMEM((count, PACK), BF16)
     return moving(
         kernel,
         "turn",
         (
-            shape((ROWS, WIDE), BF16),
             shape((ROWS, WIDE), F32),
             shape((8, ROWS, WIDE), BF16),
             shape((1, WIDE), F32),
-            shape((ROWS, n), F32),
+            half,
+            half,
+            shape((count, WIDE), BF16),
         ),
-        (part, part_out, mid, gain, cotangent, full.reshape(4, 4, 2, 64, n)),
-        [ANY, ANY, INSIDE, INSIDE, INSIDE, ANY],
-        (INSIDE, INSIDE, ANY, INSIDE, INSIDE),
-        [pltpu.VMEM((ROWS, WIDE), BF16)] + scatter_scratch() * 2 + weight_scratch(n) + sems(80),
+        (part, mid, gain, cotangent, rows, grads, d_gate, d_up, hidden, weights),
+        [ANY, INSIDE, INSIDE, INSIDE] + [ANY] * 6,
+        (INSIDE, ANY, INSIDE, INSIDE, INSIDE, ANY),
+        [pltpu.VMEM((ROWS, WIDE), BF16), wide, wide, narrow, narrow, narrow, pltpu.VMEM((WIDE, PACK), BF16), wide]
+        + scatter_scratch()
+        + gradient_scratch(n)
+        + sems(80),
         3,
     )
 
 
-def leave(part, tokens, gain, grad_mid, feed_part, full):
-    n = full.shape[1]
+def leave(part, tokens, gain, grad_mid, feed_part, rows, d_qkv, mid_rows, mixed):
+    n_qkv, n_out = d_qkv.shape[1], mixed.shape[1]
+    n = n_qkv + n_out
+    count = 8 * ROWS
 
     def kernel(
-        part_ref, tokens_ref, gain_ref, grad_ref, feed_ref, full_ref, token_ref, gains_ref, weight_ref, norm_part, parts,
-        from_y, over_y, from_chip, over_fsdp, from_tp, *rest,
+        part_ref, tokens_ref, gain_ref, grad_ref, feed_ref, rows_hbm, d_hbm, mid_hbm, mixed_hbm, token_ref, gains_ref,
+        weight_ref, norm_part, parts, from_y, over_y, from_chip, over_fsdp, from_tp, rows_ref, d_ref, mid_ref, mixed_ref, *rest,
     ):
-        first, weights, (out_sems, in_sems) = rest[:4], rest[4:10], rest[10:]
+        first, room, (sum_a, sum_b), last, (out_sems, in_sems) = rest[:4], rest[4:7], rest[7:9], rest[9:11], rest[11:]
         spot, post = Spot(), Post(out_sems, in_sems)
         sources, away = scatter_sources(spot)
+        loads = load(post, [(d_hbm, d_ref), (rows_hbm, rows_ref), (mixed_hbm, mixed_ref), (mid_hbm, mid_ref)])
         greet(spot, row_peers(spot) + y_peers(spot) + sources + gain_sources(spot), away, 9 + 13)
 
         def main():
@@ -634,21 +792,31 @@
                 parts[f, 1:2, :] = feed_ref[:, f * 128 : (f + 1) * 128]
             yield from sum_gains(spot, post, parts, gains_ref, from_y, over_y, from_chip, over_fsdp, from_tp)
 
-        run(main(), scatter_weights(spot, post, full_ref, weight_ref, *weights))
+        def gradients():
+            for copy in loads:
+                copy.wait()
+            groups = [(rows_ref, (d_ref,)), (mid_ref, (mixed_ref,))]
+            yield from Gradients(spot, post, groups, *room, sum_a, sum_b).steps()
+            yield from scatter_second(spot, post, sum_a, sum_b, weight_ref, *last)
+
+        play("mgmgmgggggmgmmgmgm", m=main(), g=gradients())
 
     small = (8, 128)
+    wide = pltpu.VMEM((count, WIDE), BF16)
     return moving(
         kernel,
         "leave",
         (shape((ROWS, WIDE), F32), shape(small, F32), shape((ROWS, n), F32)),
-        (part, tokens, gain, grad_mid, feed_part, full.reshape(4, 4, 2, 64, n)),
-        [ANY, INSIDE, INSIDE, INSIDE, INSIDE, ANY],
+        (part, tokens, gain, grad_mid, feed_part, rows, d_qkv, mid_rows, mixed),
+        [ANY, INSIDE, INSIDE, INSIDE, INSIDE] + [ANY] * 4,
         (INSIDE, INSIDE, INSIDE),
         [pltpu.VMEM((1, WIDE), F32), pltpu.VMEM((16,) + small, F32)]
         + [pltpu.VMEM(dims + small, F32) for dims in ((3, 4), (4,), (3,), (), (7,))]
+        + [wide, pltpu.VMEM((count, n_qkv), BF16), wide, pltpu.VMEM((count, n_out), BF16)]
         + scatter_scratch()
-        + weight_scratch(n)
-        + sems(80),
+        + gradient_scratch(n)
+        + second_scratch(n) * 2
+        + sems(100),
         4,
     )
 
@@ -682,15 +850,15 @@
 def project(rows, weights, cosine, sine):
     step = 256
 
-    def kernel(rows_ref, w_ref, cos_ref, sin_ref, q_ref, k_ref, v_ref):
+    def kernel(rows_ref, w_ref, cos_ref, sin_ref, q_ref, kv_ref):
         out = dot(rows_ref[...], w_ref[...])
         cos, sin = cos_ref[...], sin_ref[...]
         for head in range(4):
             u = out[:, head * HD : (head + 1) * HD]
             turned = (u * cos + pltpu.roll(u, HD // 2, 1) * sin).astype(BF16)
-            target = q_ref if head < 2 else k_ref
+            target = q_ref if head < 2 else kv_ref.at[0]
             target[:, head % 2 * HD : (head % 2 + 1) * HD] = turned
-        v_ref[...] = out[:, 4 * HD :].astype(BF16)
+        kv_ref[1] = out[:, 4 * HD :].astype(BF16)
 
     out = shape((8 * ROWS, 2 * HD), BF16)
     return plain(
@@ -699,8 +867,8 @@
         (8 * ROWS // step,),
         (rows, weights, cosine, sine),
         [by_rows(step, WIDE), whole((WIDE, PACK)), by_rows(step, HD), by_rows(step, HD)],
-        (out, out, out),
-        (by_rows(step, 2 * HD),) * 3,
+        (out, shape((2,) + out.shape, BF16)),
+        (by_rows(step, 2 * HD), pl.BlockSpec((2, step, 2 * HD), lambda i: (0, i, 0))),
     )
 
 
@@ -753,29 +921,6 @@
     )
 
 
-def outer(groups, name):
-    step = 256
-    count = 8 * ROWS
-
-    def kernel(*refs):
-        out = refs[-1]
-        at, column = 0, 0
-        for rows, values in groups:
-            left = refs[at][...]
-            for i, value in enumerate(values):
-                width = value.shape[1]
-                out[:, column : column + width] = dot(left, refs[at + 1 + i][...], 0, 0).astype(BF16)
-                column += width
-            at += 1 + len(values)
-
-    inputs, specs, total = [], [], 0
-    for rows, values in groups:
-        inputs += [rows] + list(values)
-        specs += [pl.BlockSpec((count, step), lambda i: (0, i))] + [whole(value.shape) for value in values]
-        total += sum(value.shape[1] for value in values)
-    return plain(kernel, name, (WIDE // step,), inputs, specs, shape((WIDE, total), BF16), by_rows(step, total))
-
-
 def back_to_heads(rows, weights):
     step = 256
 
@@ -787,7 +932,7 @@
         "back_to_heads",
         (8 * ROWS // step,),
         (rows, weights),
-        [by_rows(step, WIDE), whole((WIDE, 2 * HD), 0, 3)],
+        [by_rows(step, WIDE), whole((WIDE, 2 * HD))],
         shape((8 * ROWS, 2 * HD), BF16),
         by_rows(step, 2 * HD),
     )
@@ -803,148 +948,240 @@
     return 2 * (j + start) - lax.rem(j, ROWS) + xh * ROWS
 
 
-def key_chunks():
-    return [(((0, 0, 512),), None), (((1, 0, 512),), None), (((0, 512, 256), (1, 512, 256)), "near")], (
-        ((0, 768, 256), (1, 768, 256)),
-        "far",
-    )
-
-
-def allowed_in(pieces, q_pos, prefix, xh):
-    k_pos = jnp.concatenate([place_of(start, count, lax.rem(xh + side, 2), 0) for side, start, count in pieces], 0)
-    return jnp.logical_or(k_pos <= q_pos, k_pos < prefix)
-
-
-def take(pieces, sides, which, cols):
-    parts = [sides[side][which, pl.ds(start, count), cols] for side, start, count in pieces]
-    return parts[0] if len(parts) == 1 else jnp.concatenate(parts, 0)
-
-
-def attend(meta, queries, here, there):
-    def kernel(meta_ref, q_ref, here_ref, there_ref, o_ref, lse_ref, top_ref, sum_ref, acc_ref):
-        prefix, xh = meta_ref[0], meta_ref[1]
-        sides = (here_ref, there_ref)
-        always, last = key_chunks()
-
-        def step(i, carry):
-            head, tile = lax.div(i, 4), lax.rem(i, 4)
-            cols = pl.ds(pl.multiple_of(head * HD, HD), HD)
-            rows = pl.ds(pl.multiple_of(tile * TILE, TILE), TILE)
-            q = q_ref[rows, cols]
-            q_pos = place_of(tile * TILE, TILE, xh, 1)
-
-            def chunk(pieces, masked, first):
-                keys = take(pieces, sides, 0, cols)
-                scores = dot(keys, q, 1, 1) * (SCALE * LOG2E)
-                if masked:
-                    scores = jnp.where(allowed_in(pieces, q_pos, prefix, xh), scores, -1e30)
-                top = jnp.max(scores, 0, keepdims=True)
-                if not first:
-                    before = top_ref[...]
-                    top = jnp.maximum(top, before)
-                raised = jnp.exp2(scores - top)
-                total = jnp.sum(raised, 0, keepdims=True)
-                mixed = dot(take(pieces, sides, 1, cols), raised.astype(BF16), 0, 0)
-                if not first:
-                    fade = jnp.exp2(before - top)
-                    total = total + sum_ref[...] * fade
-                    mixed = mixed + acc_ref[...] * fade
-                top_ref[...] = top
-                sum_ref[...] = total
-                acc_ref[...] = mixed
-
-            for number, (pieces, masked) in enumerate(always):
-                chunk(pieces, masked, number == 0)
-
-            @pl.when(tile == 3)
-            def _():
-                chunk(*last, False)
-
-            total = sum_ref[...]
-            o_ref[rows, cols] = (acc_ref[...] / total).T.astype(BF16)
-            lse_ref[pl.ds(i, 1), :] = top_ref[...] + jnp.log2(total)
-            return carry
-
-        lax.fori_loop(0, 8, step, 0)
-
-    return pl.pallas_call(
+SPANS = ((0, 512, False), (512, 256, True))
+LAST = (768, 256, True)
+
+
+def scores_of(keys, q, span, q_pos, prefix, xh):
+    start, count, masked = span
+    scores = dot(keys, q, 1, 1) * (SCALE * LOG2E)
+    if masked:
+        k_pos = place_of(start, count, xh, 0)
+        scores = jnp.where(jnp.logical_or(k_pos <= q_pos, k_pos < prefix), scores, -1e30)
+    return scores
+
+
+def tile_at(i):
+    head, tile = lax.div(i, 4), lax.rem(i, 4)
+    return head, tile, pl.ds(pl.multiple_of(head * HD, HD), HD), pl.ds(pl.multiple_of(tile * TILE, TILE), TILE)
+
+
+def exchange(post, src, dst, device):
+    copy = post.copy(src, dst, device)
+    copy.start()
+    yield
+    copy.wait_recv()
+    yield
+    copy.wait_send()
+
+
+def attend(meta, queries, here, cotangent, shard, shard_out):
+    n, n_out = shard.shape[1], shard_out.shape[1]
+
+    def kernel(
+        meta_ref, q_ref, here_ref, cot_ref, shard_ref, shard_out_ref, o_ref, lse_ref, there_ref, grads_ref, row_ref, stage_ref,
+        out_ref, top_ref, sum_ref, acc_ref, row_out_ref, out_sems, in_sems,
+    ):
+        prefix = meta_ref[0]
+        spot, post = Spot(), Post(out_sems, in_sems)
+        seats, away = gather_sources(spot)
+        partner = spot.at(dx=2)
+        greet(spot, row_peers(spot) + y_peers(spot) + seats + [partner], away, 10)
+
+        def compute():
+            for side, keys_ref in enumerate((here_ref, there_ref)):
+                xh = spot.xh if side == 0 else 1 - spot.xh
+
+                def step(i, carry, side=side, keys_ref=keys_ref, xh=xh):
+                    head, tile, cols, rows = tile_at(i)
+                    q = q_ref[rows, cols]
+                    q_pos = place_of(tile * TILE, TILE, spot.xh, 1)
+                    one = pl.ds(i, 1)
+
+                    def chunk(span, first):
+                        keys = pl.ds(span[0], span[1])
+                        scores = scores_of(keys_ref[0, keys, cols], q, span, q_pos, prefix, xh)
+                        top = jnp.max(scores, 0, keepdims=True)
+                        if not first:
+                            before = top_ref[one, :]
+                            top = jnp.maximum(top, before)
+                        raised = jnp.exp2(scores - top)
+                        total = jnp.sum(raised, 0, keepdims=True)
+                        mixed = dot(keys_ref[1, keys, cols], raised.astype(BF16), 0, 0)
+                        if not first:
+                            fade = jnp.exp2(before - top)
+                            total = total + sum_ref[one, :] * fade
+                            mixed = mixed + acc_ref[i] * fade
+                        top_ref[one, :] = top
+                        sum_ref[one, :] = total
+                        acc_ref[i] = mixed
+
+                    for number, span in enumerate(SPANS):
+                        chunk(span, side == 0 and number == 0)
+
+                    @pl.when(tile == 3)
+                    def _():
+                        chunk(LAST, False)
+
+                    if side == 1:
+                        total = sum_ref[one, :]
+                        o_ref[rows, cols] = (acc_ref[i] / total).T.astype(BF16)
+                        lse_ref[one, :] = top_ref[one, :] + jnp.log2(total)
+                    return carry
+
+                lax.fori_loop(0, 8, step, 0)
+                yield
+
+        play(
+            "vewscsvsewcesw",
+            v=gather_x_y(spot, post, shard_out_ref, row_out_ref, out_ref),
+            e=exchange(post, here_ref, there_ref, partner),
+            w=gather_first(spot, post, shard_ref, row_ref, stage_ref),
+            s=gather_rows(spot, post, cot_ref, grads_ref),
+            c=compute(),
+        )
+
+    half = shape((4, 64, n), BF16)
+    return moving(
         kernel,
-        name="attend",
-        out_shape=(shape((8 * ROWS, 2 * HD), BF16), shape((8, TILE), F32)),
-        in_specs=[pl.BlockSpec(memory_space=pltpu.SMEM), INSIDE, INSIDE, INSIDE],
-        out_specs=(INSIDE, INSIDE),
-        scratch_shapes=[pltpu.VMEM((1, TILE), F32), pltpu.VMEM((1, TILE), F32), pltpu.VMEM((HD, TILE), F32)],
-        compiler_params=pltpu.CompilerParams(vmem_limit_bytes=VMEM),
-    )(meta, queries, here, there)
-
-
-def attend_back(meta, queries, here, there, grads, lse, delta, cosine, sine):
+        "attend",
+        (
+            shape((8 * ROWS, 2 * HD), BF16),
+            shape((8, TILE), F32),
+            shape(here.shape, BF16),
+            shape((8, ROWS, WIDE), BF16),
+            half,
+            half,
+            shape((4, 4, ROWS, n_out), BF16),
+        ),
+        (meta, queries, here, cotangent, shard.reshape(2, 64, n), shard_out),
+        [pl.BlockSpec(memory_space=pltpu.SMEM)] + [INSIDE] * 5,
+        (INSIDE, INSIDE, INSIDE, ANY, INSIDE, INSIDE, ANY),
+        [pltpu.VMEM((8, TILE), F32), pltpu.VMEM((8, TILE), F32), pltpu.VMEM((8, HD, TILE), F32)]
+        + [pltpu.VMEM((4, ROWS, n_out), BF16)]
+        + sems(60),
+        5,
+    )
+
+
+def attend_back(meta, queries, here, there, grads, mixed, lse, cosine, sine, out_part, mid, sum_a, sum_b):
+    n = sum_a.shape[-1]
+
     def kernel(
-        meta_ref, q_ref, here_ref, there_ref, g_ref, lse_ref, delta_ref, cos_ref, sin_ref, dq_ref, near_ref, far_ref,
-        dq_acc, acc_here, acc_there,
+        meta_ref, q_ref, here_ref, there_ref, g_ref, o_ref, lse_ref, cos_ref, sin_ref, part_ref, mid_ref, sum_a_ref, sum_b_ref,
+        d_ref, layer_ref, weight_ref, delta_ref, dq_ref, acc_ref, near_ref, away_ref, land_ref, *rest,
     ):
-        prefix, xh = meta_ref[0], meta_ref[1]
-        sides, accs = (here_ref, there_ref), (acc_here, acc_there)
-        always, last = key_chunks()
-        acc_here[...] = jnp.zeros_like(acc_here)
-        acc_there[...] = jnp.zeros_like(acc_there)
-
-        def step(i, carry):
-            head, tile = lax.div(i, 4), lax.rem(i, 4)
-            cols = pl.ds(pl.multiple_of(head * HD, HD), HD)
-            rows = pl.ds(pl.multiple_of(tile * TILE, TILE), TILE)
-            q, g = q_ref[rows, cols], g_ref[rows, cols]
-            q_pos = place_of(tile * TILE, TILE, xh, 1)
-            level, offset = lse_ref[pl.ds(i, 1), :], delta_ref[pl.ds(i, 1), :]
-
-            def chunk(pieces, masked, first):
-                keys = take(pieces, sides, 0, cols)
-                scores = dot(keys, q, 1, 1) * (SCALE * LOG2E)
-                if masked:
-                    scores = jnp.where(allowed_in(pieces, q_pos, prefix, xh), scores, -1e30)
-                probs = jnp.exp2(scores - level)
-                d_probs = dot(take(pieces, sides, 1, cols), g, 1, 1)
-                d_scores = (probs * (d_probs - offset)).astype(BF16)
-                d_values = dot(probs.astype(BF16), g)
-                d_keys = dot(d_scores, q)
-                at = 0
-                for side, start, count in pieces:
-                    span = pl.ds(start, count)
-                    accs[side][0, span, cols] += d_keys[at : at + count]
-                    accs[side][1, span, cols] += d_values[at : at + count]
-                    at += count
-                d_query = dot(d_scores, keys, 0, 0)
-                dq_acc[...] = d_query if first else dq_acc[...] + d_query
-
-            for number, (pieces, masked) in enumerate(always):
-                chunk(pieces, masked, number == 0)
-
-            @pl.when(tile == 3)
-            def _():
-                chunk(*last, False)
-
-            u = dq_acc[...] * SCALE
-            dq_ref[rows, cols] = (u * cos_ref[rows, :] - pltpu.roll(u, HD // 2, 1) * sin_ref[rows, :]).astype(BF16)
-            return carry
-
-        lax.fori_loop(0, 8, step, 0)
-        near_ref[...] = acc_here[...]
-        far_ref[...] = acc_there[...].astype(BF16)
-
-    pair = (2, 8 * ROWS, 2 * HD)
-    return pl.pallas_call(
+        second, last, (out_sems, in_sems) = rest[:4], rest[4:6], rest[6:]
+        prefix = meta_ref[0]
+        spot, post = Spot(), Post(out_sems, in_sems)
+        sources, away = scatter_sources(spot)
+        partner = spot.at(dx=2)
+        greet(spot, row_peers(spot) + y_peers(spot) + sources + [partner], away, 10)
+
+        def sweep(head, side, keys_ref, into):
+            xh = spot.xh if side == 0 else 1 - spot.xh
+            cols = pl.ds(head * HD, HD)
+            into[...] = jnp.zeros_like(into)
+
+            def step(tile, carry):
+                i = head * 4 + tile
+                rows = pl.ds(pl.multiple_of(tile * TILE, TILE), TILE)
+                q, g = q_ref[rows, cols], g_ref[rows, cols]
+                q_pos = place_of(tile * TILE, TILE, spot.xh, 1)
+                if side == 1:
+                    product = g.astype(F32) * o_ref[rows, cols].astype(F32)
+                    delta_ref[pl.ds(i, 1), :] = jnp.sum(product.T, 0, keepdims=True)
+                level, offset = lse_ref[pl.ds(i, 1), :], delta_ref[pl.ds(i, 1), :]
+
+                def chunk(span, first):
+                    span_rows = pl.ds(span[0], span[1])
+                    keys = keys_ref[0, span_rows, cols]
+                    probs = jnp.exp2(scores_of(keys, q, span, q_pos, prefix, xh) - level)
+                    d_probs = dot(keys_ref[1, span_rows, cols], g, 1, 1)
+                    d_scores = (probs * (d_probs - offset)).astype(BF16)
+                    into[0, span_rows, :] += dot(d_scores, q)
+                    into[1, span_rows, :] += dot(probs.astype(BF16), g)
+                    d_query = dot(d_scores, keys, 0, 0)
+                    dq_ref[i] = d_query if first else dq_ref[i] + d_query
+
+                for number, span in enumerate(SPANS):
+                    chunk(span, side == 1 and number == 0)
+
+                @pl.when(tile == 3)
+                def _():
+                    chunk(LAST, False)
+
+                if side == 0:
+                    u = dq_ref[i] * SCALE
+                    d_ref[rows, cols] = (u * cos_ref[rows, :] - pltpu.roll(u, HD // 2, 1) * sin_ref[rows, :]).astype(BF16)
+                return carry
+
+            lax.fori_loop(0, 4, step, 0)
+
+        def compute():
+            copies = []
+            for head in range(2):
+                sweep(head, 1, there_ref, acc_ref)
+                away_ref[head] = acc_ref[...].astype(BF16)
+                copies.append(post.copy(away_ref.at[head], land_ref.at[head], partner))
+                copies[-1].start()
+                yield
+            for head in range(2):
+                sweep(head, 0, here_ref, near_ref.at[head])
+                yield
+            for head in range(2):
+                copies[head].wait_recv()
+                cols = pl.ds(2 * HD + head * HD, HD)
+
+                def finish(i, carry, head=head):
+                    rows = pl.ds(pl.multiple_of(i * 128, 128), 128)
+                    u = (near_ref[head, 0, rows, :] + land_ref[head, 0, rows, :].astype(F32)) * SCALE
+                    back = u * cos_ref[rows, :] - pltpu.roll(u, HD // 2, 1) * sin_ref[rows, :]
+                    d_ref[rows, pl.ds(2 * HD + head * HD, HD)] = back.astype(BF16)
+                    v = near_ref[head, 1, rows, :] + land_ref[head, 1, rows, :].astype(F32)
+                    d_ref[rows, pl.ds(4 * HD + head * HD, HD)] = v.astype(BF16)
+                    return carry
+
+                lax.fori_loop(0, 8, finish, 0)
+            for copy in copies:
+                copy.wait_send()
+
+        def output():
+            yield from scatter_rows(spot, post, part_ref, *second)
+
+            def body(strip):
+                layer_ref[strip, :] = (mid_ref[strip, :] + row_sum(spot, second[0], second[1], second[3], strip)).astype(BF16)
+
+            in_strips(ROWS, body)
+
+        play(
+            "owcococowc",
+            c=compute(),
+            o=output(),
+            w=scatter_second(spot, post, sum_a_ref, sum_b_ref, weight_ref, *last),
+        )
+
+    pair = (2, 8 * ROWS, HD)
+    return moving(
         kernel,
-        name="attend_back",
-        out_shape=(shape((8 * ROWS, 2 * HD), BF16), shape(pair, F32), shape(pair, BF16)),
-        in_specs=[pl.BlockSpec(memory_space=pltpu.SMEM)] + [INSIDE] * 8,
-        out_specs=(INSIDE,) * 3,
-        scratch_shapes=[pltpu.VMEM((TILE, HD), F32), pltpu.VMEM(pair, F32), pltpu.VMEM(pair, F32)],
-        compiler_params=pltpu.CompilerParams(vmem_limit_bytes=VMEM),
-    )(meta, queries, here, there, grads, lse, delta, cosine, sine)
-
-
-def to_far_x(block):
-    return lax.ppermute(block, "tp", [(t, t ^ 1) for t in range(8)])
+        "attend_back",
+        (shape((8 * ROWS, PACK), BF16), shape((ROWS, WIDE), BF16), shape((ROWS, n), F32)),
+        (meta, queries, here, there, grads, mixed, lse, cosine, sine, out_part, mid, sum_a, sum_b),
+        [pl.BlockSpec(memory_space=pltpu.SMEM)] + [INSIDE] * 8 + [ANY, INSIDE, ANY, ANY],
+        (INSIDE,) * 3,
+        [
+            pltpu.VMEM((8, TILE), F32),
+            pltpu.VMEM((8, TILE, HD), F32),
+            pltpu.VMEM(pair, F32),
+            pltpu.VMEM((2,) + pair, F32),
+            pltpu.VMEM((2,) + pair, BF16),
+            pltpu.VMEM((2,) + pair, BF16),
+        ]
+        + scatter_scratch()
+        + second_scratch(n)
+        + sems(64),
+        6,
+    )
 
 
 def padded(shard):
@@ -983,39 +1220,32 @@
     cosine, sine = rope_tables(2 * j - j % ROWS + xh * ROWS)
     gain_one = norm_gain.astype(F32)[None]
     gain_two = feed_gain.astype(F32)[None]
-    shard_one = jnp.concatenate([query_weight, key_weight, value_weight, output_weight.T], 1)
+    shard_one = jnp.concatenate([query_weight, key_weight, value_weight], 1)
     shard_two = jnp.concatenate([padded(gate_weight), padded(up_weight), padded(down_weight.T)], 1)
 
     rows_one, full_one = enter(tokens, gain_one, shard_one)
     rows_one = rows_one.reshape(-1, WIDE)
     full_one = full_one.reshape(WIDE, -1)
-    queries, keys, values = project(rows_one, full_one, cosine, sine)
-    here = jnp.stack([keys, values])
-    there = to_far_x(here)
-    attended, lse = attend(meta, queries, here, there)
-    (part,) = partial_rows([(attended, full_one, width, 3)], "attention_out")
-    mid, rows_two, grad_rows, full_two = middle(part.reshape(8, ROWS, WIDE), tokens, gain_two, cotangent, shard_two)
+    queries, here = project(rows_one, full_one, cosine, sine)
+    attended, lse, there, grad_rows, row_two, stage_two, full_out = attend(meta, queries, here, cotangent, shard_two, output_weight.T)
+    full_out = full_out.reshape(WIDE, -1)
+    (part,) = partial_rows([(attended, full_out, width, 0)], "attention_out")
+    mid, rows_two, full_two = middle(part.reshape(8, ROWS, WIDE), tokens, gain_two, row_two, stage_two)
     rows_two, grad_rows, full_two = (a.reshape(-1, a.shape[-1]) for a in (rows_two, grad_rows, full_two.reshape(WIDE, -1)))
     hidden, d_gate, d_up = feed_forward(rows_two, grad_rows, full_two)
-    part, part_out = partial_rows(
-        [(d_gate, full_two, PACK, 0), (d_up, full_two, PACK, 1)], "feed_back", [(hidden, full_two, PACK, 2)]
-    )
-    grads_two = outer([(rows_two, (d_gate, d_up)), (grad_rows, (hidden,))], "feed_grads")
-    layer_output, grad_mid, mid_rows, feed_part, ffn_grad = turn(
-        part.reshape(8, ROWS, WIDE), part_out.reshape(8, ROWS, WIDE), mid, gain_two, cotangent, grads_two
+    (part,) = partial_rows([(d_gate, full_two, PACK, 0), (d_up, full_two, PACK, 1)], "feed_back")
+    grad_mid, mid_rows, feed_part, sum_a, sum_b, part_out = turn(
+        part.reshape(8, ROWS, WIDE), mid, gain_two, cotangent, rows_two, grad_rows, d_gate, d_up, hidden, full_two
     )
     mid_rows = mid_rows.reshape(-1, WIDE)
-    grad_mixed = back_to_heads(mid_rows, full_one)
-    delta = jnp.sum((grad_mixed.astype(F32) * attended.astype(F32)).reshape(4, TILE, 2, HD), -1)
-    delta = delta.transpose(2, 0, 1).reshape(8, TILE)
-    d_query, near, far = attend_back(meta, queries, here, there, grad_mixed, lse, delta, cosine, sine)
-    d_pair = near + to_far_x(far).astype(F32)
-    d_key = (d_pair[0] * SCALE).reshape(-1, 2, HD)
-    d_key = d_key * cosine[:, None] - jnp.roll(d_key, HD // 2, -1) * sine[:, None]
-    d_qkv = jnp.concatenate([d_query, d_key.reshape(-1, width).astype(BF16), d_pair[1].astype(BF16)], 1)
+    grad_mixed = back_to_heads(mid_rows, full_out)
+    d_qkv, layer_output, ffn_grad = attend_back(
+        meta, queries, here, there, grad_mixed, attended, lse, cosine, sine, part_out.reshape(8, ROWS, WIDE), mid, sum_a, sum_b
+    )
     (part,) = partial_rows([(d_qkv, full_one, PACK, 0)], "attention_back")
-    grads_one = outer([(rows_one, (d_qkv,)), (mid_rows, (attended,))], "attention_grads")
-    token_grad, gains, attention_grad = leave(part.reshape(8, ROWS, WIDE), tokens, gain_one, grad_mid, feed_part, grads_one)
+    token_grad, gains, attention_grad = leave(
+        part.reshape(8, ROWS, WIDE), tokens, gain_one, grad_mid, feed_part, rows_one, d_qkv, mid_rows, attended
+    )
     return (
         layer_output,
         token_grad,

time: 546 us -> 391 us (0.72)
  Pallas kernels: 462 us -> 367 us
  waiting for transfers between devices: 40.4 us -> 0 us
  local copies, waits for them, and re-layouts: 20.6 us -> 11.1 us
  other arithmetic: 17.3 us -> 11 us
    ppermute x2 -> x0, waiting for transfers between devices: 40.4 us -> none  [to_far_x(): return lax.ppermute(block, 'tp', [(t, t ^ 1) for t in range(8)])]
    pallas_call x2 -> x0, Pallas kernels: 32.2 us -> none  [the longest x1 16.7 us: attend_back(): pl.pallas_call(kernel, name='attend_back', out_shape=(shape((8 * ROWS, 2...]
    pallas_call x8 -> x6, Pallas kernels: 84.6 us -> 53.1 us  [plain(): pl.pallas_call(kernel, name=name, out_shape=outs, grid=grid, in_specs=in_...]
    pallas_call x4 -> x6, Pallas kernels: 345 us -> 314 us  [moving(): pl.pallas_call(kernel, name=name, out_shape=outs, in_specs=in_specs, out_...]
  transfers between devices with their start and end apart: 2 -> 0, of which waited for: 2 -> 0; matrix products, arithmetic and copies ran while one was open for 1% -> 0% of each run, Pallas kernels for 0% -> 0%
where the time goes in v2:
time: 391 us; the launch traced here: 390 us
  Pallas kernels  367 us (94%)
  local copies, waits for them, and re-layouts  11.1 us (3%)
  other arithmetic  11 us (3%)
    pallas_call x6, Pallas kernels, moving(): pl.pallas_call(kernel, name=name, out_shape=outs, in_specs=in_specs, out_...  314 us
    pallas_call x6, Pallas kernels, plain(): pl.pallas_call(kernel, name=name, out_shape=outs, grid=grid, in_specs=in_...  53.1 us

profile of v2, /device:TPU:1, one launch (start us, length us, event | category | flops | bytes accessed | tf_op | source)
XLA Modules:
  0.0 389.9 jit_solution(13172221960276461420)
XLA Ops:
  0.7 1.3 fusion.13
  2.0 1.2 pad_add_fusion.meta_ref
  3.2 1.3 broadcast_in_dim.21
  4.5 1.3 broadcast_in_dim.22
  5.8 1.6 copy.24
  7.4 1.6 pad_maximum_fusion.2
  8.9 1.1 fusion.5
  10.1 1.1 copy.23
  11.2 1.9 fusion.6
  13.1 1.3 pad_maximum_fusion
  14.4 35.0 %enter.1 = (bf16[8,128,2048]{2,1,0:T(8,128)(2,1)}, bf16[4,4,2,64,768]{4,3,2,1,0:T(8,128)(2,1)}) custom-call(bf16[128,2048]{1,0:T(8,128)(2,1)} %tokens_ref.5, f32[1,2048]{1,0:T(1,128)} %bitcast.53, bf16[2,64,768]{2,1,0:T(8,128)(2,1)} %bitcast.50), custom_call_target="tpu_custom_call" | custom-call | tf_op jit(solution)/shard_map/enter/pallas_call | solution.py:586
  49.4 7.7 %project.1 = (bf16[1024,256]{1,0:T(8,128)(2,1)}, bf16[2,1024,256]{2,1,0:T(8,128)(2,1)}) custom-call(bf16[1024,2048]{1,0:T(8,128)(2,1)} %bitcast.33, bf16[2048,768]{1,0:T(8,128)(2,1)} %bitcast.44, f32[1024,128]{1,0:T(8,128)} %get-tuple-element.92.cos_ref, f32[1024,128]{1,0:T(8,128)} %get-tuple-element.93.sin_ref), custom_call_target="tpu_custom_call" | custom-call | tf_op jit(solution)/shard_map/project/pallas_call | solution.py:829
  57.1 47.9 %attend.1 = (bf16[1024,256]{1,0:T(8,128)(2,1)}, f32[8,256]{1,0:T(8,128)}, bf16[2,1024,256]{2,1,0:T(8,128)(2,1)}, bf16[8,128,2048]{2,1,0:T(8,128)(2,1)}, bf16[4,6...) custom-call(s32[2]{0:T(128)} %pad_add_fusion.meta_ref, ...), custom_call_target="tpu_custom_call" | custom-call | tf_op jit(solution)/shard_map/attend/pallas_call | solution.py:586
  105.0 5.1 %attention_out.1 = bf16[1024,2048]{1,0:T(8,128)(2,1)} custom-call(bf16[1024,256]{1,0:T(8,128)(2,1)} %get-tuple-element.45.refs_0_.o_ref.mixed_hbm, bf16[2048,256]{1,0:T(8,128)(2,1)} %bitcast.47), custom_call_target="tpu_custom_call" | custom-call | tf_op jit(solution)/shard_map/attention_out/pallas_call | solution.py:829
  110.1 59.6 %middle.1 = (f32[128,2048]{1,0:T(8,128)}, bf16[8,128,2048]{2,1,0:T(8,128)(2,1)}, bf16[4,4,2,64,2304]{4,3,2,1,0:T(8,128)(2,1)}) custom-call(bf16[8,128,2048]{2,1,0:T(8,128)(2,1)} %bitcast.43, bf16[128,2048]{1,0:T(8,128)(2,1)} %tokens_ref.5, f32[1,2048]{1,0:T(1,128)} %bitcast.55, bf16[4,64,2304]{2,1,0:T(8,128)(2,1)} %get-tuple-element.47.row_ref, ...), custom_call_target="tpu_custom_call" | custom-call | tf_op jit(solution)/shard_map/middle/pallas_call | solution.py:586
  169.7 16.3 %feed_forward.1 = (bf16[1024,768]{1,0:T(8,128)(2,1)}, bf16[1024,768]{1,0:T(8,128)(2,1)}, bf16[1024,768]{1,0:T(8,128)(2,1)}) custom-call(bf16[1024,2048]{1,0:T(8,128)(2,1)} %bitcast.40, bf16[1024,2048]{1,0:T(8,128)(2,1)} %bitcast.38, bf16[2048,2304]{1,0:T(8,128)(2,1)} %bitcast.27, bf16[2048,2304]{1,0:T(8,128)(2,1)} %bitcast.28, bf16[2048,2304]{1,0:T(8,128)(2,1)} %bitcast.29), custom_call_target="tpu_custom_call" | custom-call | tf_op jit(solution)/shard_map/feed_forward/pallas_call | solution.py:829
  186.0 11.5 %feed_back.1 = bf16[1024,2048]{1,0:T(8,128)(2,1)} custom-call(bf16[1024,768]{1,0:T(8,128)(2,1)} %get-tuple-element.52.refs_0_.gate_hbm, bf16[2048,2304]{1,0:T(8,128)(2,1)} %bitcast.30, bf16[1024,768]{1,0:T(8,128)(2,1)} %get-tuple-element.53.refs_2_.up_hbm, bf16[2048,2304]{1,0:T(8,128)(2,1)} %bitcast.31), custom_call_target="tpu_custom_call" | custom-call | tf_op jit(solution)/shard_map/feed_back/pallas_call | solution.py:829
  197.5 68.9 %turn.1 = (f32[128,2048]{1,0:T(8,128)}, bf16[8,128,2048]{2,1,0:T(8,128)(2,1)}, f32[1,2048]{1,0:T(1,128)}, bf16[4,64,2304]{2,1,0:T(8,128)(2,1)}, bf16[4,64,2304]{...) custom-call(bf16[8,128,2048]{2,1,0:T(8,128)(2,1)} %bitcast.42, f32[128,2048]{1,0:T(8,128)} %get-tuple-element.54.mid_ref, ...), custom_call_target="tpu_custom_call" | custom-call | tf_op jit(solution)/shard_map/turn/pallas_call | solution.py:586
  266.5 5.0 %back_to_heads.1.g_ref = bf16[1024,256]{1,0:T(8,128)(2,1)} custom-call(bf16[1024,2048]{1,0:T(8,128)(2,1)} %bitcast.35, bf16[2048,256]{1,0:T(8,128)(2,1)} %bitcast.48), custom_call_target="tpu_custom_call" | custom-call | tf_op jit(solution)/shard_map/back_to_heads/pallas_call | solution.py:829
  271.5 53.5 %attend_back.1 = (bf16[1024,768]{1,0:T(8,128)(2,1)}, bf16[128,2048]{1,0:T(8,128)(2,1)}, f32[128,2304]{1,0:T(8,128)}) custom-call(s32[2]{0:T(128)} %pad_add_fusion.meta_ref, bf16[1024,256]{1,0:T(8,128)(2,1)} %get-tuple-element.42.q_ref, bf16[2,1024,256]{2,1,0:T(8,128)(2,1)} %get-tuple-element.43.here_ref, bf16[2,1024,256]{2,1,0:T(8,128)(2,1)} %get-tuple-element.44.there_ref, ...), custom_call_target="tpu_custom_call" | custom-call | tf_op jit(solution)/shard_map/attend_back/pallas_call | solution.py:586
  325.0 7.4 %attention_back.1 = bf16[1024,2048]{1,0:T(8,128)(2,1)} custom-call(bf16[1024,768]{1,0:T(8,128)(2,1)} %get-tuple-element.62.refs_0_.d_hbm, bf16[2048,768]{1,0:T(8,128)(2,1)} %bitcast.45), custom_call_target="tpu_custom_call" | custom-call | tf_op jit(solution)/shard_map/attention_back/pallas_call | solution.py:829
  332.4 49.0 %leave.1 = (f32[128,2048]{1,0:T(8,128)}, f32[8,128]{1,0:T(8,128)}, f32[128,1024]{1,0:T(8,128)}) custom-call(bf16[8,128,2048]{2,1,0:T(8,128)(2,1)} %bitcast.37, bf16[128,2048]{1,0:T(8,128)(2,1)} %tokens_ref.5, f32[1,2048]{1,0:T(1,128)} %bitcast.54, f32[128,2048]{1,0:T(8,128)} %get-tuple-element.63.grad_ref, f32[1,2048]{1,0:T(1,128)} %get-tuple-element.64.feed_ref, ...), custom_call_target="tpu_custom_call" | custom-call | tf_op jit(solution)/shard_map/leave/pallas_call | solution.py:586
  381.4 0.0 copy-start
  381.4 1.3 slice_bitcast_fusion.2
  382.7 1.8 slice_bitcast_fusion.1
  384.5 0.8 copy.25
  385.3 0.0 copy-done
  385.3 0.1 slice_bitcast_fusion
  385.4 0.0 copy-start.2
  385.4 0.9 copy.28
  386.3 0.0 copy-start.1
  386.3 0.9 copy.27
  387.2 0.9 copy.26
  388.1 0.0 copy-done.2
  388.1 0.8 copy.31
  388.9 0.0 copy-done.1
  388.9 1.0 copy.32
  (2 shorter events, 0.0 us)
Async XLA Ops:
  381.4 3.9 %copy-start = (f32[128,2304]{1,0:T(8,128)S(1)}, f32[128,2304]{1,0:T(8,128)}, u32[]{:S(2)}) copy-start(f32[128,2304]{1,0:T(8,128)} %get-tuple-element.68) | copy-start | bytes 3538948
  385.4 2.7 copy-start.2
  386.3 2.6 copy-start.1

commit v3 on v2

v3 whole, which is shorter than its diff:
```python
import functools
import math

import jax
import jax.numpy as jnp
from jax import lax
from jax.experimental import pallas as pl
from jax.experimental.pallas import tpu as pltpu
from jax.sharding import PartitionSpec as P

HD = 128
EPS = 1e-05
ROPE_BASE = 10000.0
F32 = jnp.float32
BF16 = jnp.bfloat16
MESH = pl.DeviceIdType.MESH
AXES = ("fsdp", "tp")
ROWS = 128
WIDE = 2048
PACK = 768
SCALE = 1.0 / math.sqrt(HD)
LOG2E = 1.4426950408889634
VMEM = 56 << 20


class Spot:
    def __init__(self):
        f, t = lax.axis_index("fsdp"), lax.axis_index("tp")
        self.y, self.xl, self.c = lax.div(f, 4), lax.rem(lax.div(f, 2), 2), lax.rem(f, 2)
        self.z, self.xh = lax.div(t, 2), lax.rem(t, 2)
        self.x = self.xh * 2 + self.xl
        self.own = self.xl * 2 + self.c
        self.away = lax.rem(self.xh + self.c, 2)
        self.home = self.away == 0
        self.turn = 1 - lax.rem(self.away + self.xl, 2)
        self.ahead = 1 + 2 * self.turn
        self.back = 3 - 2 * self.turn
        self.near = (1 - self.xl) * 2
        self.same = self.xl * 2

    def at(self, dy=0, dx=0, dz=0, core=None):
        y, z, x = lax.rem(self.y + dy, 4), lax.rem(self.z + dz, 4), lax.rem(self.x + dx, 4)
        return (y * 4 + lax.rem(x, 2) * 2 + (self.c if core is None else core), z * 2 + lax.div(x, 2))

    def other(self):
        return self.at(core=1 - self.c)

    def seat(self, slot):
        return (self.y * 4 + slot, self.z * 2 + self.c)

    def bench(self, slot):
        return (self.y * 4 + slot, self.z * 2 + self.xh)

    def block(self, dz=0, flip=False):
        return (1 - self.c if flip else self.c) * 4 + lax.rem(self.z + dz, 4)


class Post:
    def __init__(self, out_sems, in_sems):
        self.out_sems, self.in_sems, self.n_out, self.n_in = out_sems, in_sems, 0, 0

    def slots(self, n):
        base = self.n_in
        self.n_in += n
        return base

    def copy(self, src, dst, device, slot=None):
        slot = self.slots(1) if slot is None else slot
        self.n_out += 1
        return pltpu.make_async_remote_copy(
            src_ref=src,
            dst_ref=dst,
            send_sem=self.out_sems.at[self.n_out - 1],
            recv_sem=self.in_sems.at[slot],
            device_id=device,
            device_id_type=MESH,
        )

    def arrival(self, dst, device, slot):
        return pltpu.make_async_remote_copy(
            src_ref=dst,
            dst_ref=dst,
            send_sem=self.out_sems.at[0],
            recv_sem=self.in_sems.at[slot],
            device_id=device,
            device_id_type=MESH,
        )

    def local(self, src, dst):
        self.n_out += 1
        return pltpu.make_async_copy(src, dst, self.out_sems.at[self.n_out - 1])


def greet(spot, sources, count, home=(), away=()):
    barrier = pltpu.get_barrier_semaphore()

    def signal(devices):
        for device in devices:
            pl.semaphore_signal(barrier, inc=1, device_id=device, device_id_type=MESH)

    signal(sources)
    if home:
        count = count + 3 + spot.away

        @pl.when(spot.home)
        def _():
            signal(home)

        @pl.when(jnp.logical_not(spot.home))
        def _():
            signal(away)

    pl.semaphore_wait(barrier, count)


def row_peers(spot):
    return [spot.at(dz=1), spot.at(dz=3), spot.other()]


def y_peers(spot):
    return [spot.at(dy=1), spot.at(dy=3)]


def gather_peers(spot):
    near = [spot.at(dx=spot.back, core=0), spot.at(dx=spot.back, core=1)]
    return {"home": near + [spot.other()], "away": near + [spot.at(dx=1), spot.at(dx=3)]}


def collect_peers(spot):
    usual = [spot.at(dx=1, core=spot.xh), spot.at(dx=3, core=spot.xh), spot.at(dx=spot.ahead)]
    return {"home": usual, "away": usual + [spot.other()]}


def half_of(ref, number):
    rows = ref.shape[0] // 2
    return ref.at[pl.ds(number * rows, rows)]


def after(spot, k):
    return lax.rem(spot.own + k, 4)


def play(order, **jobs):
    for letter in order:
        next(jobs[letter], None)
    for job in jobs.values():
        for _ in job:
            pass


def gather_rows(spot, post, own, rows):
    up, down, core = spot.at(dz=1), spot.at(dz=3), spot.other()
    half = ROWS // 2
    low, high = pl.ds(0, half), pl.ds(half, half)
    here, below, above, far = (spot.block(dz) for dz in (0, 3, 1, 2))
    a = post.copy(own, rows.at[here], up)
    b = post.copy(own, rows.at[here], down)
    k0 = post.copy(own, rows.at[here], core)
    keep = post.local(own, rows.at[here])
    for copy in (a, b, k0, keep):
        copy.start()
    yield
    a.wait_recv()
    fa = post.copy(rows.at[below, low], rows.at[below, low], up)
    k1 = post.copy(rows.at[below], rows.at[below], core)
    fa.start()
    k1.start()
    b.wait_recv()
    fb = post.copy(rows.at[above, high], rows.at[above, high], down)
    k2 = post.copy(rows.at[above], rows.at[above], core)
    fb.start()
    k2.start()
    yield
    fa.wait_recv()
    fb.wait_recv()
    k3 = post.copy(rows.at[far], rows.at[far], core)
    k3.start()
    yield
    keep.wait()
    for copy in (k0, k1, k2, k3):
        copy.wait_recv()
    for copy in (a, b, fa, fb, k0, k1, k2, k3):
        copy.wait_send()


def in_strips(count, body):
    def step(i, carry):
        body(pl.ds(pl.multiple_of(i * 16, 16), 16))
        return carry

    lax.fori_loop(0, count // 16, step, 0)


def add_into(target, other, rows=ROWS, start=0):
    def body(strip):
        strip = pl.ds(pl.multiple_of(strip.start + start, 16), 16)
        target[strip, :] = (target[strip, :].astype(F32) + other[strip, :].astype(F32)).astype(BF16)

    in_strips(rows, body)


def scatter_rows(spot, post, part, mine, land, far, gone):
    up, down, core = spot.at(dz=1), spot.at(dz=3), spot.other()
    half = ROWS // 2
    low, high = pl.ds(0, half), pl.ds(half, half)
    steps = [lax.rem(spot.z + dz, 4) for dz in (2, 3, 1, 0)]
    to_core = [post.copy(part.at[(1 - spot.c) * 4 + s], land.at[s], core) for s in steps]
    load = [post.local(part.at[spot.c * 4 + s], mine.at[s]) for s in steps]
    for a, b in zip(to_core, load):
        a.start()
        b.start()
    yield

    def ready(k):
        to_core[k].wait_recv()
        load[k].wait()

    distant, lower, upper, here = steps
    ready(0)
    add_into(mine.at[distant], land.at[distant])
    f_low = post.copy(mine.at[distant, low], far.at[low], down)
    f_high = post.copy(mine.at[distant, high], far.at[high], up)
    f_low.start()
    f_high.start()
    ready(1)
    add_into(mine.at[lower], land.at[lower])
    d_high = post.copy(mine.at[lower, high], gone.at[0, high], down)
    d_high.start()
    ready(2)
    add_into(mine.at[upper], land.at[upper])
    u_low = post.copy(mine.at[upper, low], gone.at[1, low], up)
    u_low.start()
    ready(3)
    yield
    f_low.wait_recv()
    add_into(mine.at[lower], far, half)
    d_low = post.copy(mine.at[lower, low], gone.at[0, low], down)
    d_low.start()
    f_high.wait_recv()
    add_into(mine.at[upper], far, half, half)
    u_high = post.copy(mine.at[upper, high], gone.at[1, high], up)
    u_high.start()
    yield
    for copy in (d_high, u_low, d_low, u_high):
        copy.wait_recv()
    for copy in to_core + [f_low, f_high, d_high, u_low, d_low, u_high]:
        copy.wait_send()


def row_sum(spot, mine, land, gone, strip):
    parts = [mine[spot.z, strip, :], land[spot.z, strip, :], gone[0, strip, :], gone[1, strip, :]]
    return sum(part.astype(F32) for part in parts)


def scatter_scratch():
    block = (ROWS, WIDE)
    return [
        pltpu.VMEM((4,) + block, BF16),
        pltpu.VMEM((4,) + block, BF16),
        pltpu.VMEM(block, BF16),
        pltpu.VMEM((2,) + block, BF16),
    ]


def x_gather(spot, post, src, dst_at):
    base, far = post.slots(4), post.slots(4)
    sends = [post.copy(src, dst_at(spot.own), spot.at(dx=dx, core=spot.xh), base + spot.own) for dx in (1, 3)]
    cross = post.copy(src, dst_at(spot.own), spot.other(), base + spot.own)
    keep = post.local(src, dst_at(spot.own))
    for copy in sends:
        copy.start()

    @pl.when(spot.home)
    def _():
        keep.start()

    @pl.when(jnp.logical_not(spot.home))
    def _():
        cross.start()

    def landed(dst, slot):
        post.arrival(dst, spot.at(dx=1), slot).wait_recv()

    yield
    for core in range(2):
        block = dst_at(spot.near + core)
        landed(block, base + spot.near + core)
        part = half_of(block, spot.turn)
        sends.append(post.copy(part, part, spot.at(dx=spot.ahead), far + 2 * core + spot.turn))
        sends[-1].start()
    yield

    @pl.when(spot.home)
    def _():
        slot = spot.same + 1 - spot.c
        landed(dst_at(slot), base + slot)
        keep.wait()

    @pl.when(jnp.logical_not(spot.home))
    def _():
        for core in range(2):
            for number in range(2):
                landed(half_of(dst_at(spot.same + core), number), far + 2 * core + number)
        cross.wait_send()

    for copy in sends:
        copy.wait_send()


def y_gather(spot, post, src, dst_at):
    up, down = spot.at(dy=1), spot.at(dy=3)
    here, below, above = dst_at(spot.y), dst_at(lax.rem(spot.y + 3, 4)), dst_at(lax.rem(spot.y + 1, 4))
    a, b, keep = post.copy(src, here, up), post.copy(src, here, down), post.local(src, here)
    for copy in (a, b, keep):
        copy.start()
    yield
    a.wait_recv()
    fa = post.copy(half_of(below, 0), half_of(below, 0), up)
    fa.start()
    b.wait_recv()
    fb = post.copy(half_of(above, 1), half_of(above, 1), down)
    fb.start()
    yield
    keep.wait()
    for copy in (fa, fb):
        copy.wait_recv()
    for copy in (a, b, fa, fb):
        copy.wait_send()


def together(*jobs):
    live = list(jobs)
    while live:
        live = [job for job in live if next(job, job) is not job]
        if live:
            yield


def gather_first(spot, post, shard, row, stage):
    return together(
        x_gather(spot, post, shard.at[0], lambda slot: row.at[slot]),
        y_gather(spot, post, shard.at[1], lambda y: stage.at[y]),
    )


def gather_second(spot, post, row, stage, full):
    return together(
        x_gather(spot, post, stage, lambda slot: full.at[:, slot, 1]),
        y_gather(spot, post, row, lambda y: full.at[y, :, 0]),
    )


def sum_parts(parts, write):
    def body(strip):
        write(strip, sum(part[strip, :].astype(F32) for part in parts))

    in_strips(parts[0].shape[0], body)


def add_block(target, other):
    if len(target.shape) == 2:
        add_into(target, other, target.shape[0])
    else:

        def step(i, carry):
            add_into(target.at[i], other.at[i], target.shape[1])
            return carry

        lax.fori_loop(0, target.shape[0], step, 0)


class XCollect:
    def __init__(self, spot, post, src_at, land, hop):
        self.spot, self.post, self.src_at, self.land, self.hop = spot, post, src_at, land, hop
        self.in_land, self.in_hop = post.slots(5), post.slots(2)
        self.sends = []

    def to_near(self, core, src, number):
        spot = self.spot
        copy = self.post.copy(
            src,
            half_of(self.land.at[spot.turn], number),
            spot.seat(spot.near + core),
            self.in_land + 2 * spot.turn + number,
        )
        copy.start()
        self.sends.append(copy)

    def start(self):
        spot, post = self.spot, self.post
        cross_slot = spot.same + 1 - spot.c
        self.cross = post.copy(self.src_at(cross_slot), self.land.at[2], spot.other(), self.in_land + 4)
        self.keep = post.local(self.src_at(spot.own), self.land.at[2])
        self.far = []
        for core in range(2):
            for number, dx in ((0, 3), (1, 1)):
                src = half_of(self.src_at(spot.same + core), number)
                self.far.append(post.copy(src, self.hop.at[core], spot.at(dx=dx), self.in_hop + core))

        @pl.when(spot.home)
        def _():
            self.cross.start()
            self.keep.start()

        @pl.when(jnp.logical_not(spot.home))
        def _():
            for copy in self.far:
                copy.start()

        for core in range(2):
            self.to_near(core, half_of(self.src_at(spot.near + core), 1 - spot.turn), 1 - spot.turn)

    def relay(self):
        spot, post = self.spot, self.post
        for core in range(2):
            post.arrival(self.hop.at[core], spot.at(dx=1), self.in_hop + core).wait_recv()
            add_block(self.hop.at[core], half_of(self.src_at(spot.near + core), spot.turn))
            self.to_near(core, self.hop.at[core], spot.turn)

    def finish(self):
        spot, post = self.spot, self.post
        for side in range(2):
            for number in range(2):
                dst = half_of(self.land.at[side], number)
                post.arrival(dst, spot.at(dx=1), self.in_land + 2 * side + number).wait_recv()

        @pl.when(spot.home)
        def _():
            self.keep.wait()
            self.cross.wait_send()

        @pl.when(jnp.logical_not(spot.home))
        def _():
            post.arrival(self.land.at[2], spot.at(dx=1), self.in_land + 4).wait_recv()
            for copy in self.far:
                copy.wait_send()

        for copy in self.sends:
            copy.wait_send()

    def parts(self):
        return [self.land.at[side] for side in range(3)]


class YCollect:
    def __init__(self, spot, post, src_at, land, hop):
        self.spot, self.post, self.src_at, self.land, self.hop = spot, post, src_at, land, hop
        self.up, self.down = spot.at(dy=1), spot.at(dy=3)
        self.y = [lax.rem(spot.y + k, 4) for k in range(4)]

    def start_far(self):
        block = self.src_at(self.y[2])
        self.far = [
            self.post.copy(half_of(block, 0), self.hop.at[0], self.down),
            self.post.copy(half_of(block, 1), self.hop.at[1], self.up),
        ]
        for copy in self.far:
            copy.start()

    def start_lower(self):
        self.low = [self.post.copy(half_of(self.src_at(self.y[3]), 1), half_of(self.land.at[0], 1), self.down)]
        self.low[0].start()

    def start_upper(self):
        self.high = [self.post.copy(half_of(self.src_at(self.y[1]), 0), half_of(self.land.at[1], 0), self.up)]
        self.high[0].start()

    def relay(self):
        for number, k, target in ((0, 3, self.down), (1, 1, self.up)):
            self.far[number].wait_recv()
            hop = self.hop.at[number]
            add_block(hop, half_of(self.src_at(self.y[k]), number))
            copy = self.post.copy(hop, half_of(self.land.at[number], number), target)
            copy.start()
            (self.low if number == 0 else self.high).append(copy)

    def finish(self):
        for copy in self.low + self.high:
            copy.wait_recv()
        for copy in self.far + self.low + self.high:
            copy.wait_send()

    def parts(self):
        return [self.src_at(self.spot.y), self.land.at[0], self.land.at[1]]


class Gradients:
    def __init__(self, spot, post, groups, full, land_x, hop_x, land_y, hop_y, sum_a, sum_b):
        self.spot, self.groups, self.full, self.sum_a, self.sum_b = spot, groups, full, sum_a, sum_b
        self.y = [lax.rem(spot.y + k, 4) for k in (2, 3, 1, 0)]
        self.x = [
            XCollect(spot, post, lambda slot, y=y: full.at[y, slot, 0], land_x.at[j], hop_x.at[j])
            for j, y in enumerate(self.y)
        ]
        self.over_y = YCollect(spot, post, lambda y: full.at[y, :, 1], land_y, hop_y)

    def make(self, j):
        y = self.y[j]

        def part(s, carry):
            columns = pl.ds(pl.multiple_of(y * 512 + s * 256, 256), 256)
            at = 0
            for rows, values in self.groups:
                left = rows[:, columns]
                for value in values:
                    width = value.shape[1]
                    block = dot(left, value[...], 0, 0).astype(BF16)
                    for i in range(4):
                        self.full[y, 2 * s + i // 2, i % 2, :, at : at + width] = block[i * 64 : (i + 1) * 64]
                    at += width
            return carry

        lax.fori_loop(0, 2, part, 0)
        (self.over_y.start_far, self.over_y.start_lower, self.over_y.start_upper, lambda: None)[j]()
        self.x[j].start()

    def sum_x(self, j):
        def write(strip, total):
            self.sum_a[self.y[j], strip, :] = total.astype(BF16)

        self.x[j].finish()
        sum_parts(self.x[j].parts(), write)

    def sum_y(self):
        self.over_y.finish()

        def slot_sum(slot, carry):
            def write(strip, total):
                self.sum_b[slot, strip, :] = total.astype(BF16)

            sum_parts([part.at[slot] for part in self.over_y.parts()], write)
            return carry

        lax.fori_loop(0, 4, slot_sum, 0)

    def steps(self):
        self.make(0)
        yield
        self.make(1)
        yield
        self.make(2)
        self.x[0].relay()
        yield
        self.make(3)
        self.x[1].relay()
        yield
        self.over_y.relay()
        self.x[2].relay()
        yield
        self.x[3].relay()
        yield
        for j in range(4):
            self.sum_x(j)
            yield
        self.sum_y()


def load(post, pairs):
    copies = [post.local(src, dst) for src, dst in pairs]
    for copy in copies:
        copy.start()
    return copies


def gradient_scratch(n):
    return [
        pltpu.VMEM((4, 4, 2, 64, n), BF16),
        pltpu.VMEM((4, 3, 64, n), BF16),
        pltpu.VMEM((4, 2, 32, n), BF16),
        pltpu.VMEM((2, 4, 64, n), BF16),
        pltpu.VMEM((2, 2, 64, n), BF16),
    ]


def scatter_low(spot, post, sum_a, write, land, hop):
    over_y = YCollect(spot, post, lambda y: sum_a.at[y], land, hop)
    over_y.start_far()
    over_y.start_lower()
    over_y.start_upper()
    yield
    over_y.relay()
    yield
    over_y.finish()
    sum_parts(over_y.parts(), write)


def scatter_high(spot, post, sum_b, write, land, hop):
    over_x = XCollect(spot, post, lambda slot: sum_b.at[slot], land, hop)
    over_x.start()
    yield
    over_x.relay()
    yield
    over_x.finish()
    sum_parts(over_x.parts(), write)


def strip_writer(out, start=0):
    def write(strip, total):
        out[pl.ds(pl.multiple_of(strip.start + start, 16), 16), :] = total

    return write


def low_scratch(n):
    return [pltpu.VMEM((2, 64, n), BF16), pltpu.VMEM((2, 32, n), BF16)]


def high_scratch(n):
    return [pltpu.VMEM((3, 64, n), BF16), pltpu.VMEM((2, 32, n), BF16)]


def sum_gains(spot, post, parts, out, from_y, over_y, from_chip, over_fsdp, from_tp):
    y_copies = []
    for i, k in enumerate((2, 1, 3)):
        y = lax.rem(spot.y + k, 4)
        y_copies.append(post.copy(parts.at[pl.ds(y * 4, 4)], from_y.at[i], spot.at(dy=k)))
        y_copies[-1].start()
    yield
    for copy in y_copies:
        copy.wait_recv()
    over_y[...] = parts[pl.ds(spot.y * 4, 4)] + from_y[0] + from_y[1] + from_y[2]
    chip_copies = []
    for i, k in enumerate((1, 2, 3)):
        slot = after(spot, k)
        chip_copies.append(post.copy(over_y.at[slot], from_chip.at[i], spot.bench(slot)))
        chip_copies[-1].start()
    yield
    for copy in chip_copies:
        copy.wait_recv()
    over_fsdp[...] = over_y[spot.own] + from_chip[0] + from_chip[1] + from_chip[2]
    tp_copies = []
    for i, (dz, dx) in enumerate(TP_MOVES):
        tp_copies.append(post.copy(over_fsdp, from_tp.at[i], spot.at(dz=dz, dx=dx)))
        tp_copies[-1].start()
    yield
    for copy in tp_copies:
        copy.wait_recv()
    out[...] = over_fsdp[...] + sum(from_tp[i] for i in range(7))
    for copy in y_copies + chip_copies + tp_copies:
        copy.wait_send()


TP_MOVES = [(dz, dx) for dx in (0, 2) for dz in (0, 1, 2, 3) if (dz, dx) != (0, 0)]


def gain_sources(spot):
    return (
        [spot.at(dy=k) for k in (1, 2, 3)]
        + [spot.bench(after(spot, k)) for k in (1, 2, 3)]
        + [spot.at(dz=(4 - dz) % 4, dx=dx) for dz, dx in TP_MOVES]
    )


ANY = pl.BlockSpec(memory_space=pl.ANY)
INSIDE = pl.BlockSpec(memory_space=pltpu.VMEM)


def sems(n):
    return [pltpu.SemaphoreType.DMA((n,)), pltpu.SemaphoreType.DMA((n,))]


def moving(kernel, name, outs, inputs, in_specs, out_specs, scratch, cid):
    return pl.pallas_call(
        kernel,
        name=name,
        out_shape=outs,
        in_specs=in_specs,
        out_specs=out_specs,
        scratch_shapes=scratch,
        compiler_params=pltpu.CompilerParams(collective_id=cid, has_side_effects=True, vmem_limit_bytes=VMEM),
    )(*inputs)


def shape(dims, dtype):
    return jax.ShapeDtypeStruct(dims, dtype)


def normed(rows, gain):
    inverse = lax.rsqrt(jnp.mean(rows * rows, -1, keepdims=True) + EPS)
    scaled = rows * inverse
    return inverse, scaled, (scaled * gain).astype(BF16)


def enter(tokens, gain, query, key, value, out, gate, up, down):
    n_one, n_two, n_out = query.shape[1] * 3, PACK * 3, out.shape[0]

    def kernel(
        tokens_ref, gain_ref, query_ref, key_ref, value_ref, out_ref, gate_ref, up_ref, down_ref,
        rows_ref, full_ref, row_out_ref, row_ref, rest_ref, cos_ref, sin_ref,
        shard_one, row_one, stage_one, shard_out, shard_two, own, out_sems, in_sems,
    ):
        spot, post = Spot(), Post(out_sems, in_sems)
        for i in range(2):
            rows = pl.ds(i * 64, 64)
            for j, ref in enumerate((query_ref, key_ref, value_ref)):
                shard_one[i, :, j * 256 : (j + 1) * 256] = ref[rows, :]
        greet(spot, row_peers(spot) + y_peers(spot), 5, **gather_peers(spot))

        def weights():
            yield from gather_first(spot, post, shard_one, row_one, stage_one)
            yield from gather_second(spot, post, row_one, stage_one, full_ref)

        def tables():
            exponent = lax.broadcasted_iota(jnp.int32, (1, HD), 1)
            exponent = lax.rem(exponent, HD // 2).astype(F32)
            inverse = jnp.exp(exponent * (-2.0 / HD) * math.log(ROPE_BASE))
            sign = jnp.where(lax.broadcasted_iota(jnp.int32, (1, HD), 1) < HD // 2, -1.0, 1.0)

            def step(i, carry):
                angles = place_of(i * 16, 16, spot.xh, 0).astype(F32) * inverse
                strip = pl.ds(pl.multiple_of(i * 16, 16), 16)
                cos_ref[strip, :] = jnp.cos(angles)
                sin_ref[strip, :] = jnp.sin(angles) * sign
                return carry

            lax.fori_loop(0, 8 * ROWS // 16, step, 0)

        w = weights()
        next(w)

        def body(strip):
            own[strip, :] = normed(tokens_ref[strip, :].astype(F32), wide_gain(gain_ref))[2]

        in_strips(ROWS, body)
        r = gather_rows(spot, post, own, rows_ref)
        next(r)
        shard_out[...] = out_ref[...].astype(F32).T.astype(BF16)
        o = x_gather(spot, post, shard_out, lambda slot: row_out_ref.at[slot])
        next(o)
        shard_two[...] = jnp.zeros_like(shard_two)
        rest_ref[...] = jnp.zeros_like(rest_ref)
        wide = gate.shape[0]
        for j, ref in enumerate((gate_ref, up_ref, down_ref)):
            turned = ref[...].astype(F32).T.astype(BF16)
            shard_two[:, j * PACK : j * PACK + wide] = turned[:64]
            rest_ref[:, j * PACK : j * PACK + wide] = turned[64:]
        next(w)
        next(w)
        f = x_gather(spot, post, shard_two, lambda slot: row_ref.at[slot])
        next(f)
        next(o)
        next(r)
        tables()
        play("wfrwfor", r=r, w=w, f=f, o=o)

    half = pltpu.VMEM((4, 64, n_one), BF16)
    table = shape((8 * ROWS, HD), F32)
    return moving(
        kernel,
        "enter",
        (shape((8, ROWS, WIDE), BF16), shape((4, 4, 2, 64, n_one), BF16), shape((4, ROWS, n_out), BF16))
        + (shape((4, 64, n_two), BF16), shape((64, n_two), BF16), table, table),
        (tokens, gain, query, key, value, out, gate, up, down),
        [INSIDE] * 9,
        (ANY, ANY) + (INSIDE,) * 5,
        [pltpu.VMEM((2, 64, n_one), BF16), half, half, pltpu.VMEM((ROWS, n_out), BF16), pltpu.VMEM((64, n_two), BF16)]
        + [pltpu.VMEM((ROWS, WIDE), BF16)]
        + sems(60),
        1,
    )


def middle(part, tokens, gain, row, stage):
    n = row.shape[-1]

    def kernel(part_ref, tokens_ref, gain_ref, row_ref, stage_ref, mid_ref, rows_ref, full_ref, own, *rest):
        scatter, (out_sems, in_sems) = rest[:4], rest[4:]
        mine, land, far, gone = scatter
        spot, post = Spot(), Post(out_sems, in_sems)
        greet(spot, row_peers(spot) + y_peers(spot), 5, **gather_peers(spot))

        def main():
            yield from scatter_rows(spot, post, part_ref, mine, land, far, gone)

            def body(strip):
                mid = tokens_ref[strip, :].astype(F32) + row_sum(spot, mine, land, gone, strip)
                mid_ref[strip, :] = mid
                own[strip, :] = normed(mid, wide_gain(gain_ref))[2]

            in_strips(ROWS, body)
            yield from gather_rows(spot, post, own, rows_ref)

        play("mwmmmwmmm", m=main(), w=gather_second(spot, post, row_ref, stage_ref, full_ref))

    return moving(
        kernel,
        "middle",
        (shape((ROWS, WIDE), F32), shape((8, ROWS, WIDE), BF16), shape((4, 4, 2, 64, n), BF16)),
        (part, tokens, gain, row, stage),
        [ANY, INSIDE, INSIDE, INSIDE, INSIDE],
        (INSIDE, ANY, ANY),
        [pltpu.VMEM((ROWS, WIDE), BF16)] + scatter_scratch() + sems(64),
        2,
    )


def wide_gain(gain_ref):
    return gain_ref[...].astype(F32).reshape(1, WIDE)


def norm_back(upstream, rows, gain):
    inverse, scaled, _ = normed(rows, gain)
    weighted = upstream * gain
    through = inverse * (weighted - scaled * jnp.mean(weighted * scaled, -1, keepdims=True))
    return through, jnp.sum(upstream * scaled, 0, keepdims=True)


def turn(part, mid, gain, cotangent, rows, grads, d_gate, d_up, hidden, weights):
    n = 3 * PACK
    count = 8 * ROWS

    def kernel(
        part_ref, mid_ref, gain_ref, cot_ref, rows_hbm, grads_hbm, gate_hbm, up_hbm, hid_hbm, weights_hbm,
        grad_ref, mid_rows_ref, feed_ref, sum_a, sum_b, out_hbm,
        own, rows_ref, grads_ref, gate_ref, up_ref, hid_ref, down_ref, out_ref, *rest,
    ):
        first, room, (out_sems, in_sems) = rest[:4], rest[4:9], rest[9:]
        spot, post = Spot(), Post(out_sems, in_sems)
        loads = load(
            post,
            [(gate_hbm, gate_ref), (up_hbm, up_ref), (rows_hbm, rows_ref), (hid_hbm, hid_ref), (grads_hbm, grads_ref)]
            + [(weights_hbm.at[:, pl.ds(2 * PACK, PACK)], down_ref)],
        )
        greet(spot, row_peers(spot) + y_peers(spot), 5, **collect_peers(spot))

        def main():
            yield from scatter_rows(spot, post, part_ref, *first)
            feed_ref[...] = jnp.zeros_like(feed_ref)

            def body(strip):
                upstream = row_sum(spot, first[0], first[1], first[3], strip)
                through, feed = norm_back(upstream, mid_ref[strip, :], wide_gain(gain_ref))
                grad = cot_ref[strip, :].astype(F32) + through
                grad_ref[strip, :] = grad
                own[strip, :] = grad.astype(BF16)
                feed_ref[...] += feed

            in_strips(ROWS, body)
            yield from gather_rows(spot, post, own, mid_rows_ref)

        def gradients():
            for copy in loads:
                copy.wait()
            groups = [(rows_ref, (gate_ref, up_ref)), (grads_ref, (hid_ref,))]
            yield from Gradients(spot, post, groups, *room, sum_a, sum_b).steps()

        def output():
            def step(i, carry):
                rows = pl.ds(pl.multiple_of(i * 256, 256), 256)
                out_ref[rows, :] = dot(hid_ref[rows, :], down_ref[...], 1, 1).astype(BF16)
                return carry

            lax.fori_loop(0, count // 256, step, 0)
            store = post.local(out_ref, out_hbm)
            store.start()
            yield
            store.wait()

        play("mgmgmgmggomgmmgggggo", m=main(), g=gradients(), o=output())

    half = shape((4, 64, n), BF16)
    wide = pltpu.VMEM((count, WIDE), BF16)
    narrow = pltpu.VMEM((count, PACK), BF16)
    return moving(
        kernel,
        "turn",
        (
            shape((ROWS, WIDE), F32),
            shape((8, ROWS, WIDE), BF16),
            shape((1, WIDE), F32),
            half,
            half,
            shape((count, WIDE), BF16),
        ),
        (part, mid, gain, cotangent, rows, grads, d_gate, d_up, hidden, weights),
        [ANY, INSIDE, INSIDE, INSIDE] + [ANY] * 6,
        (INSIDE, ANY, INSIDE, INSIDE, INSIDE, ANY),
        [pltpu.VMEM((ROWS, WIDE), BF16), wide, wide, narrow, narrow, narrow, pltpu.VMEM((WIDE, PACK), BF16), wide]
        + scatter_scratch()
        + gradient_scratch(n)
        + sems(100),
        3,
    )


def leave(part, tokens, gain, grad_mid, feed_part, rows, d_qkv, mid_rows, mixed, sum_two):
    n_qkv, n_out = d_qkv.shape[1], mixed.shape[1]
    n, n_two = n_qkv + n_out, sum_two.shape[-1]
    count = 8 * ROWS

    def kernel(
        part_ref, tokens_ref, gain_ref, grad_ref, feed_ref, rows_hbm, d_hbm, mid_hbm, mixed_hbm, sum_two_ref,
        token_ref, gains_ref, weight_ref, high_ref,
        norm_part, parts, from_y, over_y, from_chip, over_fsdp, from_tp, rows_ref, d_ref, mid_ref, mixed_ref, *rest,
    ):
        first, room, (sum_a, sum_b), last, (out_sems, in_sems) = rest[:4], rest[4:9], rest[9:11], rest[11:17], rest[17:]
        spot, post = Spot(), Post(out_sems, in_sems)
        loads = load(post, [(d_hbm, d_ref), (rows_hbm, rows_ref), (mixed_hbm, mixed_ref), (mid_hbm, mid_ref)])
        greet(spot, row_peers(spot) + y_peers(spot) + gain_sources(spot), 5 + 13, **collect_peers(spot))

        def main():
            yield from scatter_rows(spot, post, part_ref, *first)
            norm_part[...] = jnp.zeros_like(norm_part)

            def body(strip):
                upstream = row_sum(spot, first[0], first[1], first[3], strip)
                through, norm = norm_back(upstream, tokens_ref[strip, :].astype(F32), wide_gain(gain_ref))
                token_ref[strip, :] = grad_ref[strip, :] + through
                norm_part[...] += norm

            in_strips(ROWS, body)
            parts[...] = jnp.zeros_like(parts)
            for f in range(16):
                parts[f, 0:1, :] = norm_part[:, f * 128 : (f + 1) * 128]
                parts[f, 1:2, :] = feed_ref[:, f * 128 : (f + 1) * 128]
            yield from sum_gains(spot, post, parts, gains_ref, from_y, over_y, from_chip, over_fsdp, from_tp)

        def gradients():
            for copy in loads:
                copy.wait()
            groups = [(rows_ref, (d_ref,)), (mid_ref, (mixed_ref,))]
            yield from Gradients(spot, post, groups, *room, sum_a, sum_b).steps()
            yield from together(
                scatter_low(spot, post, sum_a, strip_writer(weight_ref), *last[:2]),
                scatter_high(spot, post, sum_b, strip_writer(weight_ref, 64), *last[2:4]),
            )

        play(
            "mbgmgbmggggmgmgmggmgbgg",
            m=main(),
            g=gradients(),
            b=scatter_high(spot, post, sum_two_ref, strip_writer(high_ref), *last[4:]),
        )

    small = (8, 128)
    full_rows = pltpu.VMEM((count, WIDE), BF16)
    return moving(
        kernel,
        "leave",
        (shape((ROWS, WIDE), F32), shape(small, F32), shape((ROWS, n), F32), shape((64, n_two), F32)),
        (part, tokens, gain, grad_mid, feed_part, rows, d_qkv, mid_rows, mixed, sum_two),
        [ANY, INSIDE, INSIDE, INSIDE, INSIDE] + [ANY] * 4 + [INSIDE],
        (INSIDE,) * 4,
        [pltpu.VMEM((1, WIDE), F32), pltpu.VMEM((16,) + small, F32)]
        + [pltpu.VMEM(dims + small, F32) for dims in ((3, 4), (4,), (3,), (), (7,))]
        + [full_rows, pltpu.VMEM((count, n_qkv), BF16), full_rows, pltpu.VMEM((count, n_out), BF16)]
        + scatter_scratch()
        + gradient_scratch(n)
        + [pltpu.VMEM((4, 64, n), BF16)] * 2
        + low_scratch(n)
        + high_scratch(n)
        + high_scratch(n_two)
        + sems(120),
        4,
    )


def dot(a, b, da=1, db=0):
    return lax.dot_general(a, b, (((da,), (db,)), ((), ())), preferred_element_type=F32)


def plain(kernel, name, grid, inputs, in_specs, outs, out_specs, scratch=()):
    return pl.pallas_call(
        kernel,
        name=name,
        out_shape=outs,
        grid=grid,
        in_specs=in_specs,
        out_specs=out_specs,
        scratch_shapes=list(scratch),
        compiler_params=pltpu.CompilerParams(vmem_limit_bytes=VMEM),
    )(*inputs)


def by_rows(n, width, column=0):
    return pl.BlockSpec((n, width), lambda i: (i, column))


def whole(dims, *index):
    at = index or (0,) * len(dims)
    return pl.BlockSpec(dims, lambda i: at)


def project(rows, weights, cosine, sine):
    step = 256

    def kernel(rows_ref, w_ref, cos_ref, sin_ref, q_ref, kv_ref):
        out = dot(rows_ref[...], w_ref[...])
        cos, sin = cos_ref[...], sin_ref[...]
        for head in range(4):
            u = out[:, head * HD : (head + 1) * HD]
            turned = (u * cos + pltpu.roll(u, HD // 2, 1) * sin).astype(BF16)
            if head < 2:
                q_ref[:, head * HD : (head + 1) * HD] = turned
            else:
                kv_ref[head - 2, 0] = turned
                kv_ref[head - 2, 1] = out[:, (head + 2) * HD : (head + 3) * HD].astype(BF16)

    out = shape((8 * ROWS, 2 * HD), BF16)
    return plain(
        kernel,
        "project",
        (8 * ROWS // step,),
        (rows, weights, cosine, sine),
        [by_rows(step, WIDE), whole((WIDE, PACK)), by_rows(step, HD), by_rows(step, HD)],
        (out, shape((2, 2, 8 * ROWS, HD), BF16)),
        (by_rows(step, 2 * HD), pl.BlockSpec((2, 2, step, HD), lambda i: (0, 0, i, 0))),
    )


def partial_rows(pairs, name, extra=None):
    step = 256
    sets = [pairs] + ([extra] if extra else [])
    flat = [pair for group in sets for pair in group]

    def kernel(*refs):
        values, outs = refs[: 2 * len(flat)], refs[2 * len(flat) :]
        at = 0
        for group, out in zip(sets, outs):
            total = None
            for _ in group:
                term = dot(values[at][...], values[at + 1][...], 1, 1)
                total = term if total is None else total + term
                at += 2
            out[...] = total.astype(BF16)

    inputs, specs = [], []
    for a, b, width, column in flat:
        inputs += [a, b]
        specs += [by_rows(step, width), whole((WIDE, width), 0, column)]
    out = tuple(shape((8 * ROWS, WIDE), BF16) for _ in sets)
    return plain(kernel, name, (8 * ROWS // step,), inputs, specs, out, tuple(by_rows(step, WIDE) for _ in sets))


def feed_forward(rows, grads, weights):
    step = 256

    def kernel(rows_ref, grads_ref, g_ref, u_ref, d_ref, hid_ref, dgate_ref, dup_ref):
        gate = dot(rows_ref[...], g_ref[...])
        up = dot(rows_ref[...], u_ref[...])
        d_hid = dot(grads_ref[...], d_ref[...])
        sigma = 1.0 / (1.0 + jnp.exp(-gate))
        silu = gate * sigma
        hid_ref[...] = (silu * up).astype(BF16)
        dup_ref[...] = (d_hid * silu).astype(BF16)
        dgate_ref[...] = (d_hid * up * sigma * (1.0 + gate * (1.0 - sigma))).astype(BF16)

    out = shape((8 * ROWS, PACK), BF16)
    return plain(
        kernel,
        "feed_forward",
        (8 * ROWS // step,),
        (rows, grads, weights, weights, weights),
        [by_rows(step, WIDE)] * 2 + [whole((WIDE, PACK), 0, i) for i in range(3)],
        (out,) * 3,
        (by_rows(step, PACK),) * 3,
    )


def settle(layer, token_grad, gains, attention, low, high, wide):
    def kernel(
        layer_ref, token_ref, gains_ref, attention_ref, low_ref, high_ref,
        layer_out, token_out, norm_out, feed_out, query_out, key_out, value_out, out_out, gate_out, up_out, down_out,
    ):
        layer_out[...] = layer_ref[...]
        token_out[...] = token_ref[...]
        norm_out[...] = gains_ref[0:1, :]
        feed_out[...] = gains_ref[1:2, :]
        for i, out in enumerate((query_out, key_out, value_out)):
            out[...] = attention_ref[:, i * 2 * HD : (i + 1) * 2 * HD]
        out_out[...] = attention_ref[:, PACK:].T
        for i, out in enumerate((gate_out, up_out, down_out)):
            columns = slice(i * PACK, (i + 1) * PACK)
            out[...] = jnp.concatenate([low_ref[:, columns], high_ref[:, columns]], 0).T[:wide]

    vector = shape((1, 128), F32)
    square = shape((ROWS, 2 * HD), F32)
    tall = shape((wide, ROWS), F32)
    return pl.pallas_call(
        kernel,
        name="settle",
        out_shape=(shape(layer.shape, layer.dtype), shape(token_grad.shape, F32), vector, vector, square, square, square)
        + (shape((2 * HD, ROWS), F32), tall, tall, tall),
        in_specs=[INSIDE] * 6,
        out_specs=(INSIDE,) * 11,
        compiler_params=pltpu.CompilerParams(vmem_limit_bytes=VMEM),
    )(layer, token_grad, gains, attention, low, high)


def back_to_heads(rows, weights):
    step = 256

    def kernel(rows_ref, w_ref, out_ref):
        out_ref[...] = dot(rows_ref[...], w_ref[...]).astype(BF16)

    return plain(
        kernel,
        "back_to_heads",
        (8 * ROWS // step,),
        (rows, weights),
        [by_rows(step, WIDE), whole((WIDE, 2 * HD))],
        shape((8 * ROWS, 2 * HD), BF16),
        by_rows(step, 2 * HD),
    )


TILE = 256
CHUNK = 512


def place_of(start, count, xh, axis):
    dims = (count, 1) if axis == 0 else (1, count)
    j = lax.broadcasted_iota(jnp.int32, dims, axis)
    return 2 * (j + start) - lax.rem(j + start, ROWS) + xh * ROWS


SPANS = ((0, 512, False), (512, 256, True))
LAST = (768, 256, True)


def scores_of(keys, q, span, q_pos, prefix, xh):
    start, count, masked = span
    scores = dot(keys, q, 1, 1) * (SCALE * LOG2E)
    if masked:
        k_pos = place_of(start, count, xh, 0)
        scores = jnp.where(jnp.logical_or(k_pos <= q_pos, k_pos < prefix), scores, -1e30)
    return scores


def tile_at(i):
    head, tile = lax.div(i, 4), lax.rem(i, 4)
    return head, tile, pl.ds(pl.multiple_of(head * HD, HD), HD), pl.ds(pl.multiple_of(tile * TILE, TILE), TILE)


def exchange(post, pairs, device):
    copies = [post.copy(src, dst, device) for src, dst in pairs]
    for copy in copies:
        copy.start()
    yield
    for copy in copies:
        copy.wait_recv()
        yield
    for copy in copies:
        copy.wait_send()


def prefix_of(prefixes_ref):
    return prefixes_ref[lax.div(lax.axis_index("fsdp"), 2)]


def attend(prefixes, queries, here, cotangent, row_out, second):
    n, n_two = row_out.shape[-1], second.shape[-1]

    def kernel(
        prefixes_ref, q_ref, here_ref, cot_ref, row_ref, second_ref, o_ref, lse_ref, there_ref, grads_ref, out_ref, stage_ref,
        top_ref, sum_ref, acc_ref, out_sems, in_sems,
    ):
        prefix = prefix_of(prefixes_ref)
        spot, post = Spot(), Post(out_sems, in_sems)
        partner = spot.at(dx=2)
        greet(spot, row_peers(spot) + y_peers(spot) + [partner], 6)

        def sweep(side, begin, end):
            keys_ref = there_ref if side else here_ref
            xh = 1 - spot.xh if side else spot.xh

            def step(i, carry):
                head, tile, cols, rows = tile_at(i)
                q = q_ref[rows, cols]
                q_pos = place_of(tile * TILE, TILE, spot.xh, 1)
                one = pl.ds(i, 1)

                def chunk(span, first):
                    keys = pl.ds(span[0], span[1])
                    scores = scores_of(keys_ref[head, 0, keys, :], q, span, q_pos, prefix, xh)
                    top = jnp.max(scores, 0, keepdims=True)
                    if not first:
                        before = top_ref[one, :]
                        top = jnp.maximum(top, before)
                    raised = jnp.exp2(scores - top)
                    total = jnp.sum(raised, 0, keepdims=True)
                    mixed = dot(keys_ref[head, 1, keys, :], raised.astype(BF16), 0, 0)
                    if not first:
                        fade = jnp.exp2(before - top)
                        total = total + sum_ref[one, :] * fade
                        mixed = mixed + acc_ref[i] * fade
                    top_ref[one, :] = top
                    sum_ref[one, :] = total
                    acc_ref[i] = mixed

                for number, span in enumerate(SPANS):
                    chunk(span, side == 0 and number == 0)

                @pl.when(tile == 3)
                def _():
                    chunk(LAST, False)

                if side == 1:
                    total = sum_ref[one, :]
                    o_ref[rows, cols] = (acc_ref[i] / total).T.astype(BF16)
                    lse_ref[one, :] = top_ref[one, :] + jnp.log2(total)
                return carry

            lax.fori_loop(begin, end, step, 0)

        def compute():
            sweep(0, 0, 8)
            yield
            sweep(1, 0, 4)
            yield
            sweep(1, 4, 8)

        play(
            "vesfcvsfecvsfecse",
            v=y_gather(spot, post, row_ref, lambda y: out_ref.at[y]),
            f=y_gather(spot, post, second_ref, lambda y: stage_ref.at[y]),
            e=exchange(post, [(here_ref.at[head], there_ref.at[head]) for head in range(2)], partner),
            s=gather_rows(spot, post, cot_ref, grads_ref),
            c=compute(),
        )

    return moving(
        kernel,
        "attend",
        (
            shape((8 * ROWS, 2 * HD), BF16),
            shape((8, TILE), F32),
            shape(here.shape, BF16),
            shape((8, ROWS, WIDE), BF16),
            shape((4, 4, ROWS, n), BF16),
            shape((4, 64, n_two), BF16),
        ),
        (prefixes, queries, here, cotangent, row_out, second),
        [pl.BlockSpec(memory_space=pltpu.SMEM)] + [INSIDE] * 5,
        (INSIDE, INSIDE, INSIDE, ANY, ANY, INSIDE),
        [pltpu.VMEM((8, TILE), F32), pltpu.VMEM((8, TILE), F32), pltpu.VMEM((8, HD, TILE), F32)] + sems(60),
        5,
    )


def attend_back(prefixes, queries, here, there, grads, mixed, lse, cosine, sine, out_part, mid, sum_a):
    n = sum_a.shape[-1]

    def kernel(
        prefixes_ref, q_ref, here_ref, there_ref, g_ref, o_ref, lse_ref, cos_ref, sin_ref, part_ref, mid_ref, sum_a_ref,
        d_ref, layer_ref, weight_ref, delta_ref, dq_ref, acc_ref, near_ref, away_ref, land_ref, *rest,
    ):
        second, last, (out_sems, in_sems) = rest[:4], rest[4:6], rest[6:]
        prefix = prefix_of(prefixes_ref)
        spot, post = Spot(), Post(out_sems, in_sems)
        partner = spot.at(dx=2)
        greet(spot, row_peers(spot) + y_peers(spot) + [partner], 6)

        def sweep(head, side, keys_ref, into):
            xh = spot.xh if side == 0 else 1 - spot.xh
            cols = pl.ds(head * HD, HD)
            into[...] = jnp.zeros_like(into)

            def step(tile, carry):
                i = head * 4 + tile
                rows = pl.ds(pl.multiple_of(tile * TILE, TILE), TILE)
                q, g = q_ref[rows, cols], g_ref[rows, cols]
                q_pos = place_of(tile * TILE, TILE, spot.xh, 1)
                if side == 1:
                    product = g.astype(F32) * o_ref[rows, cols].astype(F32)
                    delta_ref[pl.ds(i, 1), :] = jnp.sum(product.T, 0, keepdims=True)
                level, offset = lse_ref[pl.ds(i, 1), :], delta_ref[pl.ds(i, 1), :]

                def chunk(span, first):
                    span_rows = pl.ds(span[0], span[1])
                    keys = keys_ref[head, 0, span_rows, :]
                    probs = jnp.exp2(scores_of(keys, q, span, q_pos, prefix, xh) - level)
                    d_probs = dot(keys_ref[head, 1, span_rows, :], g, 1, 1)
                    d_scores = (probs * (d_probs - offset)).astype(BF16)
                    into[0, span_rows, :] += dot(d_scores, q)
                    into[1, span_rows, :] += dot(probs.astype(BF16), g)
                    d_query = dot(d_scores, keys, 0, 0)
                    dq_ref[i] = d_query if first else dq_ref[i] + d_query

                for number, span in enumerate(SPANS):
                    chunk(span, side == 1 and number == 0)

                @pl.when(tile == 3)
                def _():
                    chunk(LAST, False)

                if side == 0:
                    u = dq_ref[i] * SCALE
                    d_ref[rows, cols] = (u * cos_ref[rows, :] - pltpu.roll(u, HD // 2, 1) * sin_ref[rows, :]).astype(BF16)
                return carry

            lax.fori_loop(0, 4, step, 0)

        def compute():
            copies = []
            for head in range(2):
                sweep(head, 1, there_ref, acc_ref)
                away_ref[head] = acc_ref[...].astype(BF16)
                copies.append(post.copy(away_ref.at[head], land_ref.at[head], partner))
                copies[-1].start()
                yield
            for head in range(2):
                sweep(head, 0, here_ref, near_ref.at[head])
                yield
            for head in range(2):
                copies[head].wait_recv()
                cols = pl.ds(2 * HD + head * HD, HD)

                def finish(i, carry, head=head):
                    rows = pl.ds(pl.multiple_of(i * 128, 128), 128)
                    u = (near_ref[head, 0, rows, :] + land_ref[head, 0, rows, :].astype(F32)) * SCALE
                    back = u * cos_ref[rows, :] - pltpu.roll(u, HD // 2, 1) * sin_ref[rows, :]
                    d_ref[rows, pl.ds(2 * HD + head * HD, HD)] = back.astype(BF16)
                    v = near_ref[head, 1, rows, :] + land_ref[head, 1, rows, :].astype(F32)
                    d_ref[rows, pl.ds(4 * HD + head * HD, HD)] = v.astype(BF16)
                    return carry

                lax.fori_loop(0, 8, finish, 0)
            for copy in copies:
                copy.wait_send()

        def output():
            yield from scatter_rows(spot, post, part_ref, *second)

            def body(strip):
                layer_ref[strip, :] = (mid_ref[strip, :] + row_sum(spot, second[0], second[1], second[3], strip)).astype(BF16)

            in_strips(ROWS, body)

        play(
            "owcocwocowc",
            c=compute(),
            o=output(),
            w=scatter_low(spot, post, sum_a_ref, strip_writer(weight_ref), *last),
        )

    pair = (2, 8 * ROWS, HD)
    return moving(
        kernel,
        "attend_back",
        (shape((8 * ROWS, PACK), BF16), shape((ROWS, WIDE), BF16), shape((64, n), F32)),
        (prefixes, queries, here, there, grads, mixed, lse, cosine, sine, out_part, mid, sum_a),
        [pl.BlockSpec(memory_space=pltpu.SMEM)] + [INSIDE] * 8 + [ANY, INSIDE, INSIDE],
        (INSIDE,) * 3,
        [
            pltpu.VMEM((8, TILE), F32),
            pltpu.VMEM((8, TILE, HD), F32),
            pltpu.VMEM(pair, F32),
            pltpu.VMEM((2,) + pair, F32),
            pltpu.VMEM((2,) + pair, BF16),
            pltpu.VMEM((2,) + pair, BF16),
        ]
        + scatter_scratch()
        + low_scratch(n)
        + sems(64),
        6,
    )


def on_device(
    tokens,
    prefixes,
    norm_gain,
    query_weight,
    key_weight,
    value_weight,
    output_weight,
    feed_gain,
    gate_weight,
    up_weight,
    down_weight,
    cotangent,
):
    rows_one, full_one, row_out, row_two, second, cosine, sine = enter(
        tokens, norm_gain, query_weight, key_weight, value_weight, output_weight, gate_weight.T, up_weight.T, down_weight
    )
    rows_one = rows_one.reshape(-1, WIDE)
    full_one = full_one.reshape(WIDE, -1)
    queries, here = project(rows_one, full_one, cosine, sine)
    attended, lse, there, grad_rows, full_out, stage_two = attend(prefixes, queries, here, cotangent, row_out, second)
    full_out = full_out.reshape(WIDE, -1)
    (part,) = partial_rows([(attended, full_out, 2 * HD, 0)], "attention_out")
    mid, rows_two, full_two = middle(part.reshape(8, ROWS, WIDE), tokens, feed_gain, row_two, stage_two)
    rows_two, grad_rows, full_two = (a.reshape(-1, a.shape[-1]) for a in (rows_two, grad_rows, full_two.reshape(WIDE, -1)))
    hidden, d_gate, d_up = feed_forward(rows_two, grad_rows, full_two)
    (part,) = partial_rows([(d_gate, full_two, PACK, 0), (d_up, full_two, PACK, 1)], "feed_back")
    grad_mid, mid_rows, feed_part, sum_a, sum_b, part_out = turn(
        part.reshape(8, ROWS, WIDE), mid, feed_gain, cotangent, rows_two, grad_rows, d_gate, d_up, hidden, full_two
    )
    mid_rows = mid_rows.reshape(-1, WIDE)
    grad_mixed = back_to_heads(mid_rows, full_out)
    d_qkv, layer_output, low = attend_back(
        prefixes, queries, here, there, grad_mixed, attended, lse, cosine, sine, part_out.reshape(8, ROWS, WIDE), mid, sum_a
    )
    (part,) = partial_rows([(d_qkv, full_one, PACK, 0)], "attention_back")
    token_grad, gains, attention, high = leave(
        part.reshape(8, ROWS, WIDE), tokens, norm_gain, grad_mid, feed_part, rows_one, d_qkv, mid_rows, attended, sum_b
    )
    layer_output, token_grad, norm_grad, feed_grad, *grads = settle(
        layer_output, token_grad, gains, attention, low, high, gate_weight.shape[1]
    )
    query_grad, key_grad, value_grad, output_grad, gate_grad, up_grad, down_grad = grads
    return (
        layer_output,
        token_grad,
        norm_grad[0],
        query_grad,
        key_grad,
        value_grad,
        output_grad,
        feed_grad[0],
        gate_grad.T,
        up_grad.T,
        down_grad,
    )


def solution(mesh):
    rows = P(("fsdp", "tp"), None)
    wide = P("fsdp", "tp")
    tall = P("tp", "fsdp")
    return jax.shard_map(
        on_device,
        mesh=mesh,
        in_specs=(rows, P(), P(), wide, wide, wide, tall, P(), wide, wide, tall, rows),
        out_specs=(rows, rows, P("fsdp"), wide, wide, wide, tall, P("fsdp"), wide, wide, tall),
        check_vma=False,
    )
```

time: 391 us -> 342 us (0.87)
  Pallas kernels: 367 us -> 340 us
  local copies, waits for them, and re-layouts: 11.1 us -> 0 us
  other arithmetic: 11 us -> 0 us
    pallas_call x6, Pallas kernels: 314 us -> 283 us  [moving(): pl.pallas_call(kernel, name=name, out_shape=outs, in_specs=in_specs, out_...]
    unnamed x13 -> x0, local copies, waits for them, and re-layouts: 6.8 us -> none
    concatenate x3 -> x0, other arithmetic: 4.04 us -> none  [the longest x1 1.59 us: on_device(): shard_one = jnp.concatenate([query_weight, key_weight, value_weight], 1)]
where the time goes in v3:
time: 342 us; the launch traced here: 341 us
  Pallas kernels  340 us (99%)
    pallas_call x6, Pallas kernels, moving(): pl.pallas_call(kernel, name=name, out_shape=outs, in_specs=in_specs, out_...  283 us
    pallas_call x6, Pallas kernels, plain(): pl.pallas_call(kernel, name=name, out_shape=outs, grid=grid, in_specs=in_...  53.1 us

profile of v3, /device:TPU:1, one launch (start us, length us, event | category | flops | bytes accessed | tf_op | source)
XLA Modules:
  0.0 341.1 jit_solution(14676133841674648928)
XLA Ops:
  0.6 44.8 %enter.1 = (bf16[8,128,2048]{2,1,0:T(8,128)(2,1)}, bf16[4,4,2,64,768]{4,3,2,1,0:T(8,128)(2,1)}, bf16[4,128,256]{2,1,0:T(8,128)(2,1)}, bf16[4,64,2304]{2,1,0:T(8,...) custom-call(bf16[128,2048]{1,0:T(8,128)(2,1)} %tokens_ref.5, ...), custom_call_target="tpu_custom_call" | custom-call | tf_op jit(solution)/shard_map/enter/pallas_call | solution.py:663
  45.5 7.7 %project.1 = (bf16[1024,256]{1,0:T(8,128)(2,1)}, bf16[2,2,1024,128]{3,2,1,0:T(8,128)(2,1)}) custom-call(bf16[1024,2048]{1,0:T(8,128)(2,1)} %bitcast.23, bf16[2048,768]{1,0:T(8,128)(2,1)} %bitcast.34, f32[1024,128]{1,0:T(8,128)} %get-tuple-element.58.cos_ref, f32[1024,128]{1,0:T(8,128)} %get-tuple-element.59.sin_ref), custom_call_target="tpu_custom_call" | custom-call | tf_op jit(solution)/shard_map/project/pallas_call | solution.py:963
  53.2 34.3 %attend.1 = (bf16[1024,256]{1,0:T(8,128)(2,1)}, f32[8,256]{1,0:T(8,128)}, bf16[2,2,1024,128]{3,2,1,0:T(8,128)(2,1)}, bf16[8,128,2048]{2,1,0:T(8,128)(2,1)}, bf16...) custom-call(s32[8]{0:T(128)} %prefixes_ref.3, bf16[1024,256]{1,0:T(8,128)(2,1)} %get-tuple-element.60.q_ref, ...), custom_call_target="tpu_custom_call" | custom-call | tf_op jit(solution)/shard_map/attend/pallas_call | solution.py:663
  87.6 5.1 %attention_out.1 = bf16[1024,2048]{1,0:T(8,128)(2,1)} custom-call(bf16[1024,256]{1,0:T(8,128)(2,1)} %get-tuple-element.65.refs_0_.o_ref.mixed_hbm, bf16[2048,256]{1,0:T(8,128)(2,1)} %bitcast.37), custom_call_target="tpu_custom_call" | custom-call | tf_op jit(solution)/shard_map/attention_out/pallas_call | solution.py:963
  92.7 50.6 %middle.1 = (f32[128,2048]{1,0:T(8,128)}, bf16[8,128,2048]{2,1,0:T(8,128)(2,1)}, bf16[4,4,2,64,2304]{4,3,2,1,0:T(8,128)(2,1)}) custom-call(bf16[8,128,2048]{2,1,0:T(8,128)(2,1)} %bitcast.28, bf16[128,2048]{1,0:T(8,128)(2,1)} %tokens_ref.5, bf16[2048]{0:T(1024)(128)(2,1)} %gain_ref.6, bf16[4,64,2304]{2,1,0:T(8,128)(2,1)} %get-tuple-element.67.row_ref, ...), custom_call_target="tpu_custom_call" | custom-call | tf_op jit(solution)/shard_map/middle/pallas_call | solution.py:663
  143.3 16.3 %feed_forward.1 = (bf16[1024,768]{1,0:T(8,128)(2,1)}, bf16[1024,768]{1,0:T(8,128)(2,1)}, bf16[1024,768]{1,0:T(8,128)(2,1)}) custom-call(bf16[1024,2048]{1,0:T(8,128)(2,1)} %bitcast.31, bf16[1024,2048]{1,0:T(8,128)(2,1)} %bitcast.29, bf16[2048,2304]{1,0:T(8,128)(2,1)} %bitcast.17, bf16[2048,2304]{1,0:T(8,128)(2,1)} %bitcast.18, bf16[2048,2304]{1,0:T(8,128)(2,1)} %bitcast.19), custom_call_target="tpu_custom_call" | custom-call | tf_op jit(solution)/shard_map/feed_forward/pallas_call | solution.py:963
  159.6 11.5 %feed_back.1 = bf16[1024,2048]{1,0:T(8,128)(2,1)} custom-call(bf16[1024,768]{1,0:T(8,128)(2,1)} %get-tuple-element.72.refs_0_.gate_hbm, bf16[2048,2304]{1,0:T(8,128)(2,1)} %bitcast.20, bf16[1024,768]{1,0:T(8,128)(2,1)} %get-tuple-element.73.refs_2_.up_hbm, bf16[2048,2304]{1,0:T(8,128)(2,1)} %bitcast.21), custom_call_target="tpu_custom_call" | custom-call | tf_op jit(solution)/shard_map/feed_back/pallas_call | solution.py:963
  171.1 61.0 %turn.1 = (f32[128,2048]{1,0:T(8,128)}, bf16[8,128,2048]{2,1,0:T(8,128)(2,1)}, f32[1,2048]{1,0:T(1,128)}, bf16[4,64,2304]{2,1,0:T(8,128)(2,1)}, bf16[4,64,2304]{...) custom-call(bf16[8,128,2048]{2,1,0:T(8,128)(2,1)} %bitcast.33, f32[128,2048]{1,0:T(8,128)} %get-tuple-element.74.mid_ref, ...), custom_call_target="tpu_custom_call" | custom-call | tf_op jit(solution)/shard_map/turn/pallas_call | solution.py:663
  232.1 5.0 %back_to_heads.1.g_ref = bf16[1024,256]{1,0:T(8,128)(2,1)} custom-call(bf16[1024,2048]{1,0:T(8,128)(2,1)} %bitcast.25, bf16[2048,256]{1,0:T(8,128)(2,1)} %bitcast.38), custom_call_target="tpu_custom_call" | custom-call | tf_op jit(solution)/shard_map/back_to_heads/pallas_call | solution.py:963
  237.1 38.0 %attend_back.1 = (bf16[1024,768]{1,0:T(8,128)(2,1)}, bf16[128,2048]{1,0:T(8,128)(2,1)}, f32[64,2304]{1,0:T(8,128)}) custom-call(s32[8]{0:T(128)} %prefixes_ref.3, bf16[1024,256]{1,0:T(8,128)(2,1)} %get-tuple-element.60.q_ref, bf16[2,2,1024,128]{3,2,1,0:T(8,128)(2,1)} %get-tuple-element.61.here_ref, bf16[2,2,1024,128]{3,2,1,0:T(8,128)(2,1)} %get-tuple-element.64.there_ref, ...), custom_call_target="tpu_custom_call" | custom-call | tf_op jit(solution)/shard_map/attend_back/pallas_call | solution.py:663
  275.1 7.4 %attention_back.1 = bf16[1024,2048]{1,0:T(8,128)(2,1)} custom-call(bf16[1024,768]{1,0:T(8,128)(2,1)} %get-tuple-element.81.refs_0_.d_hbm, bf16[2048,768]{1,0:T(8,128)(2,1)} %bitcast.35), custom_call_target="tpu_custom_call" | custom-call | tf_op jit(solution)/shard_map/attention_back/pallas_call | solution.py:963
  282.5 54.7 %leave.1 = (f32[128,2048]{1,0:T(8,128)}, f32[8,128]{1,0:T(8,128)}, f32[128,1024]{1,0:T(8,128)}, f32[64,2304]{1,0:T(8,128)}) custom-call(bf16[8,128,2048]{2,1,0:T(8,128)(2,1)} %bitcast.27, bf16[128,2048]{1,0:T(8,128)(2,1)} %tokens_ref.5, bf16[2048]{0:T(1024)(128)(2,1)} %gain_ref.7, f32[128,2048]{1,0:T(8,128)} %get-tuple-element.82.grad_ref, ...), custom_call_target="tpu_custom_call" | custom-call | tf_op jit(solution)/shard_map/leave/pallas_call | solution.py:663
  337.2 3.8 %settle.1 = (bf16[128,2048]{1,0:T(8,128)(2,1)}, f32[128,2048]{1,0:T(8,128)}, f32[1,128]{1,0:T(1,128)}, f32[1,128]{1,0:T(1,128)}, f32[128,256]{1,0:T(8,128)}, /*i...) custom-call(bf16[128,2048]{1,0:T(8,128)(2,1)} %get-tuple-element.80., ...), custom_call_target="tpu_custom_call" | custom-call | tf_op jit(solution)/shard_map/settle/pallas_call | solution.py:1079

commit v4 on v3

--- a/solution.py
+++ b/solution.py
@@ -20,7 +20,7 @@
 PACK = 768
 SCALE = 1.0 / math.sqrt(HD)
 LOG2E = 1.4426950408889634
-VMEM = 56 << 20
+VMEM = 60 << 20
 
 
 class Spot:
@@ -199,51 +199,80 @@
     in_strips(rows, body)
 
 
-def scatter_rows(spot, post, part, mine, land, far, gone):
+def row_products(spot, terms, outgoing, mine):
+    def make(z):
+        other, own = pl.ds(((1 - spot.c) * 4 + z) * ROWS, ROWS), pl.ds((spot.c * 4 + z) * ROWS, ROWS)
+
+        def step(i, carry):
+            columns = pl.ds(pl.multiple_of(i * 512, 512), 512)
+            total = None
+            for a, w, part in terms:
+                term = dot(jnp.concatenate([a[other, :], a[own, :]], 0), w[columns, part], 1, 1)
+                total = term if total is None else total + term
+            outgoing[z, :, columns] = total[:ROWS].astype(BF16)
+            mine[z, :, columns] = total[ROWS:].astype(BF16)
+            return carry
+
+        lax.fori_loop(0, WIDE // 512, step, 0)
+
+    return make
+
+
+def row_loads(spot, post, part, outgoing, mine):
+    def make(z):
+        copies = load(post, [(part.at[(1 - spot.c) * 4 + z], outgoing.at[z]), (part.at[spot.c * 4 + z], mine.at[z])])
+        for copy in copies:
+            copy.wait()
+
+    return make
+
+
+def scatter_rows(spot, post, make, outgoing, mine, land, far, gone):
     up, down, core = spot.at(dz=1), spot.at(dz=3), spot.other()
     half = ROWS // 2
     low, high = pl.ds(0, half), pl.ds(half, half)
     steps = [lax.rem(spot.z + dz, 4) for dz in (2, 3, 1, 0)]
-    to_core = [post.copy(part.at[(1 - spot.c) * 4 + s], land.at[s], core) for s in steps]
-    load = [post.local(part.at[spot.c * 4 + s], mine.at[s]) for s in steps]
-    for a, b in zip(to_core, load):
-        a.start()
-        b.start()
-    yield
+    distant, lower, upper, here = steps
+    to_core, others = [], []
+
+    def begin(k):
+        make(steps[k])
+        to_core.append(post.copy(outgoing.at[steps[k]], land.at[steps[k]], core))
+        to_core[k].start()
+
+    def pass_on(src, dst, device):
+        others.append(post.copy(src, dst, device))
+        others[-1].start()
+        return others[-1]
 
     def ready(k):
         to_core[k].wait_recv()
-        load[k].wait()
-
-    distant, lower, upper, here = steps
+        if k < 3:
+            add_into(mine.at[steps[k]], land.at[steps[k]])
+
+    begin(0)
+    begin(1)
     ready(0)
-    add_into(mine.at[distant], land.at[distant])
-    f_low = post.copy(mine.at[distant, low], far.at[low], down)
-    f_high = post.copy(mine.at[distant, high], far.at[high], up)
-    f_low.start()
-    f_high.start()
+    f_low = pass_on(mine.at[distant, low], far.at[low], down)
+    f_high = pass_on(mine.at[distant, high], far.at[high], up)
+    begin(2)
     ready(1)
-    add_into(mine.at[lower], land.at[lower])
-    d_high = post.copy(mine.at[lower, high], gone.at[0, high], down)
-    d_high.start()
+    gone_copies = [pass_on(mine.at[lower, high], gone.at[0, high], down)]
+    begin(3)
     ready(2)
-    add_into(mine.at[upper], land.at[upper])
-    u_low = post.copy(mine.at[upper, low], gone.at[1, low], up)
-    u_low.start()
+    gone_copies.append(pass_on(mine.at[upper, low], gone.at[1, low], up))
+    yield
     ready(3)
-    yield
     f_low.wait_recv()
     add_into(mine.at[lower], far, half)
-    d_low = post.copy(mine.at[lower, low], gone.at[0, low], down)
-    d_low.start()
+    gone_copies.append(pass_on(mine.at[lower, low], gone.at[0, low], down))
     f_high.wait_recv()
     add_into(mine.at[upper], far, half, half)
-    u_high = post.copy(mine.at[upper, high], gone.at[1, high], up)
-    u_high.start()
-    yield
-    for copy in (d_high, u_low, d_low, u_high):
+    gone_copies.append(pass_on(mine.at[upper, high], gone.at[1, high], up))
+    yield
+    for copy in gone_copies:
         copy.wait_recv()
-    for copy in to_core + [f_low, f_high, d_high, u_low, d_low, u_high]:
+    for copy in to_core + others:
         copy.wait_send()
 
 
@@ -255,6 +284,7 @@
 def scatter_scratch():
     block = (ROWS, WIDE)
     return [
+        pltpu.VMEM((4,) + block, BF16),
         pltpu.VMEM((4,) + block, BF16),
         pltpu.VMEM((4,) + block, BF16),
         pltpu.VMEM(block, BF16),
@@ -760,17 +790,23 @@
     )
 
 
-def middle(part, tokens, gain, row, stage):
+def middle(mixed, weights, tokens, gain, row, stage):
     n = row.shape[-1]
 
-    def kernel(part_ref, tokens_ref, gain_ref, row_ref, stage_ref, mid_ref, rows_ref, full_ref, own, *rest):
-        scatter, (out_sems, in_sems) = rest[:4], rest[4:]
-        mine, land, far, gone = scatter
+    def kernel(
+        mixed_hbm, weights_hbm, tokens_ref, gain_ref, row_ref, stage_ref, mid_ref, rows_ref, full_ref,
+        mixed_ref, weights_ref, own, *rest,
+    ):
+        (outgoing, mine, land, far, gone), (out_sems, in_sems) = rest[:5], rest[5:]
         spot, post = Spot(), Post(out_sems, in_sems)
+        loads = load(post, [(mixed_hbm, mixed_ref), (weights_hbm, weights_ref)])
         greet(spot, row_peers(spot) + y_peers(spot), 5, **gather_peers(spot))
 
         def main():
-            yield from scatter_rows(spot, post, part_ref, mine, land, far, gone)
+            for copy in loads:
+                copy.wait()
+            make = row_products(spot, [(mixed_ref, weights_ref, slice(None))], outgoing, mine)
+            yield from scatter_rows(spot, post, make, outgoing, mine, land, far, gone)
 
             def body(strip):
                 mid = tokens_ref[strip, :].astype(F32) + row_sum(spot, mine, land, gone, strip)
@@ -780,16 +816,18 @@
             in_strips(ROWS, body)
             yield from gather_rows(spot, post, own, rows_ref)
 
-        play("mwmmmwmmm", m=main(), w=gather_second(spot, post, row_ref, stage_ref, full_ref))
+        play("wmmmwmmm", m=main(), w=gather_second(spot, post, row_ref, stage_ref, full_ref))
 
     return moving(
         kernel,
         "middle",
         (shape((ROWS, WIDE), F32), shape((8, ROWS, WIDE), BF16), shape((4, 4, 2, 64, n), BF16)),
-        (part, tokens, gain, row, stage),
-        [ANY, INSIDE, INSIDE, INSIDE, INSIDE],
+        (mixed, weights, tokens, gain, row, stage),
+        [ANY, ANY, INSIDE, INSIDE, INSIDE, INSIDE],
         (INSIDE, ANY, ANY),
-        [pltpu.VMEM((ROWS, WIDE), BF16)] + scatter_scratch() + sems(64),
+        [pltpu.VMEM(mixed.shape, BF16), pltpu.VMEM(weights.shape, BF16), pltpu.VMEM((ROWS, WIDE), BF16)]
+        + scatter_scratch()
+        + sems(64),
         2,
     )
 
@@ -805,30 +843,34 @@
     return through, jnp.sum(upstream * scaled, 0, keepdims=True)
 
 
-def turn(part, mid, gain, cotangent, rows, grads, d_gate, d_up, hidden, weights):
+def turn(mid, gain, cotangent, rows, grads, d_gate, d_up, hidden, weights):
     n = 3 * PACK
     count = 8 * ROWS
 
     def kernel(
-        part_ref, mid_ref, gain_ref, cot_ref, rows_hbm, grads_hbm, gate_hbm, up_hbm, hid_hbm, weights_hbm,
+        mid_ref, gain_ref, cot_ref, rows_hbm, grads_hbm, gate_hbm, up_hbm, hid_hbm, weights_hbm,
         grad_ref, mid_rows_ref, feed_ref, sum_a, sum_b, out_hbm,
-        own, rows_ref, grads_ref, gate_ref, up_ref, hid_ref, down_ref, out_ref, *rest,
+        own, rows_ref, grads_ref, gate_ref, up_ref, hid_ref, weights_ref, out_ref, *rest,
     ):
-        first, room, (out_sems, in_sems) = rest[:4], rest[4:9], rest[9:]
+        (outgoing, mine, land, far, gone), room, (out_sems, in_sems) = rest[:5], rest[5:10], rest[10:]
         spot, post = Spot(), Post(out_sems, in_sems)
         loads = load(
             post,
-            [(gate_hbm, gate_ref), (up_hbm, up_ref), (rows_hbm, rows_ref), (hid_hbm, hid_ref), (grads_hbm, grads_ref)]
-            + [(weights_hbm.at[:, pl.ds(2 * PACK, PACK)], down_ref)],
+            [(gate_hbm, gate_ref), (up_hbm, up_ref), (weights_hbm, weights_ref)]
+            + [(rows_hbm, rows_ref), (hid_hbm, hid_ref), (grads_hbm, grads_ref)],
         )
         greet(spot, row_peers(spot) + y_peers(spot), 5, **collect_peers(spot))
 
         def main():
-            yield from scatter_rows(spot, post, part_ref, *first)
+            for copy in loads[:3]:
+                copy.wait()
+            terms = [(ref, weights_ref, slice(i * PACK, (i + 1) * PACK)) for i, ref in enumerate((gate_ref, up_ref))]
+            make = row_products(spot, terms, outgoing, mine)
+            yield from scatter_rows(spot, post, make, outgoing, mine, land, far, gone)
             feed_ref[...] = jnp.zeros_like(feed_ref)
 
             def body(strip):
-                upstream = row_sum(spot, first[0], first[1], first[3], strip)
+                upstream = row_sum(spot, mine, land, gone, strip)
                 through, feed = norm_back(upstream, mid_ref[strip, :], wide_gain(gain_ref))
                 grad = cot_ref[strip, :].astype(F32) + through
                 grad_ref[strip, :] = grad
@@ -839,7 +881,7 @@
             yield from gather_rows(spot, post, own, mid_rows_ref)
 
         def gradients():
-            for copy in loads:
+            for copy in loads[3:]:
                 copy.wait()
             groups = [(rows_ref, (gate_ref, up_ref)), (grads_ref, (hid_ref,))]
             yield from Gradients(spot, post, groups, *room, sum_a, sum_b).steps()
@@ -847,7 +889,7 @@
         def output():
             def step(i, carry):
                 rows = pl.ds(pl.multiple_of(i * 256, 256), 256)
-                out_ref[rows, :] = dot(hid_ref[rows, :], down_ref[...], 1, 1).astype(BF16)
+                out_ref[rows, :] = dot(hid_ref[rows, :], weights_ref[:, 2 * PACK :], 1, 1).astype(BF16)
                 return carry
 
             lax.fori_loop(0, count // 256, step, 0)
@@ -856,7 +898,7 @@
             yield
             store.wait()
 
-        play("mgmgmgmggomgmmgggggo", m=main(), g=gradients(), o=output())
+        play("mggmgmgogmmgggggo", m=main(), g=gradients(), o=output())
 
     half = shape((4, 64, n), BF16)
     wide = pltpu.VMEM((count, WIDE), BF16)
@@ -872,10 +914,10 @@
             half,
             shape((count, WIDE), BF16),
         ),
-        (part, mid, gain, cotangent, rows, grads, d_gate, d_up, hidden, weights),
-        [ANY, INSIDE, INSIDE, INSIDE] + [ANY] * 6,
+        (mid, gain, cotangent, rows, grads, d_gate, d_up, hidden, weights),
+        [INSIDE, INSIDE, INSIDE] + [ANY] * 6,
         (INSIDE, ANY, INSIDE, INSIDE, INSIDE, ANY),
-        [pltpu.VMEM((ROWS, WIDE), BF16), wide, wide, narrow, narrow, narrow, pltpu.VMEM((WIDE, PACK), BF16), wide]
+        [pltpu.VMEM((ROWS, WIDE), BF16), wide, wide, narrow, narrow, narrow, pltpu.VMEM((WIDE, n), BF16), wide]
         + scatter_scratch()
         + gradient_scratch(n)
         + sems(100),
@@ -883,27 +925,31 @@
     )
 
 
-def leave(part, tokens, gain, grad_mid, feed_part, rows, d_qkv, mid_rows, mixed, sum_two):
+def leave(weights, tokens, gain, grad_mid, feed_part, rows, d_qkv, mid_rows, mixed, sum_two):
     n_qkv, n_out = d_qkv.shape[1], mixed.shape[1]
     n, n_two = n_qkv + n_out, sum_two.shape[-1]
     count = 8 * ROWS
 
     def kernel(
-        part_ref, tokens_ref, gain_ref, grad_ref, feed_ref, rows_hbm, d_hbm, mid_hbm, mixed_hbm, sum_two_ref,
-        token_ref, gains_ref, weight_ref, high_ref,
-        norm_part, parts, from_y, over_y, from_chip, over_fsdp, from_tp, rows_ref, d_ref, mid_ref, mixed_ref, *rest,
+        weights_hbm, tokens_ref, gain_ref, grad_ref, feed_ref, rows_hbm, d_hbm, mid_hbm, mixed_hbm, sum_two_ref,
+        token_ref, gains_ref, weight_ref, high_ref, norm_part, parts, from_y, over_y, from_chip, over_fsdp, from_tp,
+        rows_ref, d_ref, mid_ref, mixed_ref, weights_ref, *rest,
     ):
-        first, room, (sum_a, sum_b), last, (out_sems, in_sems) = rest[:4], rest[4:9], rest[9:11], rest[11:17], rest[17:]
+        (outgoing, mine, land, far, gone), room, (sum_a, sum_b) = rest[:5], rest[5:10], rest[10:12]
+        last, (out_sems, in_sems) = rest[12:18], rest[18:]
         spot, post = Spot(), Post(out_sems, in_sems)
-        loads = load(post, [(d_hbm, d_ref), (rows_hbm, rows_ref), (mixed_hbm, mixed_ref), (mid_hbm, mid_ref)])
+        pairs = [(d_hbm, d_ref), (weights_hbm, weights_ref), (rows_hbm, rows_ref), (mixed_hbm, mixed_ref), (mid_hbm, mid_ref)]
+        loads = load(post, pairs)
         greet(spot, row_peers(spot) + y_peers(spot) + gain_sources(spot), 5 + 13, **collect_peers(spot))
 
         def main():
-            yield from scatter_rows(spot, post, part_ref, *first)
+            loads[1].wait()
+            make = row_products(spot, [(d_ref, weights_ref, slice(None))], outgoing, mine)
+            yield from scatter_rows(spot, post, make, outgoing, mine, land, far, gone)
             norm_part[...] = jnp.zeros_like(norm_part)
 
             def body(strip):
-                upstream = row_sum(spot, first[0], first[1], first[3], strip)
+                upstream = row_sum(spot, mine, land, gone, strip)
                 through, norm = norm_back(upstream, tokens_ref[strip, :].astype(F32), wide_gain(gain_ref))
                 token_ref[strip, :] = grad_ref[strip, :] + through
                 norm_part[...] += norm
@@ -916,7 +962,7 @@
             yield from sum_gains(spot, post, parts, gains_ref, from_y, over_y, from_chip, over_fsdp, from_tp)
 
         def gradients():
-            for copy in loads:
+            for copy in loads[:1] + loads[2:]:
                 copy.wait()
             groups = [(rows_ref, (d_ref,)), (mid_ref, (mixed_ref,))]
             yield from Gradients(spot, post, groups, *room, sum_a, sum_b).steps()
@@ -926,7 +972,7 @@
             )
 
         play(
-            "mbgmgbmggggmgmgmggmgbgg",
+            "bgmgbmgggmgggggmgmgmgbg",
             m=main(),
             g=gradients(),
             b=scatter_high(spot, post, sum_two_ref, strip_writer(high_ref), *last[4:]),
@@ -938,12 +984,13 @@
         kernel,
         "leave",
         (shape((ROWS, WIDE), F32), shape(small, F32), shape((ROWS, n), F32), shape((64, n_two), F32)),
-        (part, tokens, gain, grad_mid, feed_part, rows, d_qkv, mid_rows, mixed, sum_two),
+        (weights, tokens, gain, grad_mid, feed_part, rows, d_qkv, mid_rows, mixed, sum_two),
         [ANY, INSIDE, INSIDE, INSIDE, INSIDE] + [ANY] * 4 + [INSIDE],
         (INSIDE,) * 4,
         [pltpu.VMEM((1, WIDE), F32), pltpu.VMEM((16,) + small, F32)]
         + [pltpu.VMEM(dims + small, F32) for dims in ((3, 4), (4,), (3,), (), (7,))]
         + [full_rows, pltpu.VMEM((count, n_qkv), BF16), full_rows, pltpu.VMEM((count, n_out), BF16)]
+        + [pltpu.VMEM(weights.shape, BF16)]
         + scatter_scratch()
         + gradient_scratch(n)
         + [pltpu.VMEM((4, 64, n), BF16)] * 2
@@ -982,7 +1029,7 @@
 
 
 def project(rows, weights, cosine, sine):
-    step = 256
+    step = 512
 
     def kernel(rows_ref, w_ref, cos_ref, sin_ref, q_ref, kv_ref):
         out = dot(rows_ref[...], w_ref[...])
@@ -1006,30 +1053,6 @@
         (out, shape((2, 2, 8 * ROWS, HD), BF16)),
         (by_rows(step, 2 * HD), pl.BlockSpec((2, 2, step, HD), lambda i: (0, 0, i, 0))),
     )
-
-
-def partial_rows(pairs, name, extra=None):
-    step = 256
-    sets = [pairs] + ([extra] if extra else [])
-    flat = [pair for group in sets for pair in group]
-
-    def kernel(*refs):
-        values, outs = refs[: 2 * len(flat)], refs[2 * len(flat) :]
-        at = 0
-        for group, out in zip(sets, outs):
-            total = None
-            for _ in group:
-                term = dot(values[at][...], values[at + 1][...], 1, 1)
-                total = term if total is None else total + term
-                at += 2
-            out[...] = total.astype(BF16)
-
-    inputs, specs = [], []
-    for a, b, width, column in flat:
-        inputs += [a, b]
-        specs += [by_rows(step, width), whole((WIDE, width), 0, column)]
-    out = tuple(shape((8 * ROWS, WIDE), BF16) for _ in sets)
-    return plain(kernel, name, (8 * ROWS // step,), inputs, specs, out, tuple(by_rows(step, WIDE) for _ in sets))
 
 
 def feed_forward(rows, grads, weights):
@@ -1085,23 +1108,6 @@
         out_specs=(INSIDE,) * 11,
         compiler_params=pltpu.CompilerParams(vmem_limit_bytes=VMEM),
     )(layer, token_grad, gains, attention, low, high)
-
-
-def back_to_heads(rows, weights):
-    step = 256
-
-    def kernel(rows_ref, w_ref, out_ref):
-        out_ref[...] = dot(rows_ref[...], w_ref[...]).astype(BF16)
-
-    return plain(
-        kernel,
-        "back_to_heads",
-        (8 * ROWS // step,),
-        (rows, weights),
-        [by_rows(step, WIDE), whole((WIDE, 2 * HD))],
-        shape((8 * ROWS, 2 * HD), BF16),
-        by_rows(step, 2 * HD),
-    )
 
 
 TILE = 256
@@ -1238,16 +1244,17 @@
     )
 
 
-def attend_back(prefixes, queries, here, there, grads, mixed, lse, cosine, sine, out_part, mid, sum_a):
+def attend_back(prefixes, queries, here, there, rows, weights, mixed, lse, cosine, sine, out_part, mid, sum_a):
     n = sum_a.shape[-1]
 
     def kernel(
-        prefixes_ref, q_ref, here_ref, there_ref, g_ref, o_ref, lse_ref, cos_ref, sin_ref, part_ref, mid_ref, sum_a_ref,
-        d_ref, layer_ref, weight_ref, delta_ref, dq_ref, acc_ref, near_ref, away_ref, land_ref, *rest,
+        prefixes_ref, rows_hbm, weights_hbm, q_ref, here_ref, there_ref, o_ref, lse_ref, cos_ref, sin_ref, part_ref, mid_ref,
+        sum_a_ref, d_ref, layer_ref, weight_ref, rows_ref, weights_ref, g_ref, delta_ref, dq_ref, acc_ref, near_ref, away_ref, land_ref, *rest,
     ):
-        second, last, (out_sems, in_sems) = rest[:4], rest[4:6], rest[6:]
+        (outgoing, mine, land, far, gone), last, (out_sems, in_sems) = rest[:5], rest[5:7], rest[7:]
         prefix = prefix_of(prefixes_ref)
         spot, post = Spot(), Post(out_sems, in_sems)
+        loads = load(post, [(weights_hbm, weights_ref), (rows_hbm, rows_ref)])
         partner = spot.at(dx=2)
         greet(spot, row_peers(spot) + y_peers(spot) + [partner], 6)
 
@@ -1292,6 +1299,15 @@
             lax.fori_loop(0, 4, step, 0)
 
         def compute():
+            for copy in loads:
+                copy.wait()
+
+            def heads(i, carry):
+                span = pl.ds(pl.multiple_of(i * 256, 256), 256)
+                g_ref[span, :] = dot(rows_ref[span, :], weights_ref[...]).astype(BF16)
+                return carry
+
+            lax.fori_loop(0, 4, heads, 0)
             copies = []
             for head in range(2):
                 sweep(head, 1, there_ref, acc_ref)
@@ -1320,15 +1336,16 @@
                 copy.wait_send()
 
         def output():
-            yield from scatter_rows(spot, post, part_ref, *second)
+            make = row_loads(spot, post, part_ref, outgoing, mine)
+            yield from scatter_rows(spot, post, make, outgoing, mine, land, far, gone)
 
             def body(strip):
-                layer_ref[strip, :] = (mid_ref[strip, :] + row_sum(spot, second[0], second[1], second[3], strip)).astype(BF16)
+                layer_ref[strip, :] = (mid_ref[strip, :] + row_sum(spot, mine, land, gone, strip)).astype(BF16)
 
             in_strips(ROWS, body)
 
         play(
-            "owcocwocowc",
+            "wcocowcoc",
             c=compute(),
             o=output(),
             w=scatter_low(spot, post, sum_a_ref, strip_writer(weight_ref), *last),
@@ -1339,10 +1356,13 @@
         kernel,
         "attend_back",
         (shape((8 * ROWS, PACK), BF16), shape((ROWS, WIDE), BF16), shape((64, n), F32)),
-        (prefixes, queries, here, there, grads, mixed, lse, cosine, sine, out_part, mid, sum_a),
-        [pl.BlockSpec(memory_space=pltpu.SMEM)] + [INSIDE] * 8 + [ANY, INSIDE, INSIDE],
+        (prefixes, rows, weights, queries, here, there, mixed, lse, cosine, sine, out_part, mid, sum_a),
+        [pl.BlockSpec(memory_space=pltpu.SMEM), ANY, ANY] + [INSIDE] * 7 + [ANY, INSIDE, INSIDE],
         (INSIDE,) * 3,
         [
+            pltpu.VMEM(rows.shape, BF16),
+            pltpu.VMEM(weights.shape, BF16),
+            pltpu.VMEM((8 * ROWS, 2 * HD), BF16),
             pltpu.VMEM((8, TILE), F32),
             pltpu.VMEM((8, TILE, HD), F32),
             pltpu.VMEM(pair, F32),
@@ -1379,22 +1399,18 @@
     queries, here = project(rows_one, full_one, cosine, sine)
     attended, lse, there, grad_rows, full_out, stage_two = attend(prefixes, queries, here, cotangent, row_out, second)
     full_out = full_out.reshape(WIDE, -1)
-    (part,) = partial_rows([(attended, full_out, 2 * HD, 0)], "attention_out")
-    mid, rows_two, full_two = middle(part.reshape(8, ROWS, WIDE), tokens, feed_gain, row_two, stage_two)
+    mid, rows_two, full_two = middle(attended, full_out, tokens, feed_gain, row_two, stage_two)
     rows_two, grad_rows, full_two = (a.reshape(-1, a.shape[-1]) for a in (rows_two, grad_rows, full_two.reshape(WIDE, -1)))
     hidden, d_gate, d_up = feed_forward(rows_two, grad_rows, full_two)
-    (part,) = partial_rows([(d_gate, full_two, PACK, 0), (d_up, full_two, PACK, 1)], "feed_back")
     grad_mid, mid_rows, feed_part, sum_a, sum_b, part_out = turn(
-        part.reshape(8, ROWS, WIDE), mid, feed_gain, cotangent, rows_two, grad_rows, d_gate, d_up, hidden, full_two
+        mid, feed_gain, cotangent, rows_two, grad_rows, d_gate, d_up, hidden, full_two
     )
     mid_rows = mid_rows.reshape(-1, WIDE)
-    grad_mixed = back_to_heads(mid_rows, full_out)
     d_qkv, layer_output, low = attend_back(
-        prefixes, queries, here, there, grad_mixed, attended, lse, cosine, sine, part_out.reshape(8, ROWS, WIDE), mid, sum_a
-    )
-    (part,) = partial_rows([(d_qkv, full_one, PACK, 0)], "attention_back")
+        prefixes, queries, here, there, mid_rows, full_out, attended, lse, cosine, sine, part_out.reshape(8, ROWS, WIDE), mid, sum_a
+    )
     token_grad, gains, attention, high = leave(
-        part.reshape(8, ROWS, WIDE), tokens, norm_gain, grad_mid, feed_part, rows_one, d_qkv, mid_rows, attended, sum_b
+        full_one, tokens, norm_gain, grad_mid, feed_part, rows_one, d_qkv, mid_rows, attended, sum_b
     )
     layer_output, token_grad, norm_grad, feed_grad, *grads = settle(
         layer_output, token_grad, gains, attention, low, high, gate_weight.shape[1]

time: 342 us -> 319 us (0.933)
  Pallas kernels: 340 us -> 317 us
    pallas_call x6 -> x2, Pallas kernels: 53.1 us -> 23.7 us  [plain(): pl.pallas_call(kernel, name=name, out_shape=outs, grid=grid, in_specs=in_...]
    pallas_call x6, Pallas kernels: 283 us -> 290 us  [moving(): pl.pallas_call(kernel, name=name, out_shape=outs, in_specs=in_specs, out_...]
where the time goes in v4:
time: 319 us; the launch traced here: 318 us
  Pallas kernels  317 us (99%)
    pallas_call x6, Pallas kernels, moving(): pl.pallas_call(kernel, name=name, out_shape=outs, in_specs=in_specs, out_...  290 us
    pallas_call x2, Pallas kernels, plain(): pl.pallas_call(kernel, name=name, out_shape=outs, grid=grid, in_specs=in_...  23.7 us

profile of v4, /device:TPU:1, one launch (start us, length us, event | category | flops | bytes accessed | tf_op | source)
XLA Modules:
  0.0 318.2 jit_solution(17066396911974502248)
XLA Ops:
  0.6 44.8 %enter.1 = (bf16[8,128,2048]{2,1,0:T(8,128)(2,1)}, bf16[4,4,2,64,768]{4,3,2,1,0:T(8,128)(2,1)}, bf16[4,128,256]{2,1,0:T(8,128)(2,1)}, bf16[4,64,2304]{2,1,0:T(8,...) custom-call(bf16[128,2048]{1,0:T(8,128)(2,1)} %tokens_ref.5, ...), custom_call_target="tpu_custom_call" | custom-call | tf_op jit(solution)/shard_map/enter/pallas_call | solution.py:693
  45.4 7.3 %project.1 = (bf16[1024,256]{1,0:T(8,128)(2,1)}, bf16[2,2,1024,128]{3,2,1,0:T(8,128)(2,1)}) custom-call(bf16[1024,2048]{1,0:T(8,128)(2,1)} %bitcast.22, bf16[2048,768]{1,0:T(8,128)(2,1)} %bitcast.26, f32[1024,128]{1,0:T(8,128)} %get-tuple-element.58.cos_ref, f32[1024,128]{1,0:T(8,128)} %get-tuple-element.59.sin_ref), custom_call_target="tpu_custom_call" | custom-call | tf_op jit(solution)/shard_map/project/pallas_call | solution.py:1010
  52.8 34.3 %attend.1 = (bf16[1024,256]{1,0:T(8,128)(2,1)}, f32[8,256]{1,0:T(8,128)}, bf16[2,2,1024,128]{3,2,1,0:T(8,128)(2,1)}, bf16[8,128,2048]{2,1,0:T(8,128)(2,1)}, bf16...) custom-call(s32[8]{0:T(128)} %prefixes_ref.3, bf16[1024,256]{1,0:T(8,128)(2,1)} %get-tuple-element.60.q_ref, ...), custom_call_target="tpu_custom_call" | custom-call | tf_op jit(solution)/shard_map/attend/pallas_call | solution.py:693
  87.1 51.6 %middle.1 = (f32[128,2048]{1,0:T(8,128)}, bf16[8,128,2048]{2,1,0:T(8,128)(2,1)}, bf16[4,4,2,64,2304]{4,3,2,1,0:T(8,128)(2,1)}) custom-call(bf16[1024,256]{1,0:T(8,128)(2,1)} %get-tuple-element.64.mixed_hbm.o_ref, bf16[2048,256]{1,0:T(8,128)(2,1)} %bitcast.28, bf16[128,2048]{1,0:T(8,128)(2,1)} %tokens_ref.5, bf16[2048]{0:T(1024)(128)(2,1)} %gain_ref.6, ...), custom_call_target="tpu_custom_call" | custom-call | tf_op jit(solution)/shard_map/middle/pallas_call | solution.py:693
  138.8 16.3 %feed_forward.1 = (bf16[1024,768]{1,0:T(8,128)(2,1)}, bf16[1024,768]{1,0:T(8,128)(2,1)}, bf16[1024,768]{1,0:T(8,128)(2,1)}) custom-call(bf16[1024,2048]{1,0:T(8,128)(2,1)} %bitcast.20, bf16[1024,2048]{1,0:T(8,128)(2,1)} %bitcast.18, bf16[2048,2304]{1,0:T(8,128)(2,1)} %bitcast.14, bf16[2048,2304]{1,0:T(8,128)(2,1)} %bitcast.15, bf16[2048,2304]{1,0:T(8,128)(2,1)} %bitcast.16), custom_call_target="tpu_custom_call" | custom-call | tf_op jit(solution)/shard_map/feed_forward/pallas_call | solution.py:1010
  155.1 66.2 %turn.1 = (f32[128,2048]{1,0:T(8,128)}, bf16[8,128,2048]{2,1,0:T(8,128)(2,1)}, f32[1,2048]{1,0:T(1,128)}, bf16[4,64,2304]{2,1,0:T(8,128)(2,1)}, bf16[4,64,2304]{...) custom-call(f32[128,2048]{1,0:T(8,128)} %get-tuple-element.68.mid_ref, bf16[2048]{0:T(1024)(128)(2,1)} %gain_ref.6, ...), custom_call_target="tpu_custom_call" | custom-call | tf_op jit(solution)/shard_map/turn/pallas_call | solution.py:693
  221.2 42.5 %attend_back.1 = (bf16[1024,768]{1,0:T(8,128)(2,1)}, bf16[128,2048]{1,0:T(8,128)(2,1)}, f32[64,2304]{1,0:T(8,128)}) custom-call(s32[8]{0:T(128)} %prefixes_ref.3, bf16[1024,2048]{1,0:T(8,128)(2,1)} %bitcast.24, bf16[2048,256]{1,0:T(8,128)(2,1)} %bitcast.29, bf16[1024,256]{1,0:T(8,128)(2,1)} %get-tuple-element.60.q_ref, ...), custom_call_target="tpu_custom_call" | custom-call | tf_op jit(solution)/shard_map/attend_back/pallas_call | solution.py:693
  263.8 50.4 %leave.1 = (f32[128,2048]{1,0:T(8,128)}, f32[8,128]{1,0:T(8,128)}, f32[128,1024]{1,0:T(8,128)}, f32[64,2304]{1,0:T(8,128)}) custom-call(bf16[2048,768]{1,0:T(8,128)(2,1)} %bitcast.27, bf16[128,2048]{1,0:T(8,128)(2,1)} %tokens_ref.5, bf16[2048]{0:T(1024)(128)(2,1)} %gain_ref.7, f32[128,2048]{1,0:T(8,128)} %get-tuple-element.81.grad_ref, ...), custom_call_target="tpu_custom_call" | custom-call | tf_op jit(solution)/shard_map/leave/pallas_call | solution.py:693
  314.2 3.8 %settle.1 = (bf16[128,2048]{1,0:T(8,128)(2,1)}, f32[128,2048]{1,0:T(8,128)}, f32[1,128]{1,0:T(1,128)}, f32[1,128]{1,0:T(1,128)}, f32[128,256]{1,0:T(8,128)}, /*i...) custom-call(bf16[128,2048]{1,0:T(8,128)(2,1)} %get-tuple-element.80., ...), custom_call_target="tpu_custom_call" | custom-call | tf_op jit(solution)/shard_map/settle/pallas_call | solution.py:1102

commit v5 on v4

--- a/solution.py
+++ b/solution.py
@@ -200,7 +200,7 @@
 
 
 def row_products(spot, terms, outgoing, mine):
-    def make(z):
+    def make(k, z):
         other, own = pl.ds(((1 - spot.c) * 4 + z) * ROWS, ROWS), pl.ds((spot.c * 4 + z) * ROWS, ROWS)
 
         def step(i, carry):
@@ -219,24 +219,34 @@
 
 
 def row_loads(spot, post, part, outgoing, mine):
-    def make(z):
-        copies = load(post, [(part.at[(1 - spot.c) * 4 + z], outgoing.at[z]), (part.at[spot.c * 4 + z], mine.at[z])])
-        for copy in copies:
+    copies = []
+    for z in row_order(spot):
+        pairs = [(part.at[(1 - spot.c) * 4 + z], outgoing.at[z]), (part.at[spot.c * 4 + z], mine.at[z])]
+        copies.append(load(post, pairs))
+
+    def make(k, z):
+        for copy in copies[k]:
             copy.wait()
 
     return make
 
 
-def scatter_rows(spot, post, make, outgoing, mine, land, far, gone):
+def row_order(spot):
+    return [lax.rem(spot.z + dz, 4) for dz in (2, 3, 1, 0)]
+
+
+def scatter_rows(spot, post, make, outgoing, mine, land, far, gone, ahead=False):
     up, down, core = spot.at(dz=1), spot.at(dz=3), spot.other()
     half = ROWS // 2
     low, high = pl.ds(0, half), pl.ds(half, half)
-    steps = [lax.rem(spot.z + dz, 4) for dz in (2, 3, 1, 0)]
+    steps = row_order(spot)
     distant, lower, upper, here = steps
     to_core, others = [], []
 
     def begin(k):
-        make(steps[k])
+        if len(to_core) > k:
+            return
+        make(k, steps[k])
         to_core.append(post.copy(outgoing.at[steps[k]], land.at[steps[k]], core))
         to_core[k].start()
 
@@ -250,6 +260,10 @@
         if k < 3:
             add_into(mine.at[steps[k]], land.at[steps[k]])
 
+    if ahead:
+        for k in range(4):
+            begin(k)
+        yield
     begin(0)
     begin(1)
     ready(0)
@@ -1335,9 +1349,10 @@
             for copy in copies:
                 copy.wait_send()
 
+        make = row_loads(spot, post, part_ref, outgoing, mine)
+
         def output():
-            make = row_loads(spot, post, part_ref, outgoing, mine)
-            yield from scatter_rows(spot, post, make, outgoing, mine, land, far, gone)
+            yield from scatter_rows(spot, post, make, outgoing, mine, land, far, gone, True)
 
             def body(strip):
                 layer_ref[strip, :] = (mid_ref[strip, :] + row_sum(spot, mine, land, gone, strip)).astype(BF16)
@@ -1345,7 +1360,7 @@
             in_strips(ROWS, body)
 
         play(
-            "wcocowcoc",
+            "wcococwcoow",
             c=compute(),
             o=output(),
             w=scatter_low(spot, post, sum_a_ref, strip_writer(weight_ref), *last),

time: 319 us -> 316 us (level)
  no operation moved by 1% of the time
where the time goes in v5:
time: 316 us; the launch traced here: 315 us
  Pallas kernels  315 us (100%)
    pallas_call x6, Pallas kernels, moving(): pl.pallas_call(kernel, name=name, out_shape=outs, in_specs=in_specs, out_...  287 us
    pallas_call x2, Pallas kernels, plain(): pl.pallas_call(kernel, name=name, out_shape=outs, grid=grid, in_specs=in_...  23.7 us

profile of v5, /device:TPU:1, one launch (start us, length us, event | category | flops | bytes accessed | tf_op | source)
XLA Modules:
  0.0 315.4 jit_solution(800941820528325305)
XLA Ops:
  0.6 44.8 %enter.1 = (bf16[8,128,2048]{2,1,0:T(8,128)(2,1)}, bf16[4,4,2,64,768]{4,3,2,1,0:T(8,128)(2,1)}, bf16[4,128,256]{2,1,0:T(8,128)(2,1)}, bf16[4,64,2304]{2,1,0:T(8,...) custom-call(bf16[128,2048]{1,0:T(8,128)(2,1)} %tokens_ref.5, ...), custom_call_target="tpu_custom_call" | custom-call | tf_op jit(solution)/shard_map/enter/pallas_call | solution.py:707
  45.4 7.3 %project.1 = (bf16[1024,256]{1,0:T(8,128)(2,1)}, bf16[2,2,1024,128]{3,2,1,0:T(8,128)(2,1)}) custom-call(bf16[1024,2048]{1,0:T(8,128)(2,1)} %bitcast.22, bf16[2048,768]{1,0:T(8,128)(2,1)} %bitcast.26, f32[1024,128]{1,0:T(8,128)} %get-tuple-element.58.cos_ref, f32[1024,128]{1,0:T(8,128)} %get-tuple-element.59.sin_ref), custom_call_target="tpu_custom_call" | custom-call | tf_op jit(solution)/shard_map/project/pallas_call | solution.py:1024
  52.8 34.3 %attend.1 = (bf16[1024,256]{1,0:T(8,128)(2,1)}, f32[8,256]{1,0:T(8,128)}, bf16[2,2,1024,128]{3,2,1,0:T(8,128)(2,1)}, bf16[8,128,2048]{2,1,0:T(8,128)(2,1)}, bf16...) custom-call(s32[8]{0:T(128)} %prefixes_ref.3, bf16[1024,256]{1,0:T(8,128)(2,1)} %get-tuple-element.60.q_ref, ...), custom_call_target="tpu_custom_call" | custom-call | tf_op jit(solution)/shard_map/attend/pallas_call | solution.py:707
  87.1 51.6 %middle.1 = (f32[128,2048]{1,0:T(8,128)}, bf16[8,128,2048]{2,1,0:T(8,128)(2,1)}, bf16[4,4,2,64,2304]{4,3,2,1,0:T(8,128)(2,1)}) custom-call(bf16[1024,256]{1,0:T(8,128)(2,1)} %get-tuple-element.64.mixed_hbm.o_ref, bf16[2048,256]{1,0:T(8,128)(2,1)} %bitcast.28, bf16[128,2048]{1,0:T(8,128)(2,1)} %tokens_ref.5, bf16[2048]{0:T(1024)(128)(2,1)} %gain_ref.6, ...), custom_call_target="tpu_custom_call" | custom-call | tf_op jit(solution)/shard_map/middle/pallas_call | solution.py:707
  138.8 16.3 %feed_forward.1 = (bf16[1024,768]{1,0:T(8,128)(2,1)}, bf16[1024,768]{1,0:T(8,128)(2,1)}, bf16[1024,768]{1,0:T(8,128)(2,1)}) custom-call(bf16[1024,2048]{1,0:T(8,128)(2,1)} %bitcast.20, bf16[1024,2048]{1,0:T(8,128)(2,1)} %bitcast.18, bf16[2048,2304]{1,0:T(8,128)(2,1)} %bitcast.14, bf16[2048,2304]{1,0:T(8,128)(2,1)} %bitcast.15, bf16[2048,2304]{1,0:T(8,128)(2,1)} %bitcast.16), custom_call_target="tpu_custom_call" | custom-call | tf_op jit(solution)/shard_map/feed_forward/pallas_call | solution.py:1024
  155.1 66.2 %turn.1 = (f32[128,2048]{1,0:T(8,128)}, bf16[8,128,2048]{2,1,0:T(8,128)(2,1)}, f32[1,2048]{1,0:T(1,128)}, bf16[4,64,2304]{2,1,0:T(8,128)(2,1)}, bf16[4,64,2304]{...) custom-call(f32[128,2048]{1,0:T(8,128)} %get-tuple-element.68.mid_ref, bf16[2048]{0:T(1024)(128)(2,1)} %gain_ref.6, ...), custom_call_target="tpu_custom_call" | custom-call | tf_op jit(solution)/shard_map/turn/pallas_call | solution.py:707
  221.2 40.2 %attend_back.1 = (bf16[1024,768]{1,0:T(8,128)(2,1)}, bf16[128,2048]{1,0:T(8,128)(2,1)}, f32[64,2304]{1,0:T(8,128)}) custom-call(s32[8]{0:T(128)} %prefixes_ref.3, bf16[1024,2048]{1,0:T(8,128)(2,1)} %bitcast.24, bf16[2048,256]{1,0:T(8,128)(2,1)} %bitcast.29, bf16[1024,256]{1,0:T(8,128)(2,1)} %get-tuple-element.60.q_ref, ...), custom_call_target="tpu_custom_call" | custom-call | tf_op jit(solution)/shard_map/attend_back/pallas_call | solution.py:707
  261.4 50.1 %leave.1 = (f32[128,2048]{1,0:T(8,128)}, f32[8,128]{1,0:T(8,128)}, f32[128,1024]{1,0:T(8,128)}, f32[64,2304]{1,0:T(8,128)}) custom-call(bf16[2048,768]{1,0:T(8,128)(2,1)} %bitcast.27, bf16[128,2048]{1,0:T(8,128)(2,1)} %tokens_ref.5, bf16[2048]{0:T(1024)(128)(2,1)} %gain_ref.7, f32[128,2048]{1,0:T(8,128)} %get-tuple-element.81.grad_ref, ...), custom_call_target="tpu_custom_call" | custom-call | tf_op jit(solution)/shard_map/leave/pallas_call | solution.py:707
  311.5 3.8 %settle.1 = (bf16[128,2048]{1,0:T(8,128)(2,1)}, f32[128,2048]{1,0:T(8,128)}, f32[1,128]{1,0:T(1,128)}, f32[1,128]{1,0:T(1,128)}, f32[128,256]{1,0:T(8,128)}, /*i...) custom-call(bf16[128,2048]{1,0:T(8,128)(2,1)} %get-tuple-element.80., ...), custom_call_target="tpu_custom_call" | custom-call | tf_op jit(solution)/shard_map/settle/pallas_call | solution.py:1116

commit v6 on v5

--- a/solution.py
+++ b/solution.py
@@ -1098,17 +1098,22 @@
     def kernel(
         layer_ref, token_ref, gains_ref, attention_ref, low_ref, high_ref,
         layer_out, token_out, norm_out, feed_out, query_out, key_out, value_out, out_out, gate_out, up_out, down_out,
+        sem_ref,
     ):
-        layer_out[...] = layer_ref[...]
-        token_out[...] = token_ref[...]
+        moves = [(layer_ref, layer_out), (token_ref, token_out)]
+        for i, out in enumerate((query_out, key_out, value_out)):
+            moves.append((attention_ref.at[:, pl.ds(i * 2 * HD, 2 * HD)], out))
+        copies = [pltpu.make_async_copy(src, dst, sem_ref.at[i]) for i, (src, dst) in enumerate(moves)]
+        for copy in copies:
+            copy.start()
         norm_out[...] = gains_ref[0:1, :]
         feed_out[...] = gains_ref[1:2, :]
-        for i, out in enumerate((query_out, key_out, value_out)):
-            out[...] = attention_ref[:, i * 2 * HD : (i + 1) * 2 * HD]
         out_out[...] = attention_ref[:, PACK:].T
         for i, out in enumerate((gate_out, up_out, down_out)):
             columns = slice(i * PACK, (i + 1) * PACK)
             out[...] = jnp.concatenate([low_ref[:, columns], high_ref[:, columns]], 0).T[:wide]
+        for copy in copies:
+            copy.wait()
 
     vector = shape((1, 128), F32)
     square = shape((ROWS, 2 * HD), F32)
@@ -1119,7 +1124,8 @@
         out_shape=(shape(layer.shape, layer.dtype), shape(token_grad.shape, F32), vector, vector, square, square, square)
         + (shape((2 * HD, ROWS), F32), tall, tall, tall),
         in_specs=[INSIDE] * 6,
-        out_specs=(INSIDE,) * 11,
+        out_specs=(ANY, ANY, INSIDE, INSIDE, ANY, ANY, ANY) + (INSIDE,) * 4,
+        scratch_shapes=[pltpu.SemaphoreType.DMA((5,))],
         compiler_params=pltpu.CompilerParams(vmem_limit_bytes=VMEM),
     )(layer, token_grad, gains, attention, low, high)
 

time: 316 us -> 316 us (level)
  no operation moved by 1% of the time
where the time goes in v6:
time: 316 us
  Pallas kernels  315 us (100%)
    pallas_call x6, Pallas kernels, moving(): pl.pallas_call(kernel, name=name, out_shape=outs, in_specs=in_specs, out_...  287 us
    pallas_call x2, Pallas kernels, plain(): pl.pallas_call(kernel, name=name, out_shape=outs, grid=grid, in_specs=in_...  23.7 us

profile of v6, /device:TPU:1, one launch (start us, length us, event | category | flops | bytes accessed | tf_op | source)
XLA Modules:
  0.0 315.9 jit_solution(17846713825982559564)
XLA Ops:
  0.6 44.8 %enter.1 = (bf16[8,128,2048]{2,1,0:T(8,128)(2,1)}, bf16[4,4,2,64,768]{4,3,2,1,0:T(8,128)(2,1)}, bf16[4,128,256]{2,1,0:T(8,128)(2,1)}, bf16[4,64,2304]{2,1,0:T(8,...) custom-call(bf16[128,2048]{1,0:T(8,128)(2,1)} %tokens_ref.5, ...), custom_call_target="tpu_custom_call" | custom-call | tf_op jit(solution)/shard_map/enter/pallas_call | solution.py:707
  45.4 7.3 %project.1 = (bf16[1024,256]{1,0:T(8,128)(2,1)}, bf16[2,2,1024,128]{3,2,1,0:T(8,128)(2,1)}) custom-call(bf16[1024,2048]{1,0:T(8,128)(2,1)} %bitcast.22, bf16[2048,768]{1,0:T(8,128)(2,1)} %bitcast.26, f32[1024,128]{1,0:T(8,128)} %get-tuple-element.58.cos_ref, f32[1024,128]{1,0:T(8,128)} %get-tuple-element.59.sin_ref), custom_call_target="tpu_custom_call" | custom-call | tf_op jit(solution)/shard_map/project/pallas_call | solution.py:1024
  52.8 34.3 %attend.1 = (bf16[1024,256]{1,0:T(8,128)(2,1)}, f32[8,256]{1,0:T(8,128)}, bf16[2,2,1024,128]{3,2,1,0:T(8,128)(2,1)}, bf16[8,128,2048]{2,1,0:T(8,128)(2,1)}, bf16...) custom-call(s32[8]{0:T(128)} %prefixes_ref.3, bf16[1024,256]{1,0:T(8,128)(2,1)} %get-tuple-element.60.q_ref, ...), custom_call_target="tpu_custom_call" | custom-call | tf_op jit(solution)/shard_map/attend/pallas_call | solution.py:707
  87.1 51.6 %middle.1 = (f32[128,2048]{1,0:T(8,128)}, bf16[8,128,2048]{2,1,0:T(8,128)(2,1)}, bf16[4,4,2,64,2304]{4,3,2,1,0:T(8,128)(2,1)}) custom-call(bf16[1024,256]{1,0:T(8,128)(2,1)} %get-tuple-element.64.mixed_hbm.o_ref, bf16[2048,256]{1,0:T(8,128)(2,1)} %bitcast.28, bf16[128,2048]{1,0:T(8,128)(2,1)} %tokens_ref.5, bf16[2048]{0:T(1024)(128)(2,1)} %gain_ref.6, ...), custom_call_target="tpu_custom_call" | custom-call | tf_op jit(solution)/shard_map/middle/pallas_call | solution.py:707
  138.8 16.3 %feed_forward.1 = (bf16[1024,768]{1,0:T(8,128)(2,1)}, bf16[1024,768]{1,0:T(8,128)(2,1)}, bf16[1024,768]{1,0:T(8,128)(2,1)}) custom-call(bf16[1024,2048]{1,0:T(8,128)(2,1)} %bitcast.20, bf16[1024,2048]{1,0:T(8,128)(2,1)} %bitcast.18, bf16[2048,2304]{1,0:T(8,128)(2,1)} %bitcast.14, bf16[2048,2304]{1,0:T(8,128)(2,1)} %bitcast.15, bf16[2048,2304]{1,0:T(8,128)(2,1)} %bitcast.16), custom_call_target="tpu_custom_call" | custom-call | tf_op jit(solution)/shard_map/feed_forward/pallas_call | solution.py:1024
  155.1 66.2 %turn.1 = (f32[128,2048]{1,0:T(8,128)}, bf16[8,128,2048]{2,1,0:T(8,128)(2,1)}, f32[1,2048]{1,0:T(1,128)}, bf16[4,64,2304]{2,1,0:T(8,128)(2,1)}, bf16[4,64,2304]{...) custom-call(f32[128,2048]{1,0:T(8,128)} %get-tuple-element.68.mid_ref, bf16[2048]{0:T(1024)(128)(2,1)} %gain_ref.6, ...), custom_call_target="tpu_custom_call" | custom-call | tf_op jit(solution)/shard_map/turn/pallas_call | solution.py:707
  221.2 40.2 %attend_back.1 = (bf16[1024,768]{1,0:T(8,128)(2,1)}, bf16[128,2048]{1,0:T(8,128)(2,1)}, f32[64,2304]{1,0:T(8,128)}) custom-call(s32[8]{0:T(128)} %prefixes_ref.3, bf16[1024,2048]{1,0:T(8,128)(2,1)} %bitcast.24, bf16[2048,256]{1,0:T(8,128)(2,1)} %bitcast.29, bf16[1024,256]{1,0:T(8,128)(2,1)} %get-tuple-element.60.q_ref, ...), custom_call_target="tpu_custom_call" | custom-call | tf_op jit(solution)/shard_map/attend_back/pallas_call | solution.py:707
  261.4 50.1 %leave.1 = (f32[128,2048]{1,0:T(8,128)}, f32[8,128]{1,0:T(8,128)}, f32[128,1024]{1,0:T(8,128)}, f32[64,2304]{1,0:T(8,128)}) custom-call(bf16[2048,768]{1,0:T(8,128)(2,1)} %bitcast.27, bf16[128,2048]{1,0:T(8,128)(2,1)} %tokens_ref.5, bf16[2048]{0:T(1024)(128)(2,1)} %gain_ref.7, f32[128,2048]{1,0:T(8,128)} %get-tuple-element.81.grad_ref, ...), custom_call_target="tpu_custom_call" | custom-call | tf_op jit(solution)/shard_map/leave/pallas_call | solution.py:707
  311.5 4.2 %settle.1 = (bf16[128,2048]{1,0:T(8,128)(2,1)}, f32[128,2048]{1,0:T(8,128)}, f32[1,128]{1,0:T(1,128)}, f32[1,128]{1,0:T(1,128)}, f32[128,256]{1,0:T(8,128)}, /*i...) custom-call(bf16[128,2048]{1,0:T(8,128)(2,1)} %get-tuple-element.80., ...), custom_call_target="tpu_custom_call" | custom-call | tf_op jit(solution)/shard_map/settle/pallas_call | solution.py:1121
